TPU v7x, 256 devices: a whole 4x4x8 slice. The times are simulated.
256 devices in a mesh: ctx: 16 (over x_lo, z), head: 16 (over x_hi, y, core).
Axes of the slice: x: 4 (x_hi: 2, x_lo: 2; x = x_hi * 2 + x_lo), y: 4, z: 8, core: 2. Of those that a mesh axis runs over, the one named last changes fastest.
Arguments:
- query: bfloat16 [4096, 8192], P('ctx', 'head'), may hold values from -6 to 6
- keyval: bfloat16 [4096, 2048], P('ctx'), may hold values from -6 to 6
- grad_out: bfloat16 [4096, 8192], P('ctx', 'head'), may hold values from -6 to 6
- vis_blocks: int32 [32, 24], replicated, may hold values from 0 to 31, as said below
- vis_count: int32 [32], replicated, may hold values from 1 to 24, as said below
- segment_ids: int32 [4096], replicated, may hold values from 0 to 31, never falling along the last dimension, each value on 1 to 256 neighbouring positions
- block_order: int32 [32], replicated, may hold values from 0 to 31, as said below
Outputs:
- attn_out: bfloat16 [4096, 8192], P('ctx', 'head')
- grad_query: bfloat16 [4096, 8192], P('ctx', 'head')
- grad_keyval: float32 [4096, 2048], P('ctx')
Inputs may be any that keep to these rules, and one draw needn't show every extreme that they name: `vis_blocks`: row b lists in rising order the blocks that block b's queries may see (block 0 and b itself always among them), then repeats b up to 24 entries. `vis_count`: the number of listed blocks of each row; some row lists exactly 24. `block_order`: storage blocks 2 i and 2 i + 1 hold visibility blocks p and 31 - p for some p; every block is held once. `segment_ids`: segment numbers never fall along the tokens in visibility-block order.
All inputs are finite; a program needn't handle non-finite values.
Results may differ from a plain program's by a relative error of at most 0.025.
Values may be sent and summed in bfloat16 or wider, within the bound.
No kernel may reach another device: no remote copies, remote signals or barrier semaphores. Data moves between devices by JAX's collectives and lax.ppermute only.
A program may use at most 64 MiB of HBM per device.

v0:
```python
import functools

import jax
import jax.numpy as jnp
from jax import lax
from jax.experimental import pallas as pl
from jax.experimental.pallas import tpu as pltpu
from jax.sharding import Mesh, PartitionSpec as P

QH = 64
KVH = 8
HD = 128
BLK = 128
NB = 32
HEADS = 4
GROUP = 4
ROWS = HEADS * BLK
SCALE = HD**-0.5
LOG2E = 1.4426950408889634
MASKED = -1e30
BF = jnp.bfloat16
F32 = jnp.float32


def shift(value, axis, size, by):
    return lax.ppermute(value, axis, [(i, (i + by) % size) for i in range(size)])


def swap(value, axis):
    return lax.ppermute(value, axis, [(0, 1), (1, 0)])


def nt(a, b):
    return lax.dot_general(a, b, (((1,), (1,)), ((), ())), preferred_element_type=F32)


def nn(a, b):
    return lax.dot_general(a, b, (((1,), (0,)), ((), ())), preferred_element_type=F32)


def tn(a, b):
    return lax.dot_general(a, b, (((0,), (0,)), ((), ())), preferred_element_type=F32)


def attention_kernel(
    vis_any, count_any, order_any, q_any, g_any, seg_any, k_ref, v_ref,
    out_any, dq_any, mine_ref, other_ref,
    store, low, diag_scr, low_diag, accum, q_scr, g_scr, acc, q_ref, g_ref, seg_ref, out_ref, dq_ref,
    vis, count, order, inv, io_sem,
):
    x, z, core = lax.axis_index("x"), lax.axis_index("z"), lax.axis_index("core")
    own = x * 8 + z
    pairs = [
        (order_any, order),
        (count_any, count),
        (vis_any, vis),
        (q_any, q_ref),
        (seg_any, seg_ref),
        (g_any, g_ref),
    ]
    inputs = [pltpu.make_async_copy(*pair, io_sem.at[k]) for k, pair in enumerate(pairs)]
    for copy in inputs:
        copy.start()
    acc[...] = jnp.zeros_like(acc)
    inputs[0].wait()

    def place(j, carry):
        shard = j // 2
        by_z = lax.rem(shard - z + 16, 8)
        by_x = jnp.where(shard // 8 == x, 0, 2)
        inv[order[j]] = 4 * by_z + by_x + lax.rem(j, 2)
        return carry

    lax.fori_loop(0, NB, place, 0)
    for copy in inputs[1:5]:
        copy.wait()

    u_pos = lax.broadcasted_iota(jnp.int32, (BLK, BLK), 0)
    t_pos = lax.broadcasted_iota(jnp.int32, (BLK, BLK), 1)

    def kv(which, j):
        return (k_ref, v_ref)[which][pl.ds(pl.multiple_of(j * BLK, BLK), BLK), :]

    def listed(b, n, s):
        s = jnp.minimum(s, n - 1)
        v = vis[b, s]
        return inv[jnp.where(v < b, v, vis[b, s + 1])]

    def fold(fn, value):
        return functools.reduce(fn, [value[8 * r : 8 * r + 8] for r in range(value.shape[0] // 8)])

    blocks = [order[2 * own + i] for i in range(2)]
    counts = [count[b] - 1 for b in blocks]
    groups = [(n + GROUP - 1) // GROUP for n in counts]
    diags = [0, 1]
    tops, totals, deltas = [], [], []

    def tiles(i, group, which):
        stored = [listed(blocks[i], counts[i], group * GROUP + r) for r in range(GROUP)]
        return stored, jnp.concatenate([kv(which, j) for j in stored], axis=0)

    for i in range(2):
        at = slice(i * BLK, (i + 1) * BLK)
        for h in range(HEADS):
            q_scr[i, h * BLK : (h + 1) * BLK, :] = q_ref[at, h * HD : (h + 1) * HD]
        seg_t = jnp.broadcast_to(seg_ref[pl.ds(blocks[i], 1), :], (BLK, BLK))
        seg_u = jnp.transpose(seg_t)
        seen = (u_pos <= t_pos) & (seg_u == seg_t)
        seen = jnp.concatenate([seen.astype(F32)] * HEADS, axis=1) > 0.5
        scores = jnp.where(seen, nt(kv(0, diags[i]), q_scr[i]), MASKED)
        diag_scr[i] = scores
        tops.append(fold(jnp.maximum, scores))

    for i in range(2):

        def score_pass(group, top, i=i):
            _, keys = tiles(i, group, 0)
            scores = nt(keys, q_scr[i])
            store[i, group] = scores
            return jnp.maximum(top, fold(jnp.maximum, scores))

        tops[i] = lax.fori_loop(0, groups[i], score_pass, tops[i])

    for i in range(2):
        tops[i] = jnp.max(tops[i], axis=0, keepdims=True)
        weights = jnp.exp2((diag_scr[i] - tops[i]) * (SCALE * LOG2E))
        totals.append(fold(jnp.add, weights))
        weights = weights.astype(BF)
        low_diag[i] = weights
        accum[i] = tn(kv(1, diags[i]), weights)

    for i in range(2):

        def value_pass(group, total, i=i):
            lows = []
            for r in range(GROUP):
                base = jnp.where(group * GROUP + r < counts[i], tops[i], -MASKED)
                weights = jnp.exp2((store[i, group, r * BLK : (r + 1) * BLK] - base) * (SCALE * LOG2E))
                total = total + fold(jnp.add, weights)
                lows.append(weights.astype(BF))
            lows = jnp.concatenate(lows, axis=0)
            low[i, group] = lows
            _, values = tiles(i, group, 1)
            accum[i] += tn(values, lows)
            return total

        totals[i] = lax.fori_loop(0, groups[i], value_pass, totals[i])

    def grads(i, weights, values, stored):
        g = g_scr[i]
        grad = (weights.astype(F32) * (nt(values, g) - deltas[i])).astype(BF)
        grad_values = nn(weights, g)
        grad_keys = nn(grad, q_scr[i])
        for r, j in enumerate(stored):
            acc[1, j] += grad_values[r * BLK : (r + 1) * BLK]
            acc[0, j] += grad_keys[r * BLK : (r + 1) * BLK]
        return grad

    inputs[5].wait()
    eighth = jnp.full((16, HD), 0.125, BF)
    ones = jnp.ones((8, HD), BF)
    for i in range(2):
        at = slice(i * BLK, (i + 1) * BLK)
        norm = 1.0 / jnp.sum(totals[i], axis=0, keepdims=True)
        out_low = jnp.transpose((accum[i] * norm).astype(BF))
        norm = jnp.broadcast_to(norm, (8, ROWS))
        high = norm.astype(BF)
        rest_low = (norm - high.astype(F32)).astype(BF)
        norm_col = tn(jnp.concatenate([high, rest_low], axis=0), eighth)
        delta = jnp.zeros((8, ROWS), F32)
        for h in range(HEADS):
            rows = slice(h * BLK, (h + 1) * BLK)
            out_ref[at, h * HD : (h + 1) * HD] = out_low[rows]
            g = g_ref[at, h * HD : (h + 1) * HD].astype(F32)
            g_scr[i, rows, :] = (g * norm_col[rows]).astype(BF)
        g = g_scr[i].astype(F32) * out_low.astype(F32)
        high = g.astype(BF)
        rest_low = (g - high.astype(F32)).astype(BF)
        deltas.append((nt(ones, high) + nt(ones, rest_low))[0:1])
    outputs = [
        pltpu.make_async_copy(out_ref, out_any, io_sem.at[6]),
        pltpu.make_async_copy(dq_ref, dq_any, io_sem.at[7]),
    ]
    outputs[0].start()
    for i in range(2):
        accum[i] = tn(kv(0, diags[i]), grads(i, low_diag[i], kv(1, diags[i]), diags[i : i + 1]))

    for i in range(2):

        def grad_pass(group, carry, i=i):
            stored, values = tiles(i, group, 1)
            _, keys = tiles(i, group, 0)
            accum[i] += tn(keys, grads(i, low[i, group], values, stored))
            return carry

        lax.fori_loop(0, groups[i], grad_pass, 0)

    for i in range(2):
        at = slice(i * BLK, (i + 1) * BLK)
        dq = jnp.transpose((accum[i] * SCALE).astype(BF))
        for h in range(HEADS):
            dq_ref[at, h * HD : (h + 1) * HD] = dq[h * BLK : (h + 1) * BLK]

    outputs[1].start()
    own_scale = jnp.where(core == 0, SCALE, 1.0)
    other_scale = jnp.where(core == 0, 1.0, SCALE)
    for r in range(8):
        at = slice(4 * r, 4 * r + 4)
        mine_ref[r] = (acc[core, at] * own_scale).astype(BF).reshape(4 * BLK, HD)
        other_ref[r] = (acc[1 - core, at] * other_scale).astype(BF).reshape(4 * BLK, HD)
    for copy in outputs:
        copy.wait()


def attention(vis, count, order, query, grad_out, segments, keys, values):
    vmem = pl.BlockSpec(memory_space=pltpu.VMEM)
    hbm = pl.BlockSpec(memory_space=pltpu.HBM)
    part = jax.ShapeDtypeStruct((8, 4 * BLK, HD), BF)
    return pl.pallas_call(
        attention_kernel,
        in_specs=[hbm] * 6 + [vmem] * 2,
        out_specs=[hbm] * 2 + [vmem] * 2,
        out_shape=[
            jax.ShapeDtypeStruct(query.shape, BF),
            jax.ShapeDtypeStruct(query.shape, BF),
            part,
            part,
        ],
        scratch_shapes=[
            pltpu.VMEM((2, 24 // GROUP, GROUP * BLK, ROWS), F32),
            pltpu.VMEM((2, 24 // GROUP, GROUP * BLK, ROWS), BF),
            pltpu.VMEM((2, BLK, ROWS), F32),
            pltpu.VMEM((2, BLK, ROWS), BF),
            pltpu.VMEM((2, HD, ROWS), F32),
            pltpu.VMEM((2, ROWS, HD), BF),
            pltpu.VMEM((2, ROWS, HD), BF),
            pltpu.VMEM((2, NB, BLK, HD), F32),
            pltpu.VMEM(query.shape, BF),
            pltpu.VMEM(query.shape, BF),
            pltpu.VMEM((NB, BLK), jnp.int32),
            pltpu.VMEM(query.shape, BF),
            pltpu.VMEM(query.shape, BF),
            pltpu.SMEM(vis.shape, jnp.int32),
            pltpu.SMEM((NB,), jnp.int32),
            pltpu.SMEM((NB,), jnp.int32),
            pltpu.SMEM((NB,), jnp.int32),
            pltpu.SemaphoreType.DMA((8,)),
        ],
        compiler_params=pltpu.CompilerParams(vmem_limit_bytes=48 * 1024 * 1024),
        name="attention",
    )(vis, count, order, query, grad_out, segments, keys, values)


def assemble_kernel(mine_ref, other_ref, out_ref):
    core = lax.axis_index("core")
    for y in range(4):
        for xh in range(2):
            rows = slice((2 * y + xh) * 2 * BLK, (2 * y + xh + 1) * 2 * BLK)
            for ref, which in ((mine_ref, core), (other_ref, 1 - core)):
                column = pl.multiple_of((2 * (xh * 4 + y) + which) * HD, HD)
                out_ref[:, pl.ds(column, HD)] = ref[rows, :].astype(F32)


def assemble(mine, other):
    vmem = pl.BlockSpec(memory_space=pltpu.VMEM)
    return pl.pallas_call(
        assemble_kernel,
        in_specs=[vmem] * 2,
        out_specs=vmem,
        out_shape=jax.ShapeDtypeStruct((2 * BLK, 2 * KVH * HD), F32),
        compiler_params=pltpu.CompilerParams(vmem_limit_bytes=32 * 1024 * 1024),
        name="assemble",
    )(mine, other)


def wide(*parts):
    return functools.reduce(jnp.add, [p.astype(F32) for p in parts])


def shards(query, keyval, grad_out, vis_blocks, vis_count, segment_ids, block_order):
    xh, y, core = (lax.axis_index(a) for a in ("xh", "y", "core"))
    half = 2 * BLK
    mine = lax.dynamic_slice_in_dim(keyval, ((xh * 4 + y) * 2 + core) * HD, HD, 1)
    both = jnp.concatenate([mine, swap(mine, "x")], axis=0)
    up2, down2 = shift(both, "z", 8, 2), shift(both, "z", 8, -2)
    up1, down1 = shift(both, "z", 8, 1), shift(both, "z", 8, -1)
    up4, down4 = shift(up2[:half], "z", 8, 2), shift(down2[half:], "z", 8, -2)
    up3, down3 = shift(up2, "z", 8, 1), shift(down2, "z", 8, -1)
    mine = jnp.concatenate([both, down1, down2, down3, up4, down4, up3, up2, up1], axis=0)
    other = swap(mine, "core")
    keys, values = jnp.where(core == 0, mine, other), jnp.where(core == 0, other, mine)
    attn_out, grad_query, mine, other = attention(
        vis_blocks, vis_count, block_order, query, grad_out, segment_ids.reshape(NB, BLK), keys, values
    )
    joined = wide(mine, swap(other, "core")).astype(BF)
    for4_up, for4_down = shift(joined[4, :half], "z", 8, 2), shift(joined[4, half:], "z", 8, -2)
    for3_up, for3_down = shift(joined[3], "z", 8, 1), shift(joined[5], "z", 8, -1)
    up2 = jnp.concatenate(
        [wide(joined[2, :half], for3_up[:half], for4_up), wide(joined[2, half:], for3_up[half:])], axis=0
    )
    down2 = jnp.concatenate(
        [wide(joined[6, :half], for3_down[:half]), wide(joined[6, half:], for3_down[half:], for4_down)], axis=0
    )
    for2_up, for2_down = shift(up2.astype(BF), "z", 8, 2), shift(down2.astype(BF), "z", 8, -2)
    near_up, near_down, _ = lax.optimization_barrier((joined[1], joined[7], for3_down))
    for1_up, for1_down = shift(near_up, "z", 8, 1), shift(near_down, "z", 8, -1)
    summed = wide(joined[0], for1_up, for1_down, for2_up, for2_down)
    got = swap(summed[half:].astype(BF), "x")
    summed = wide(summed[:half], got).astype(BF)
    mine = lax.all_to_all(jnp.concatenate([summed] * KVH, axis=0), ("y", "xh"), 0, 0, tiled=True)
    return attn_out, grad_query, assemble(mine, swap(mine, "core"))


def solution(mesh):
    fine = Mesh(mesh.devices.reshape(2, 8, 2, 4, 2), ("x", "z", "xh", "y", "core"))
    ctx, head = ("x", "z"), ("xh", "y", "core")
    return jax.shard_map(
        shards,
        mesh=fine,
        in_specs=(P(ctx, head), P(ctx, None), P(ctx, head), P(), P(), P(), P()),
        out_specs=(P(ctx, head), P(ctx, head), P(ctx, None)),
        check_vma=False,
    )
```

profile of v0, /device:TPU:1, one launch (start us, length us, event | category | flops | bytes accessed | tf_op | source)
XLA Modules:
  0.0 101.3 jit_solution(14402490604737230386)
XLA Ops:
  0.6 0.9 constant_dynamic-update-slice_fusion.9
  1.5 2.1 %collective-permute-start = (bf16[256,128]{1,0:T(8,128)(2,1)S(1)}, bf16[256,128]{1,0:T(8,128)(2,1)S(1)}, u32[]{:S(2)}, u32[]{:S(2)}) collective-permute-start(bf16[256,128]{1,0:T(8,128)(2,1)S(1)} %get-tuple-element.18), channel_id=1, source_target_pairs={{0,128},{128,0},{1,129},{129,1},{2,130},{130,2},{3,131},{131,3},{4... | collective-permute-start | bytes 196616 | tf_op jit(solution)/shard_map/ppermute | solution.py:30
  3.6 1.7 %collective-permute-done = bf16[256,128]{1,0:T(8,128)(2,1)S(1)} collective-permute-done((bf16[256,128]{1,0:T(8,128)(2,1)S(1)}, bf16[256,128]{1,0:T(8,128)(2,1)S(1)}, u32[]{:S(2)}, u32[]{:S(2)}) %collective-permute-start) | collective-permute-done | bytes 65568 | tf_op jit(solution)/shard_map/ppermute | solution.py:30
  5.3 3.3 %collective-permute-start.4 = (bf16[512,128]{1,0:T(8,128)(2,1)S(1)}, bf16[512,128]{1,0:T(8,128)(2,1)S(1)}, u32[]{:S(2)}, u32[]{:S(2)}) collective-permute-start(bf16[512,128]{1,0:T(8,128)(2,1)S(1)} %pad_maximum_fusion), channel_id=1, source_target_pairs={{0,32},{16,48},{32,64},{48,80},{64,96},{80,112},{96,0},{112,16},{1... | collective-permute-start | bytes 393224 | tf_op jit(solution)/shard_map/ppermute | solution.py:26
  8.6 3.1 %collective-permute-start.2 = (bf16[512,128]{1,0:T(8,128)(2,1)S(1)}, bf16[512,128]{1,0:T(8,128)(2,1)S(1)}, u32[]{:S(2)}, u32[]{:S(2)}) collective-permute-start(bf16[512,128]{1,0:T(8,128)(2,1)S(1)} %pad_maximum_fusion), channel_id=1, source_target_pairs={{0,96},{16,112},{32,0},{48,16},{64,32},{80,48},{96,64},{112,80},{1... | collective-permute-start | bytes 393224 | tf_op jit(solution)/shard_map/ppermute | solution.py:26
  11.8 1.8 %collective-permute-start.1 = (bf16[512,128]{1,0:T(8,128)(2,1)S(1)}, bf16[512,128]{1,0:T(8,128)(2,1)S(1)}, u32[]{:S(2)}, u32[]{:S(2)}) collective-permute-start(bf16[512,128]{1,0:T(8,128)(2,1)S(1)} %pad_maximum_fusion), channel_id=1, source_target_pairs={{0,112},{16,0},{32,16},{48,32},{64,48},{80,64},{96,80},{112,96},{1... | collective-permute-start | bytes 393224 | tf_op jit(solution)/shard_map/ppermute | solution.py:26
  13.6 0.5 collective-permute-done.4
  14.1 1.4 %collective-permute-start.5 = (bf16[256,128]{1,0:T(8,128)(2,1)S(1)}, bf16[256,128]{1,0:T(8,128)(2,1)S(1)}, u32[]{:S(2)}, u32[]{:S(2)}) collective-permute-start(bf16[256,128]{1,0:T(8,128)(2,1)S(1)} %slice.77), channel_id=1, source_target_pairs={{0,32},{16,48},{32,64},{48,80},{64,96},{80,112},{96,0},{112,16},{1... | collective-permute-start | bytes 196616 | tf_op jit(solution)/shard_map/ppermute | solution.py:26
  15.6 2.1 %collective-permute-done.2 = bf16[512,128]{1,0:T(8,128)(2,1)S(1)} collective-permute-done((bf16[512,128]{1,0:T(8,128)(2,1)S(1)}, bf16[512,128]{1,0:T(8,128)(2,1)S(1)}, u32[]{:S(2)}, u32[]{:S(2)}) %collective-permute-start.2) | collective-permute-done | bytes 131104 | tf_op jit(solution)/shard_map/ppermute | solution.py:26
  17.6 2.1 %collective-permute-start.6 = (bf16[256,128]{1,0:T(8,128)(2,1)S(1)}, bf16[256,128]{1,0:T(8,128)(2,1)S(1)}, u32[]{:S(2)}, u32[]{:S(2)}) collective-permute-start(bf16[256,128]{1,0:T(8,128)(2,1)S(1)} %slice.78), channel_id=1, source_target_pairs={{0,96},{16,112},{32,0},{48,16},{64,32},{80,48},{96,64},{112,80},{1... | collective-permute-start | bytes 196616 | tf_op jit(solution)/shard_map/ppermute | solution.py:26
  19.7 2.5 %collective-permute-start.7 = (bf16[512,128]{1,0:T(8,128)(2,1)S(1)}, bf16[512,128]{1,0:T(8,128)(2,1)S(1)}, u32[]{:S(2)}, u32[]{:S(2)}) collective-permute-start(bf16[512,128]{1,0:T(8,128)(2,1)S(1)} %collective-permute-done.4), channel_id=1, source_target_pairs={{0,16},{16,32},{32,48},{48,64},{64,80},{80,96},{96,112},{112,0},{1... | collective-permute-start | bytes 393224 | tf_op jit(solution)/shard_map/ppermute | solution.py:26
  22.3 0.5 collective-permute-start.3
  22.8 4.0 %collective-permute-done.3 = bf16[512,128]{1,0:T(8,128)(2,1)S(1)} collective-permute-done((bf16[512,128]{1,0:T(8,128)(2,1)S(1)}, bf16[512,128]{1,0:T(8,128)(2,1)S(1)}, u32[]{:S(2)}, u32[]{:S(2)}) %collective-permute-start.3) | collective-permute-done | bytes 131104 | tf_op jit(solution)/shard_map/ppermute | solution.py:26
  27.0 3.5 %collective-permute-start.9 = (bf16[4096,128]{1,0:T(8,128)(2,1)S(1)}, bf16[4096,128]{1,0:T(8,128)(2,1)S(1)}, u32[]{:S(2)}, u32[]{:S(2)}) collective-permute-start(bf16[4096,128]{1,0:T(8,128)(2,1)S(1)} %constant_dynamic-update-slice_fusion), channel_id=1, source_target_pairs={{0,1},{1,0},{2,3},{3,2},{4,5},{5,4},{6,7},{7,6},{8,9},{9,8},{10,11... | collective-permute-start | bytes 3145736 | tf_op jit(solution)/shard_map/ppermute | solution.py:30
  30.7 2.2 %collective-permute-done.9 = bf16[4096,128]{1,0:T(8,128)(2,1)S(1)} collective-permute-done((bf16[4096,128]{1,0:T(8,128)(2,1)S(1)}, bf16[4096,128]{1,0:T(8,128)(2,1)S(1)}, u32[]{:S(2)}, u32[]{:S(2)}) %collective-permute-start.9) | collective-permute-done | bytes 1048608 | tf_op jit(solution)/shard_map/ppermute | solution.py:30
  33.0 11.5 %attention.1 = (bf16[256,512]{1,0:T(8,128)(2,1)}, bf16[256,512]{1,0:T(8,128)(2,1)}, bf16[8,512,128]{2,1,0:T(8,128)(2,1)S(1)}, bf16[8,512,128]{2,1,0:T(8,128)(2,1)S(1)}) custom-call(s32[32,24]{1,0:T(8,128)S(1)} %copy.10.vis_any, s32[32]{0:T(128)S(1)} %copy-done.3, s32[32]{0:T(128)S(1)} %copy-done.4, bf16[256,512]{1,0:T(8,128)(2,1)S(1)} %copy-done, ...), custom_call_target="tpu_custom_call" | custom-call | tf_op jit(solution)/shard_map/attention/pallas_call | solution.py:219
  44.6 0.6 collective-permute-start.10
  45.2 2.3 %collective-permute-done.10 = bf16[8,512,128]{2,1,0:T(8,128)(2,1)S(1)} collective-permute-done((bf16[8,512,128]{2,1,0:T(8,128)(2,1)S(1)}, bf16[8,512,128]{2,1,0:T(8,128)(2,1)S(1)}, u32[]{:S(2)}, u32[]{:S(2)}) %collective-permute-start.10) | collective-permute-done | bytes 1048608 | tf_op jit(solution)/shard_map/ppermute | solution.py:30
  47.9 6.0 %collective-permute-start.11 = (bf16[512,128]{1,0:T(8,128)(2,1)S(1)}, bf16[512,128]{1,0:T(8,128)(2,1)S(1)}, u32[]{:S(2)}, u32[]{:S(2)}) collective-permute-start(bf16[512,128]{1,0:T(8,128)(2,1)S(1)} %get-tuple-element.27), channel_id=1, source_target_pairs={{0,112},{16,0},{32,16},{48,32},{64,48},{80,64},{96,80},{112,96},{1... | collective-permute-start | bytes 393224 | tf_op jit(solution)/shard_map/ppermute | solution.py:26
  54.1 3.6 %collective-permute-start.17 = (bf16[256,128]{1,0:T(8,128)(2,1)S(1)}, bf16[256,128]{1,0:T(8,128)(2,1)S(1)}, u32[]{:S(2)}, u32[]{:S(2)}) collective-permute-start(bf16[256,128]{1,0:T(8,128)(2,1)S(1)} %get-tuple-element.32), channel_id=1, source_target_pairs={{0,96},{16,112},{32,0},{48,16},{64,32},{80,48},{96,64},{112,80},{1... | collective-permute-start | bytes 196616 | tf_op jit(solution)/shard_map/ppermute | solution.py:26
  57.6 4.0 %collective-permute-done.15 = bf16[256,128]{1,0:T(8,128)(2,1)S(1)} collective-permute-done((bf16[256,128]{1,0:T(8,128)(2,1)S(1)}, bf16[256,128]{1,0:T(8,128)(2,1)S(1)}, u32[]{:S(2)}, u32[]{:S(2)}) %collective-permute-start.15) | collective-permute-done | bytes 65568 | tf_op jit(solution)/shard_map/ppermute | solution.py:26
  61.6 1.1 %collective-permute-done.17 = bf16[256,128]{1,0:T(8,128)(2,1)S(1)} collective-permute-done((bf16[256,128]{1,0:T(8,128)(2,1)S(1)}, bf16[256,128]{1,0:T(8,128)(2,1)S(1)}, u32[]{:S(2)}, u32[]{:S(2)}) %collective-permute-start.17) | collective-permute-done | bytes 65568 | tf_op jit(solution)/shard_map/ppermute | solution.py:26
  62.8 0.9 collective-permute-start.18
  63.7 2.7 %collective-permute-start.13 = (bf16[512,128]{1,0:T(8,128)(2,1)S(1)}, bf16[512,128]{1,0:T(8,128)(2,1)S(1)}, u32[]{:S(2)}, u32[]{:S(2)}) collective-permute-start(bf16[512,128]{1,0:T(8,128)(2,1)S(1)} %get-tuple-element.14), channel_id=1, source_target_pairs={{0,112},{16,0},{32,16},{48,32},{64,48},{80,64},{96,80},{112,96},{1... | collective-permute-start | bytes 393224 | tf_op jit(solution)/shard_map/ppermute | solution.py:26
  66.4 0.4 collective-permute-start.16
  66.8 4.7 %collective-permute-done.18 = bf16[512,128]{1,0:T(8,128)(2,1)S(1)} collective-permute-done((bf16[512,128]{1,0:T(8,128)(2,1)S(1)}, bf16[512,128]{1,0:T(8,128)(2,1)S(1)}, u32[]{:S(2)}, u32[]{:S(2)}) %collective-permute-start.18) | collective-permute-done | bytes 131104 | tf_op jit(solution)/shard_map/ppermute | solution.py:26
  71.5 1.7 %collective-permute-done.16 = bf16[512,128]{1,0:T(8,128)(2,1)S(1)} collective-permute-done((bf16[512,128]{1,0:T(8,128)(2,1)S(1)}, bf16[512,128]{1,0:T(8,128)(2,1)S(1)}, u32[]{:S(2)}, u32[]{:S(2)}) %collective-permute-start.16) | collective-permute-done | bytes 131104 | tf_op jit(solution)/shard_map/ppermute | solution.py:26
  73.5 3.1 %collective-permute-done.19 = bf16[256,128]{1,0:T(8,128)(2,1)S(1)} collective-permute-done((bf16[256,128]{1,0:T(8,128)(2,1)S(1)}, bf16[256,128]{1,0:T(8,128)(2,1)S(1)}, u32[]{:S(2)}, u32[]{:S(2)}) %collective-permute-start.19) | collective-permute-done | bytes 65568 | tf_op jit(solution)/shard_map/ppermute | solution.py:30
  76.7 15.5 %all_to_all.11 = bf16[8,256,128]{2,1,0:T(8,128)(2,1)S(1)} all-to-all(bf16[8,256,128]{2,1,0:T(8,128)(2,1)S(1)} %bitcast.43), channel_id=1, replica_groups=mesh['x'=2,'z'=8,'xh'=2,'y'=4,'core'=2] {'y','xh'}, dimensions={0} | all-to-all | bytes 1048576 | tf_op jit(solution)/shard_map/all_to_all | solution.py:310
  92.2 6.0 %collective-permute-start.20 = (bf16[2048,128]{1,0:T(8,128)(2,1)S(1)}, bf16[2048,128]{1,0:T(8,128)(2,1)S(1)}, u32[]{:S(2)}, u32[]{:S(2)}) collective-permute-start(bf16[2048,128]{1,0:T(8,128)(2,1)S(1)} %bitcast.40), channel_id=1, source_target_pairs={{0,1},{1,0},{2,3},{3,2},{4,5},{5,4},{6,7},{7,6},{8,9},{9,8},{10,11... | collective-permute-start | bytes 1572872 | tf_op jit(solution)/shard_map/ppermute | solution.py:30
  98.1 1.5 %collective-permute-done.20.other_ref = bf16[2048,128]{1,0:T(8,128)(2,1)S(1)} collective-permute-done((bf16[2048,128]{1,0:T(8,128)(2,1)S(1)}, bf16[2048,128]{1,0:T(8,128)(2,1)S(1)}, u32[]{:S(2)}, u32[]{:S(2)}) %collective-permute-start.20) | collective-permute-done | bytes 524320 | tf_op jit(solution)/shard_map/ppermute | solution.py:30
  99.7 1.6 %assemble.1 = f32[256,2048]{1,0:T(8,128)} custom-call(bf16[2048,128]{1,0:T(8,128)(2,1)S(1)} %bitcast.41, bf16[2048,128]{1,0:T(8,128)(2,1)S(1)} %collective-permute-done.20.other_ref), custom_call_target="tpu_custom_call" | custom-call | tf_op jit(solution)/shard_map/assemble/pallas_call | solution.py:266
  (56 shorter events, 1.4 us)
Async XLA Ops:
  0.6 29.9 %copy-start.5 = (s32[32,24]{0,1:T(8,128)S(1)}, s32[32,24]{0,1:T(8,128)}, u32[]{:S(2)}) copy-start(s32[32,24]{0,1:T(8,128)} %param.10) | copy-start | bytes 9220
  1.5 3.8 %collective-permute-start = (bf16[256,128]{1,0:T(8,128)(2,1)S(1)}, bf16[256,128]{1,0:T(8,128)(2,1)S(1)}, u32[]{:S(2)}, u32[]{:S(2)}) collective-permute-start(bf16[256,128]{1,0:T(8,128)(2,1)S(1)} %get-tuple-element.18), channel_id=1, source_target_pairs={{0,128},{128,0},{1,129},{129,1},{2,130},{130,2},{3,131},{131,3},{4... | collective-permute-start | bytes 196616 | tf_op jit(solution)/shard_map/ppermute | solution.py:30
  5.3 8.8 %collective-permute-start.4 = (bf16[512,128]{1,0:T(8,128)(2,1)S(1)}, bf16[512,128]{1,0:T(8,128)(2,1)S(1)}, u32[]{:S(2)}, u32[]{:S(2)}) collective-permute-start(bf16[512,128]{1,0:T(8,128)(2,1)S(1)} %pad_maximum_fusion), channel_id=1, source_target_pairs={{0,32},{16,48},{32,64},{48,80},{64,96},{80,112},{96,0},{112,16},{1... | collective-permute-start | bytes 393224 | tf_op jit(solution)/shard_map/ppermute | solution.py:26
  8.6 9.0 %collective-permute-start.2 = (bf16[512,128]{1,0:T(8,128)(2,1)S(1)}, bf16[512,128]{1,0:T(8,128)(2,1)S(1)}, u32[]{:S(2)}, u32[]{:S(2)}) collective-permute-start(bf16[512,128]{1,0:T(8,128)(2,1)S(1)} %pad_maximum_fusion), channel_id=1, source_target_pairs={{0,96},{16,112},{32,0},{48,16},{64,32},{80,48},{96,64},{112,80},{1... | collective-permute-start | bytes 393224 | tf_op jit(solution)/shard_map/ppermute | solution.py:26
  11.8 10.5 %collective-permute-start.1 = (bf16[512,128]{1,0:T(8,128)(2,1)S(1)}, bf16[512,128]{1,0:T(8,128)(2,1)S(1)}, u32[]{:S(2)}, u32[]{:S(2)}) collective-permute-start(bf16[512,128]{1,0:T(8,128)(2,1)S(1)} %pad_maximum_fusion), channel_id=1, source_target_pairs={{0,112},{16,0},{32,16},{48,32},{64,48},{80,64},{96,80},{112,96},{1... | collective-permute-start | bytes 393224 | tf_op jit(solution)/shard_map/ppermute | solution.py:26
  13.6 13.4 %collective-permute-start.8 = (bf16[512,128]{1,0:T(8,128)(2,1)S(1)}, bf16[512,128]{1,0:T(8,128)(2,1)S(1)}, u32[]{:S(2)}, u32[]{:S(2)}) collective-permute-start(bf16[512,128]{1,0:T(8,128)(2,1)S(1)} %pad_maximum_fusion), channel_id=1, source_target_pairs={{0,16},{16,32},{32,48},{48,64},{64,80},{80,96},{96,112},{112,0},{1... | collective-permute-start | bytes 393224 | tf_op jit(solution)/shard_map/ppermute | solution.py:26
  14.1 12.8 %collective-permute-start.5 = (bf16[256,128]{1,0:T(8,128)(2,1)S(1)}, bf16[256,128]{1,0:T(8,128)(2,1)S(1)}, u32[]{:S(2)}, u32[]{:S(2)}) collective-permute-start(bf16[256,128]{1,0:T(8,128)(2,1)S(1)} %slice.77), channel_id=1, source_target_pairs={{0,32},{16,48},{32,64},{48,80},{64,96},{80,112},{96,0},{112,16},{1... | collective-permute-start | bytes 196616 | tf_op jit(solution)/shard_map/ppermute | solution.py:26
  17.6 9.3 %collective-permute-start.6 = (bf16[256,128]{1,0:T(8,128)(2,1)S(1)}, bf16[256,128]{1,0:T(8,128)(2,1)S(1)}, u32[]{:S(2)}, u32[]{:S(2)}) collective-permute-start(bf16[256,128]{1,0:T(8,128)(2,1)S(1)} %slice.78), channel_id=1, source_target_pairs={{0,96},{16,112},{32,0},{48,16},{64,32},{80,48},{96,64},{112,80},{1... | collective-permute-start | bytes 196616 | tf_op jit(solution)/shard_map/ppermute | solution.py:26
  19.7 7.2 %collective-permute-start.7 = (bf16[512,128]{1,0:T(8,128)(2,1)S(1)}, bf16[512,128]{1,0:T(8,128)(2,1)S(1)}, u32[]{:S(2)}, u32[]{:S(2)}) collective-permute-start(bf16[512,128]{1,0:T(8,128)(2,1)S(1)} %collective-permute-done.4), channel_id=1, source_target_pairs={{0,16},{16,32},{32,48},{48,64},{64,80},{80,96},{96,112},{112,0},{1... | collective-permute-start | bytes 393224 | tf_op jit(solution)/shard_map/ppermute | solution.py:26
  22.3 4.6 %collective-permute-start.3 = (bf16[512,128]{1,0:T(8,128)(2,1)S(1)}, bf16[512,128]{1,0:T(8,128)(2,1)S(1)}, u32[]{:S(2)}, u32[]{:S(2)}) collective-permute-start(bf16[512,128]{1,0:T(8,128)(2,1)S(1)} %collective-permute-done.2), channel_id=1, source_target_pairs={{0,112},{16,0},{32,16},{48,32},{64,48},{80,64},{96,80},{112,96},{1... | collective-permute-start | bytes 393224 | tf_op jit(solution)/shard_map/ppermute | solution.py:26
  27.0 5.8 %collective-permute-start.9 = (bf16[4096,128]{1,0:T(8,128)(2,1)S(1)}, bf16[4096,128]{1,0:T(8,128)(2,1)S(1)}, u32[]{:S(2)}, u32[]{:S(2)}) collective-permute-start(bf16[4096,128]{1,0:T(8,128)(2,1)S(1)} %constant_dynamic-update-slice_fusion), channel_id=1, source_target_pairs={{0,1},{1,0},{2,3},{3,2},{4,5},{5,4},{6,7},{7,6},{8,9},{9,8},{10,11... | collective-permute-start | bytes 3145736 | tf_op jit(solution)/shard_map/ppermute | solution.py:30
  30.6 2.4 %copy-start = (bf16[256,512]{1,0:T(8,128)(2,1)S(1)}, bf16[256,512]{1,0:T(8,128)(2,1)}, u32[]{:S(2)}) copy-start(bf16[256,512]{1,0:T(8,128)(2,1)} %q_any.1) | copy-start | bytes 786436
  30.6 2.4 %copy-start.1 = (bf16[256,512]{1,0:T(8,128)(2,1)S(1)}, bf16[256,512]{1,0:T(8,128)(2,1)}, u32[]{:S(2)}) copy-start(bf16[256,512]{1,0:T(8,128)(2,1)} %g_any.1) | copy-start | bytes 786436
  30.6 2.4 %copy-start.2 = (s32[4096]{0:T(1024)S(1)}, s32[4096]{0:T(1024)}, u32[]{:S(2)}) copy-start(s32[4096]{0:T(1024)} %param.12) | copy-start | bytes 49156
  30.6 2.4 %copy-start.3 = (s32[32]{0:T(128)S(1)}, s32[32]{0:T(128)}, u32[]{:S(2)}) copy-start(s32[32]{0:T(128)} %count_any.1) | copy-start | bytes 388
  30.6 2.4 %copy-start.4 = (s32[32]{0:T(128)S(1)}, s32[32]{0:T(128)}, u32[]{:S(2)}) copy-start(s32[32]{0:T(128)} %order_any.1) | copy-start | bytes 388
  44.6 2.9 %collective-permute-start.10 = (bf16[8,512,128]{2,1,0:T(8,128)(2,1)S(1)}, bf16[8,512,128]{2,1,0:T(8,128)(2,1)S(1)}, u32[]{:S(2)}, u32[]{:S(2)}) collective-permute-start(bf16[8,512,128]{2,1,0:T(8,128)(2,1)S(1)} %get-tuple-element.12), channel_id=1, source_target_pairs={{0,1},{1,0},{2,3},{3,2},{4,5},{5,4},{6,7},{7,6},{8,9},{9,8},{10,11... | collective-permute-start | bytes 3145736 | tf_op jit(solution)/shard_map/ppermute | solution.py:30
  47.8 14.9 %collective-permute-start.14 = (bf16[512,128]{1,0:T(8,128)(2,1)S(1)}, bf16[512,128]{1,0:T(8,128)(2,1)S(1)}, u32[]{:S(2)}, u32[]{:S(2)}) collective-permute-start(bf16[512,128]{1,0:T(8,128)(2,1)S(1)} %get-tuple-element.26), channel_id=1, source_target_pairs={{0,16},{16,32},{32,48},{48,64},{64,80},{80,96},{96,112},{112,0},{1... | collective-permute-start | bytes 393224 | tf_op jit(solution)/shard_map/ppermute | solution.py:26
  47.9 9.7 %collective-permute-start.11 = (bf16[512,128]{1,0:T(8,128)(2,1)S(1)}, bf16[512,128]{1,0:T(8,128)(2,1)S(1)}, u32[]{:S(2)}, u32[]{:S(2)}) collective-permute-start(bf16[512,128]{1,0:T(8,128)(2,1)S(1)} %get-tuple-element.27), channel_id=1, source_target_pairs={{0,112},{16,0},{32,16},{48,32},{64,48},{80,64},{96,80},{112,96},{1... | collective-permute-start | bytes 393224 | tf_op jit(solution)/shard_map/ppermute | solution.py:26
  54.0 7.6 %collective-permute-start.15 = (bf16[256,128]{1,0:T(8,128)(2,1)S(1)}, bf16[256,128]{1,0:T(8,128)(2,1)S(1)}, u32[]{:S(2)}, u32[]{:S(2)}) collective-permute-start(bf16[256,128]{1,0:T(8,128)(2,1)S(1)} %get-tuple-element.31), channel_id=1, source_target_pairs={{0,32},{16,48},{32,64},{48,80},{64,96},{80,112},{96,0},{112,16},{1... | collective-permute-start | bytes 196616 | tf_op jit(solution)/shard_map/ppermute | solution.py:26
  54.1 8.7 %collective-permute-start.17 = (bf16[256,128]{1,0:T(8,128)(2,1)S(1)}, bf16[256,128]{1,0:T(8,128)(2,1)S(1)}, u32[]{:S(2)}, u32[]{:S(2)}) collective-permute-start(bf16[256,128]{1,0:T(8,128)(2,1)S(1)} %get-tuple-element.32), channel_id=1, source_target_pairs={{0,96},{16,112},{32,0},{48,16},{64,32},{80,48},{96,64},{112,80},{1... | collective-permute-start | bytes 196616 | tf_op jit(solution)/shard_map/ppermute | solution.py:26
  62.8 8.7 %collective-permute-start.18 = (bf16[512,128]{1,0:T(8,128)(2,1)S(1)}, bf16[512,128]{1,0:T(8,128)(2,1)S(1)}, u32[]{:S(2)}, u32[]{:S(2)}) collective-permute-start(bf16[512,128]{1,0:T(8,128)(2,1)S(1)} %pad_maximum_fusion.2), channel_id=1, source_target_pairs={{0,96},{16,112},{32,0},{48,16},{64,32},{80,48},{96,64},{112,80},{1... | collective-permute-start | bytes 393224 | tf_op jit(solution)/shard_map/ppermute | solution.py:26
  63.7 7.8 %collective-permute-start.12 = (bf16[512,128]{1,0:T(8,128)(2,1)S(1)}, bf16[512,128]{1,0:T(8,128)(2,1)S(1)}, u32[]{:S(2)}, u32[]{:S(2)}) collective-permute-start(bf16[512,128]{1,0:T(8,128)(2,1)S(1)} %get-tuple-element.13), channel_id=1, source_target_pairs={{0,16},{16,32},{32,48},{48,64},{64,80},{80,96},{96,112},{112,0},{1... | collective-permute-start | bytes 393224 | tf_op jit(solution)/shard_map/ppermute | solution.py:26
  63.7 7.8 %collective-permute-start.13 = (bf16[512,128]{1,0:T(8,128)(2,1)S(1)}, bf16[512,128]{1,0:T(8,128)(2,1)S(1)}, u32[]{:S(2)}, u32[]{:S(2)}) collective-permute-start(bf16[512,128]{1,0:T(8,128)(2,1)S(1)} %get-tuple-element.14), channel_id=1, source_target_pairs={{0,112},{16,0},{32,16},{48,32},{64,48},{80,64},{96,80},{112,96},{1... | collective-permute-start | bytes 393224 | tf_op jit(solution)/shard_map/ppermute | solution.py:26
  66.4 6.8 %collective-permute-start.16 = (bf16[512,128]{1,0:T(8,128)(2,1)S(1)}, bf16[512,128]{1,0:T(8,128)(2,1)S(1)}, u32[]{:S(2)}, u32[]{:S(2)}) collective-permute-start(bf16[512,128]{1,0:T(8,128)(2,1)S(1)} %pad_maximum_fusion.1), channel_id=1, source_target_pairs={{0,32},{16,48},{32,64},{48,80},{64,96},{80,112},{96,0},{112,16},{1... | collective-permute-start | bytes 393224 | tf_op jit(solution)/shard_map/ppermute | solution.py:26
  73.3 3.2 %collective-permute-start.19 = (bf16[256,128]{1,0:T(8,128)(2,1)S(1)}, bf16[256,128]{1,0:T(8,128)(2,1)S(1)}, u32[]{:S(2)}, u32[]{:S(2)}) collective-permute-start(bf16[256,128]{1,0:T(8,128)(2,1)S(1)} %slice.125), channel_id=1, source_target_pairs={{0,128},{128,0},{1,129},{129,1},{2,130},{130,2},{3,131},{131,3},{4... | collective-permute-start | bytes 196616 | tf_op jit(solution)/shard_map/ppermute | solution.py:30
  92.2 7.5 %collective-permute-start.20 = (bf16[2048,128]{1,0:T(8,128)(2,1)S(1)}, bf16[2048,128]{1,0:T(8,128)(2,1)S(1)}, u32[]{:S(2)}, u32[]{:S(2)}) collective-permute-start(bf16[2048,128]{1,0:T(8,128)(2,1)S(1)} %bitcast.40), channel_id=1, source_target_pairs={{0,1},{1,0},{2,3},{3,2},{4,5},{5,4},{6,7},{7,6},{8,9},{9,8},{10,11... | collective-permute-start | bytes 1572872 | tf_op jit(solution)/shard_map/ppermute | solution.py:30
where the time goes:
time: 100 us; the launch traced here: 101 us
  starting transfers between devices  41 us (41%)
  waiting for transfers between devices  28.8 us (29%)
  blocking collectives  15.5 us (16%)
  Pallas kernels  13.1 us (13%)
  local copies, waits for them, and re-layouts  1.29 us (1%)
    ppermute x16, starting transfers between devices, shift(): lax.ppermute(value, axis, [(i, (i + by) % size) for i in range(size)])  28.6 us
    ppermute x16, waiting for transfers between devices, shift(): lax.ppermute(value, axis, [(i, (i + by) % size) for i in range(size)])  18.1 us
    all_to_all x1, blocking collectives, shards(): lax.all_to_all(jnp.concatenate([summed] * KVH, axis=0), ('y', 'xh'), 0, 0...  15.5 us
    ppermute x5, starting transfers between devices, swap(): return lax.ppermute(value, axis, [(0, 1), (1, 0)])  12.4 us
    pallas_call x1, Pallas kernels, attention(): pl.pallas_call(attention_kernel, in_specs=[hbm] * 6 + [vmem] * 2, out_spe...  11.5 us
    ppermute x5, waiting for transfers between devices, swap(): return lax.ppermute(value, axis, [(0, 1), (1, 0)])  10.7 us
  transfers between devices with their start and end apart: 21, of which 12 were waited for; matrix products, arithmetic and copies ran while one was open for 0% of the time, Pallas kernels for 0%

commit v1 on v0

--- a/solution.py
+++ b/solution.py
@@ -14,6 +14,8 @@
 NB = 32
 HEADS = 4
 GROUP = 4
+REACHED = (0, 1, 2, 6, 7)
+RELAYED = (3, 4, 5)
 ROWS = HEADS * BLK
 SCALE = HD**-0.5
 LOG2E = 1.4426950408889634
@@ -43,9 +45,9 @@
 
 
 def attention_kernel(
-    vis_any, count_any, order_any, q_any, g_any, seg_any, k_ref, v_ref,
-    out_any, dq_any, mine_ref, other_ref,
-    store, low, diag_scr, low_diag, accum, q_scr, g_scr, acc, q_ref, g_ref, seg_ref, out_ref, dq_ref,
+    vis_any, count_any, order_any, q_any, g_any, seg_any, kv_ref,
+    out_any, dq_any, other_relayed_ref, mine_relayed_ref, other_ref, mine_ref,
+    store, low, accum, q_scr, g_scr, acc, q_ref, g_ref, seg_ref, out_ref, dq_ref,
     vis, count, order, inv, io_sem,
 ):
     x, z, core = lax.axis_index("x"), lax.axis_index("z"), lax.axis_index("core")
@@ -67,8 +69,8 @@
     def place(j, carry):
         shard = j // 2
         by_z = lax.rem(shard - z + 16, 8)
-        by_x = jnp.where(shard // 8 == x, 0, 2)
-        inv[order[j]] = 4 * by_z + by_x + lax.rem(j, 2)
+        at = jnp.where(by_z < 3, by_z, jnp.where(by_z > 5, by_z - 3, by_z + 2))
+        inv[order[j]] = jnp.where(shard // 8 == x, 0, 16) + 2 * at + lax.rem(j, 2)
         return carry
 
     lax.fori_loop(0, NB, place, 0)
@@ -79,24 +81,24 @@
     t_pos = lax.broadcasted_iota(jnp.int32, (BLK, BLK), 1)
 
     def kv(which, j):
-        return (k_ref, v_ref)[which][pl.ds(pl.multiple_of(j * BLK, BLK), BLK), :]
-
-    def listed(b, n, s):
-        s = jnp.minimum(s, n - 1)
-        v = vis[b, s]
-        return inv[jnp.where(v < b, v, vis[b, s + 1])]
+        return kv_ref[pl.ds(pl.multiple_of(j * BLK, BLK), BLK), which * HD : (which + 1) * HD]
+
+    def listed(i, s):
+        s = jnp.minimum(s, counts[i] - 1)
+        b = blocks[i]
+        v = vis[b, jnp.maximum(s - 1, 0)]
+        return jnp.where(s == 0, i, inv[jnp.where(v < b, v, vis[b, s])])
 
     def fold(fn, value):
         return functools.reduce(fn, [value[8 * r : 8 * r + 8] for r in range(value.shape[0] // 8)])
 
     blocks = [order[2 * own + i] for i in range(2)]
-    counts = [count[b] - 1 for b in blocks]
+    counts = [count[b] for b in blocks]
     groups = [(n + GROUP - 1) // GROUP for n in counts]
-    diags = [0, 1]
     tops, totals, deltas = [], [], []
 
     def tiles(i, group, which):
-        stored = [listed(blocks[i], counts[i], group * GROUP + r) for r in range(GROUP)]
+        stored = [listed(i, group * GROUP + r) for r in range(GROUP)]
         return stored, jnp.concatenate([kv(which, j) for j in stored], axis=0)
 
     for i in range(2):
@@ -107,9 +109,16 @@
         seg_u = jnp.transpose(seg_t)
         seen = (u_pos <= t_pos) & (seg_u == seg_t)
         seen = jnp.concatenate([seen.astype(F32)] * HEADS, axis=1) > 0.5
-        scores = jnp.where(seen, nt(kv(0, diags[i]), q_scr[i]), MASKED)
-        diag_scr[i] = scores
-        tops.append(fold(jnp.maximum, scores))
+        _, keys = tiles(i, 0, 0)
+        scores = nt(keys, q_scr[i])
+        for r in range(GROUP):
+            ok = seen if r == 0 else counts[i] > r
+            part = jnp.where(ok, scores[r * BLK : (r + 1) * BLK], MASKED)
+            store[i, 0, r * BLK : (r + 1) * BLK] = part
+            top = fold(jnp.maximum, part) if r == 0 else jnp.maximum(top, fold(jnp.maximum, part))
+        tops.append(top)
+        totals.append(jnp.zeros((8, ROWS), F32))
+        accum[i] = jnp.zeros((HD, ROWS), F32)
 
     for i in range(2):
 
@@ -119,15 +128,10 @@
             store[i, group] = scores
             return jnp.maximum(top, fold(jnp.maximum, scores))
 
-        tops[i] = lax.fori_loop(0, groups[i], score_pass, tops[i])
+        tops[i] = lax.fori_loop(1, groups[i], score_pass, tops[i])
 
     for i in range(2):
         tops[i] = jnp.max(tops[i], axis=0, keepdims=True)
-        weights = jnp.exp2((diag_scr[i] - tops[i]) * (SCALE * LOG2E))
-        totals.append(fold(jnp.add, weights))
-        weights = weights.astype(BF)
-        low_diag[i] = weights
-        accum[i] = tn(kv(1, diags[i]), weights)
 
     for i in range(2):
 
@@ -183,7 +187,7 @@
     ]
     outputs[0].start()
     for i in range(2):
-        accum[i] = tn(kv(0, diags[i]), grads(i, low_diag[i], kv(1, diags[i]), diags[i : i + 1]))
+        accum[i] = jnp.zeros((HD, ROWS), F32)
 
     for i in range(2):
 
@@ -202,35 +206,36 @@
             dq_ref[at, h * HD : (h + 1) * HD] = dq[h * BLK : (h + 1) * BLK]
 
     outputs[1].start()
-    own_scale = jnp.where(core == 0, SCALE, 1.0)
-    other_scale = jnp.where(core == 0, 1.0, SCALE)
-    for r in range(8):
-        at = slice(4 * r, 4 * r + 4)
-        mine_ref[r] = (acc[core, at] * own_scale).astype(BF).reshape(4 * BLK, HD)
-        other_ref[r] = (acc[1 - core, at] * other_scale).astype(BF).reshape(4 * BLK, HD)
+    for ref, side, start in (
+        (other_relayed_ref, 1 - core, 5),
+        (mine_relayed_ref, core, 5),
+        (other_ref, 1 - core, 0),
+        (mine_ref, core, 0),
+    ):
+        for r in range(ref.shape[0]):
+            at = pl.ds(16 * side + 2 * (start + r), 2)
+            ref[r, :, :HD] = (acc[0, at] * SCALE).astype(BF).reshape(2 * BLK, HD)
+            ref[r, :, HD:] = acc[1, at].astype(BF).reshape(2 * BLK, HD)
     for copy in outputs:
         copy.wait()
 
 
-def attention(vis, count, order, query, grad_out, segments, keys, values):
+def attention(vis, count, order, query, grad_out, segments, gathered):
     vmem = pl.BlockSpec(memory_space=pltpu.VMEM)
     hbm = pl.BlockSpec(memory_space=pltpu.HBM)
-    part = jax.ShapeDtypeStruct((8, 4 * BLK, HD), BF)
+    parts = [jax.ShapeDtypeStruct((n, 2 * BLK, 2 * HD), BF) for n in (len(RELAYED), len(REACHED)) for _ in range(2)]
     return pl.pallas_call(
         attention_kernel,
-        in_specs=[hbm] * 6 + [vmem] * 2,
-        out_specs=[hbm] * 2 + [vmem] * 2,
+        in_specs=[hbm] * 6 + [vmem],
+        out_specs=[hbm] * 2 + [vmem] * 4,
         out_shape=[
             jax.ShapeDtypeStruct(query.shape, BF),
             jax.ShapeDtypeStruct(query.shape, BF),
-            part,
-            part,
+            *parts,
         ],
         scratch_shapes=[
             pltpu.VMEM((2, 24 // GROUP, GROUP * BLK, ROWS), F32),
             pltpu.VMEM((2, 24 // GROUP, GROUP * BLK, ROWS), BF),
-            pltpu.VMEM((2, BLK, ROWS), F32),
-            pltpu.VMEM((2, BLK, ROWS), BF),
             pltpu.VMEM((2, HD, ROWS), F32),
             pltpu.VMEM((2, ROWS, HD), BF),
             pltpu.VMEM((2, ROWS, HD), BF),
@@ -248,7 +253,7 @@
         ],
         compiler_params=pltpu.CompilerParams(vmem_limit_bytes=48 * 1024 * 1024),
         name="attention",
-    )(vis, count, order, query, grad_out, segments, keys, values)
+    )(vis, count, order, query, grad_out, segments, gathered)
 
 
 def assemble_kernel(mine_ref, other_ref, out_ref):
@@ -279,34 +284,51 @@
 
 def shards(query, keyval, grad_out, vis_blocks, vis_count, segment_ids, block_order):
     xh, y, core = (lax.axis_index(a) for a in ("xh", "y", "core"))
-    half = 2 * BLK
-    mine = lax.dynamic_slice_in_dim(keyval, ((xh * 4 + y) * 2 + core) * HD, HD, 1)
-    both = jnp.concatenate([mine, swap(mine, "x")], axis=0)
-    up2, down2 = shift(both, "z", 8, 2), shift(both, "z", 8, -2)
-    up1, down1 = shift(both, "z", 8, 1), shift(both, "z", 8, -1)
-    up4, down4 = shift(up2[:half], "z", 8, 2), shift(down2[half:], "z", 8, -2)
+    first = core == 0
+
+    def across(value, by):
+        pairs = [
+            ((a * 8 + i) * 2 + c, ((a ^ c) * 8 + (i + by) % 8) * 2 + c)
+            for a in range(2)
+            for i in range(8)
+            for c in range(2)
+            if by or c
+        ]
+        return lax.ppermute(value, ("x", "z", "core"), pairs)
+
+    def halves(value):
+        return jnp.where(first, value[:, :HD], value[:, HD:]), jnp.where(first, value[:, HD:], value[:, :HD])
+
+    near = lax.dynamic_slice_in_dim(keyval, (xh * 4 + y) * 2 * HD, 2 * HD, 1)
+    up2, down2 = across(near, 2), across(near, -2)
+    up1, down1 = across(near, 1), across(near, -1)
+    own = jnp.where(first, near, across(near, 0))
     up3, down3 = shift(up2, "z", 8, 1), shift(down2, "z", 8, -1)
-    mine = jnp.concatenate([both, down1, down2, down3, up4, down4, up3, up2, up1], axis=0)
-    other = swap(mine, "core")
-    keys, values = jnp.where(core == 0, mine, other), jnp.where(core == 0, other, mine)
-    attn_out, grad_query, mine, other = attention(
-        vis_blocks, vis_count, block_order, query, grad_out, segment_ids.reshape(NB, BLK), keys, values
+    up4, down4 = shift(up2[:BLK], "z", 8, 2), shift(down2[BLK:], "z", 8, -2)
+    reached = jnp.concatenate([own, down1, down2, up2, up1], axis=0)
+    relayed = jnp.concatenate([down3, up4, down4, up3], axis=0)
+    sides = [(mine, swap(mine, "core")) for mine in (reached, relayed)]
+    gathered = [jnp.where(first, mine, other) for mine, other in sides]
+    gathered = jnp.concatenate(gathered + [jnp.where(first, other, mine) for mine, other in sides], axis=0)
+    attn_out, grad_query, other_relayed, mine_relayed, other, mine = attention(
+        vis_blocks, vis_count, block_order, query, grad_out, segment_ids.reshape(NB, BLK), gathered
     )
-    joined = wide(mine, swap(other, "core")).astype(BF)
-    for4_up, for4_down = shift(joined[4, :half], "z", 8, 2), shift(joined[4, half:], "z", 8, -2)
+    relayed = wide(mine_relayed, swap(other_relayed, "core")).astype(BF)
+    reached = wide(mine, swap(other, "core")).astype(BF)
+    joined = dict(zip(RELAYED + REACHED, [relayed[k] for k in range(3)] + [reached[k] for k in range(5)]))
+    for4_up, for4_down = shift(joined[4][:BLK], "z", 8, 2), shift(joined[4][BLK:], "z", 8, -2)
     for3_up, for3_down = shift(joined[3], "z", 8, 1), shift(joined[5], "z", 8, -1)
     up2 = jnp.concatenate(
-        [wide(joined[2, :half], for3_up[:half], for4_up), wide(joined[2, half:], for3_up[half:])], axis=0
+        [wide(joined[2][:BLK], for3_up[:BLK], for4_up), wide(joined[2][BLK:], for3_up[BLK:])], axis=0
     )
     down2 = jnp.concatenate(
-        [wide(joined[6, :half], for3_down[:half]), wide(joined[6, half:], for3_down[half:], for4_down)], axis=0
+        [wide(joined[6][:BLK], for3_down[:BLK]), wide(joined[6][BLK:], for3_down[BLK:], for4_down)], axis=0
     )
-    for2_up, for2_down = shift(up2.astype(BF), "z", 8, 2), shift(down2.astype(BF), "z", 8, -2)
-    near_up, near_down, _ = lax.optimization_barrier((joined[1], joined[7], for3_down))
-    for1_up, for1_down = shift(near_up, "z", 8, 1), shift(near_down, "z", 8, -1)
-    summed = wide(joined[0], for1_up, for1_down, for2_up, for2_down)
-    got = swap(summed[half:].astype(BF), "x")
-    summed = wide(summed[:half], got).astype(BF)
+    for2_up, for2_down = across(up2.astype(BF), 2), across(down2.astype(BF), -2)
+    for1_up, for1_down = across(joined[1], 1), across(joined[7], -1)
+    own = jnp.where(first, joined[0], across(joined[0], 0))
+    kept, given = halves(wide(own, for1_up, for1_down, for2_up, for2_down))
+    summed = wide(kept, swap(given.astype(BF), "core")).astype(BF)
     mine = lax.all_to_all(jnp.concatenate([summed] * KVH, axis=0), ("y", "xh"), 0, 0, tiled=True)
     return attn_out, grad_query, assemble(mine, swap(mine, "core"))
 

time: 100 us -> 97.3 us (0.973)
  waiting for transfers between devices: 28.8 us -> 18.3 us
  Pallas kernels: 13.1 us -> 16.2 us
  blocking collectives: 15.5 us -> 17 us
  other arithmetic: 0.64 us -> 1.76 us
    ppermute x0 -> x10, starting transfers between devices: none -> 22.8 us  [across(): return lax.ppermute(value, ('x', 'z', 'core'), pairs)]
    ppermute x16 -> x8, starting transfers between devices: 28.6 us -> 13 us  [shift(): lax.ppermute(value, axis, [(i, (i + by) % size) for i in range(size)])]
    ppermute x16 -> x8, waiting for transfers between devices: 18.1 us -> 6.01 us  [shift(): lax.ppermute(value, axis, [(i, (i + by) % size) for i in range(size)])]
    ppermute x5 -> x6, starting transfers between devices: 12.4 us -> 5.7 us  [swap(): return lax.ppermute(value, axis, [(0, 1), (1, 0)])]
    ppermute x0 -> x10, waiting for transfers between devices: none -> 6.6 us  [across(): return lax.ppermute(value, ('x', 'z', 'core'), pairs)]
    ppermute x5 -> x6, waiting for transfers between devices: 10.7 us -> 5.68 us  [swap(): return lax.ppermute(value, axis, [(0, 1), (1, 0)])]
    pallas_call x1, Pallas kernels: 11.5 us -> 14.6 us  [attention(): pl.pallas_call(attention_kernel, in_specs=[hbm] * 6 + [vmem], out_specs=[...]
    all_to_all x1, blocking collectives: 15.5 us -> 17 us  [shards(): lax.all_to_all(jnp.concatenate([summed] * KVH, axis=0), ('y', 'xh'), 0, 0...]
  transfers between devices with their start and end apart: 21 -> 24, of which waited for: 12 -> 14; matrix products, arithmetic and copies ran while one was open for 0% -> 2% of each run, Pallas kernels for 0% -> 0%
where the time goes in v1:
time: 97.3 us; the launch traced here: 97.7 us
  starting transfers between devices  41.5 us (43%)
  waiting for transfers between devices  18.3 us (19%)
  blocking collectives  17 us (17%)
  Pallas kernels  16.2 us (17%)
  local copies, waits for them, and re-layouts  2.09 us (2%)
  other arithmetic  1.76 us (2%)
    ppermute x10, starting transfers between devices, across(): return lax.ppermute(value, ('x', 'z', 'core'), pairs)  22.8 us
    all_to_all x1, blocking collectives, shards(): lax.all_to_all(jnp.concatenate([summed] * KVH, axis=0), ('y', 'xh'), 0, 0...  17 us
    pallas_call x1, Pallas kernels, attention(): pl.pallas_call(attention_kernel, in_specs=[hbm] * 6 + [vmem], out_specs=[...  14.6 us
    ppermute x8, starting transfers between devices, shift(): lax.ppermute(value, axis, [(i, (i + by) % size) for i in range(size)])  13 us
    ppermute x10, waiting for transfers between devices, across(): return lax.ppermute(value, ('x', 'z', 'core'), pairs)  6.6 us
    ppermute x8, waiting for transfers between devices, shift(): lax.ppermute(value, axis, [(i, (i + by) % size) for i in range(size)])  6.01 us
    ppermute x6, starting transfers between devices, swap(): return lax.ppermute(value, axis, [(0, 1), (1, 0)])  5.7 us
    ppermute x6, waiting for transfers between devices, swap(): return lax.ppermute(value, axis, [(0, 1), (1, 0)])  5.68 us
  transfers between devices with their start and end apart: 24, of which 14 were waited for; matrix products, arithmetic and copies ran while one was open for 2% of the time, Pallas kernels for 0%

profile of v1, /device:TPU:1, one launch (start us, length us, event | category | flops | bytes accessed | tf_op | source)
XLA Modules:
  0.0 97.7 jit_solution(3715982313100354121)
XLA Ops:
  0.6 0.9 constant_dynamic-slice_fusion
  1.6 4.8 %collective-permute-start.3 = (bf16[256,256]{1,0:T(8,128)(2,1)S(1)}, bf16[256,256]{1,0:T(8,128)(2,1)S(1)}, u32[]{:S(2)}, u32[]{:S(2)}) collective-permute-start(bf16[256,256]{1,0:T(8,128)(2,1)S(1)} %constant_dynamic-slice_fusion), channel_id=1, source_target_pairs={{0,32},{1,161},{16,48},{17,177},{32,64},{33,193},{48,80},{49,209},... | collective-permute-start | bytes 393224 | tf_op jit(solution)/shard_map/ppermute | solution.py:297
  6.4 3.1 %collective-permute-start.2 = (bf16[256,256]{1,0:T(8,128)(2,1)S(1)}, bf16[256,256]{1,0:T(8,128)(2,1)S(1)}, u32[]{:S(2)}, u32[]{:S(2)}) collective-permute-start(bf16[256,256]{1,0:T(8,128)(2,1)S(1)} %constant_dynamic-slice_fusion), channel_id=1, source_target_pairs={{0,96},{1,225},{16,112},{17,241},{32,0},{33,129},{48,16},{49,145},... | collective-permute-start | bytes 393224 | tf_op jit(solution)/shard_map/ppermute | solution.py:297
  9.5 2.2 %collective-permute-start = (bf16[256,256]{1,0:T(8,128)(2,1)S(1)}, bf16[256,256]{1,0:T(8,128)(2,1)S(1)}, u32[]{:S(2)}, u32[]{:S(2)}) collective-permute-start(bf16[256,256]{1,0:T(8,128)(2,1)S(1)} %constant_dynamic-slice_fusion), channel_id=1, source_target_pairs={{1,129},{17,145},{33,161},{49,177},{65,193},{81,209},{97,225},{113... | collective-permute-start | bytes 393224 | tf_op jit(solution)/shard_map/ppermute | solution.py:297
  11.7 2.8 %collective-permute-start.1 = (bf16[256,256]{1,0:T(8,128)(2,1)S(1)}, bf16[256,256]{1,0:T(8,128)(2,1)S(1)}, u32[]{:S(2)}, u32[]{:S(2)}) collective-permute-start(bf16[256,256]{1,0:T(8,128)(2,1)S(1)} %constant_dynamic-slice_fusion), channel_id=1, source_target_pairs={{0,112},{1,241},{16,0},{17,129},{32,16},{33,145},{48,32},{49,161},... | collective-permute-start | bytes 393224 | tf_op jit(solution)/shard_map/ppermute | solution.py:297
  14.5 1.5 %collective-permute-start.7 = (bf16[128,256]{1,0:T(8,128)(2,1)S(1)}, bf16[128,256]{1,0:T(8,128)(2,1)S(1)}, u32[]{:S(2)}, u32[]{:S(2)}) collective-permute-start(bf16[128,256]{1,0:T(8,128)(2,1)S(1)} %slice.99), channel_id=1, source_target_pairs={{0,32},{16,48},{32,64},{48,80},{64,96},{80,112},{96,0},{112,16},{1... | collective-permute-start | bytes 196616 | tf_op jit(solution)/shard_map/ppermute | solution.py:28
  16.7 2.3 %collective-permute-start.8 = (bf16[128,256]{1,0:T(8,128)(2,1)S(1)}, bf16[128,256]{1,0:T(8,128)(2,1)S(1)}, u32[]{:S(2)}, u32[]{:S(2)}) collective-permute-start(bf16[128,256]{1,0:T(8,128)(2,1)S(1)} %slice.100), channel_id=1, source_target_pairs={{0,96},{16,112},{32,0},{48,16},{64,32},{80,48},{96,64},{112,80},{1... | collective-permute-start | bytes 196616 | tf_op jit(solution)/shard_map/ppermute | solution.py:28
  19.0 0.9 collective-permute-start.9
  19.9 0.9 select_dynamic-update-slice_fusion
  20.8 1.9 %collective-permute-start.6 = (bf16[256,256]{1,0:T(8,128)(2,1)S(1)}, bf16[256,256]{1,0:T(8,128)(2,1)S(1)}, u32[]{:S(2)}, u32[]{:S(2)}) collective-permute-start(bf16[256,256]{1,0:T(8,128)(2,1)S(1)} %collective-permute-done.2), channel_id=1, source_target_pairs={{0,112},{16,0},{32,16},{48,32},{64,48},{80,64},{96,80},{112,96},{1... | collective-permute-start | bytes 393224 | tf_op jit(solution)/shard_map/ppermute | solution.py:28
  22.8 3.4 %collective-permute-done.6 = bf16[256,256]{1,0:T(8,128)(2,1)S(1)} collective-permute-done((bf16[256,256]{1,0:T(8,128)(2,1)S(1)}, bf16[256,256]{1,0:T(8,128)(2,1)S(1)}, u32[]{:S(2)}, u32[]{:S(2)}) %collective-permute-start.6) | collective-permute-done | bytes 131104 | tf_op jit(solution)/shard_map/ppermute | solution.py:28
  26.2 1.6 %collective-permute-start.10 = (bf16[768,256]{1,0:T(8,128)(2,1)S(1)}, bf16[768,256]{1,0:T(8,128)(2,1)S(1)}, u32[]{:S(2)}, u32[]{:S(2)}) collective-permute-start(bf16[768,256]{1,0:T(8,128)(2,1)S(1)} %constant_dynamic-update-slice_fusion.4), channel_id=1, source_target_pairs={{0,1},{1,0},{2,3},{3,2},{4,5},{5,4},{6,7},{7,6},{8,9},{9,8},{10,11... | collective-permute-start | bytes 1179656 | tf_op jit(solution)/shard_map/ppermute | solution.py:32
  28.0 1.1 %collective-permute-done.10 = bf16[768,256]{1,0:T(8,128)(2,1)S(1)} collective-permute-done((bf16[768,256]{1,0:T(8,128)(2,1)S(1)}, bf16[768,256]{1,0:T(8,128)(2,1)S(1)}, u32[]{:S(2)}, u32[]{:S(2)}) %collective-permute-start.10) | collective-permute-done | bytes 393248 | tf_op jit(solution)/shard_map/ppermute | solution.py:32
  29.2 0.9 collective-permute-done.5
  31.2 14.6 %attention.1 = (bf16[256,512]{1,0:T(8,128)(2,1)}, bf16[256,512]{1,0:T(8,128)(2,1)}, bf16[3,256,256]{2,1,0:T(8,128)(2,1)S(1)}, bf16[3,256,256]{2,1,0:T(8,128)(2,1...) custom-call(s32[32,24]{1,0:T(8,128)S(1)} %copy.10.vis_any, s32[32]{0:T(128)S(1)} %copy-done.3, ...), custom_call_target="tpu_custom_call" | custom-call | tf_op jit(solution)/shard_map/attention/pallas_call | solution.py:227
  46.6 1.2 %collective-permute-done.15 = bf16[3,256,256]{2,1,0:T(8,128)(2,1)S(1)} collective-permute-done((bf16[3,256,256]{2,1,0:T(8,128)(2,1)S(1)}, bf16[3,256,256]{2,1,0:T(8,128)(2,1)S(1)}, u32[]{:S(2)}, u32[]{:S(2)}) %collective-permute-start.15) | collective-permute-done | bytes 393248 | tf_op jit(solution)/shard_map/ppermute | solution.py:32
  48.8 2.8 %collective-permute-start.20 = (bf16[128,256]{1,0:T(8,128)(2,1)S(1)}, bf16[128,256]{1,0:T(8,128)(2,1)S(1)}, u32[]{:S(2)}, u32[]{:S(2)}) collective-permute-start(bf16[128,256]{1,0:T(8,128)(2,1)S(1)} %get-tuple-element.31), channel_id=1, source_target_pairs={{0,96},{16,112},{32,0},{48,16},{64,32},{80,48},{96,64},{112,80},{1... | collective-permute-start | bytes 196616 | tf_op jit(solution)/shard_map/ppermute | solution.py:28
  51.7 2.7 %collective-permute-start.19 = (bf16[256,256]{1,0:T(8,128)(2,1)S(1)}, bf16[256,256]{1,0:T(8,128)(2,1)S(1)}, u32[]{:S(2)}, u32[]{:S(2)}) collective-permute-start(bf16[256,256]{1,0:T(8,128)(2,1)S(1)} %get-tuple-element.33), channel_id=1, source_target_pairs={{0,112},{16,0},{32,16},{48,32},{64,48},{80,64},{96,80},{112,96},{1... | collective-permute-start | bytes 393224 | tf_op jit(solution)/shard_map/ppermute | solution.py:28
  55.4 1.3 %collective-permute-done.16 = bf16[256,256]{1,0:T(8,128)(2,1)S(1)} collective-permute-done((bf16[256,256]{1,0:T(8,128)(2,1)S(1)}, bf16[256,256]{1,0:T(8,128)(2,1)S(1)}, u32[]{:S(2)}, u32[]{:S(2)}) %collective-permute-start.16) | collective-permute-done | bytes 131104 | tf_op jit(solution)/shard_map/ppermute | solution.py:28
  57.3 2.1 %collective-permute-start.21 = (bf16[256,256]{1,0:T(8,128)(2,1)S(1)}, bf16[256,256]{1,0:T(8,128)(2,1)S(1)}, u32[]{:S(2)}, u32[]{:S(2)}) collective-permute-start(bf16[256,256]{1,0:T(8,128)(2,1)S(1)} %pad_maximum_fusion.2), channel_id=1, source_target_pairs={{0,96},{1,225},{16,112},{17,241},{32,0},{33,129},{48,16},{49,145},... | collective-permute-start | bytes 393224 | tf_op jit(solution)/shard_map/ppermute | solution.py:297
  59.4 1.3 %collective-permute-start.18 = (bf16[256,256]{1,0:T(8,128)(2,1)S(1)}, bf16[256,256]{1,0:T(8,128)(2,1)S(1)}, u32[]{:S(2)}, u32[]{:S(2)}) collective-permute-start(bf16[256,256]{1,0:T(8,128)(2,1)S(1)} %pad_maximum_fusion.1), channel_id=1, source_target_pairs={{0,32},{1,161},{16,48},{17,177},{32,64},{33,193},{48,80},{49,209},... | collective-permute-start | bytes 393224 | tf_op jit(solution)/shard_map/ppermute | solution.py:297
  60.8 2.7 %collective-permute-start.12 = (bf16[256,256]{1,0:T(8,128)(2,1)S(1)}, bf16[256,256]{1,0:T(8,128)(2,1)S(1)}, u32[]{:S(2)}, u32[]{:S(2)}) collective-permute-start(bf16[256,256]{1,0:T(8,128)(2,1)S(1)} %get-tuple-element.25), channel_id=1, source_target_pairs={{1,129},{17,145},{33,161},{49,177},{65,193},{81,209},{97,225},{113... | collective-permute-start | bytes 393224 | tf_op jit(solution)/shard_map/ppermute | solution.py:297
  63.4 3.9 %collective-permute-start.14 = (bf16[256,256]{1,0:T(8,128)(2,1)S(1)}, bf16[256,256]{1,0:T(8,128)(2,1)S(1)}, u32[]{:S(2)}, u32[]{:S(2)}) collective-permute-start(bf16[256,256]{1,0:T(8,128)(2,1)S(1)} %get-tuple-element.26), channel_id=1, source_target_pairs={{0,112},{1,241},{16,0},{17,129},{32,16},{33,145},{48,32},{49,161},... | collective-permute-start | bytes 393224 | tf_op jit(solution)/shard_map/ppermute | solution.py:297
  67.3 1.8 %collective-permute-done.18 = bf16[256,256]{1,0:T(8,128)(2,1)S(1)} collective-permute-done((bf16[256,256]{1,0:T(8,128)(2,1)S(1)}, bf16[256,256]{1,0:T(8,128)(2,1)S(1)}, u32[]{:S(2)}, u32[]{:S(2)}) %collective-permute-start.18) | collective-permute-done | bytes 131104 | tf_op jit(solution)/shard_map/ppermute | solution.py:297
  69.1 1.3 %collective-permute-done.12 = bf16[256,256]{1,0:T(8,128)(2,1)S(1)} collective-permute-done((bf16[256,256]{1,0:T(8,128)(2,1)S(1)}, bf16[256,256]{1,0:T(8,128)(2,1)S(1)}, u32[]{:S(2)}, u32[]{:S(2)}) %collective-permute-start.12) | collective-permute-done | bytes 131104 | tf_op jit(solution)/shard_map/ppermute | solution.py:297
  70.7 2.5 %collective-permute-done.13 = bf16[256,256]{1,0:T(8,128)(2,1)S(1)} collective-permute-done((bf16[256,256]{1,0:T(8,128)(2,1)S(1)}, bf16[256,256]{1,0:T(8,128)(2,1)S(1)}, u32[]{:S(2)}, u32[]{:S(2)}) %collective-permute-start.13) | collective-permute-done | bytes 131104 | tf_op jit(solution)/shard_map/ppermute | solution.py:297
  73.4 1.4 %collective-permute-start.22 = (bf16[256,128]{1,0:T(8,128)(2,1)S(1)}, bf16[256,128]{1,0:T(8,128)(2,1)S(1)}, u32[]{:S(2)}, u32[]{:S(2)}) collective-permute-start(bf16[256,128]{1,0:T(8,128)(2,1)S(1)} %select_convert_fusion), channel_id=1, source_target_pairs={{0,1},{1,0},{2,3},{3,2},{4,5},{5,4},{6,7},{7,6},{8,9},{9,8},{10,11... | collective-permute-start | bytes 196616 | tf_op jit(solution)/shard_map/ppermute | solution.py:32
  74.8 0.9 collective-permute-done.22
  75.8 17.0 %all_to_all.11 = bf16[8,256,128]{2,1,0:T(8,128)(2,1)S(1)} all-to-all(bf16[8,256,128]{2,1,0:T(8,128)(2,1)S(1)} %bitcast.42), channel_id=1, replica_groups=mesh['x'=2,'z'=8,'xh'=2,'y'=4,'core'=2] {'y','xh'}, dimensions={0} | all-to-all | bytes 1048576 | tf_op jit(solution)/shard_map/all_to_all | solution.py:332
  92.8 1.8 %collective-permute-start.23 = (bf16[2048,128]{1,0:T(8,128)(2,1)S(1)}, bf16[2048,128]{1,0:T(8,128)(2,1)S(1)}, u32[]{:S(2)}, u32[]{:S(2)}) collective-permute-start(bf16[2048,128]{1,0:T(8,128)(2,1)S(1)} %bitcast.39), channel_id=1, source_target_pairs={{0,1},{1,0},{2,3},{3,2},{4,5},{5,4},{6,7},{7,6},{8,9},{9,8},{10,11... | collective-permute-start | bytes 1572872 | tf_op jit(solution)/shard_map/ppermute | solution.py:32
  94.6 1.5 %collective-permute-done.23.other_ref = bf16[2048,128]{1,0:T(8,128)(2,1)S(1)} collective-permute-done((bf16[2048,128]{1,0:T(8,128)(2,1)S(1)}, bf16[2048,128]{1,0:T(8,128)(2,1)S(1)}, u32[]{:S(2)}, u32[]{:S(2)}) %collective-permute-start.23) | collective-permute-done | bytes 524320 | tf_op jit(solution)/shard_map/ppermute | solution.py:32
  96.1 1.6 %assemble.1 = f32[256,2048]{1,0:T(8,128)} custom-call(bf16[2048,128]{1,0:T(8,128)(2,1)S(1)} %bitcast.40, bf16[2048,128]{1,0:T(8,128)(2,1)S(1)} %collective-permute-done.23.other_ref), custom_call_target="tpu_custom_call" | custom-call | tf_op jit(solution)/shard_map/assemble/pallas_call | solution.py:271
  (65 shorter events, 6.1 us)
Async XLA Ops:
  0.6 27.3 %copy-start.5 = (s32[32,24]{0,1:T(8,128)S(1)}, s32[32,24]{0,1:T(8,128)}, u32[]{:S(2)}) copy-start(s32[32,24]{0,1:T(8,128)} %param.10) | copy-start | bytes 9220
  1.6 12.9 %collective-permute-start.3 = (bf16[256,256]{1,0:T(8,128)(2,1)S(1)}, bf16[256,256]{1,0:T(8,128)(2,1)S(1)}, u32[]{:S(2)}, u32[]{:S(2)}) collective-permute-start(bf16[256,256]{1,0:T(8,128)(2,1)S(1)} %constant_dynamic-slice_fusion), channel_id=1, source_target_pairs={{0,32},{1,161},{16,48},{17,177},{32,64},{33,193},{48,80},{49,209},... | collective-permute-start | bytes 393224 | tf_op jit(solution)/shard_map/ppermute | solution.py:297
  6.4 10.3 %collective-permute-start.2 = (bf16[256,256]{1,0:T(8,128)(2,1)S(1)}, bf16[256,256]{1,0:T(8,128)(2,1)S(1)}, u32[]{:S(2)}, u32[]{:S(2)}) collective-permute-start(bf16[256,256]{1,0:T(8,128)(2,1)S(1)} %constant_dynamic-slice_fusion), channel_id=1, source_target_pairs={{0,96},{1,225},{16,112},{17,241},{32,0},{33,129},{48,16},{49,145},... | collective-permute-start | bytes 393224 | tf_op jit(solution)/shard_map/ppermute | solution.py:297
  9.5 9.5 %collective-permute-start = (bf16[256,256]{1,0:T(8,128)(2,1)S(1)}, bf16[256,256]{1,0:T(8,128)(2,1)S(1)}, u32[]{:S(2)}, u32[]{:S(2)}) collective-permute-start(bf16[256,256]{1,0:T(8,128)(2,1)S(1)} %constant_dynamic-slice_fusion), channel_id=1, source_target_pairs={{1,129},{17,145},{33,161},{49,177},{65,193},{81,209},{97,225},{113... | collective-permute-start | bytes 393224 | tf_op jit(solution)/shard_map/ppermute | solution.py:297
  11.7 9.2 %collective-permute-start.1 = (bf16[256,256]{1,0:T(8,128)(2,1)S(1)}, bf16[256,256]{1,0:T(8,128)(2,1)S(1)}, u32[]{:S(2)}, u32[]{:S(2)}) collective-permute-start(bf16[256,256]{1,0:T(8,128)(2,1)S(1)} %constant_dynamic-slice_fusion), channel_id=1, source_target_pairs={{0,112},{1,241},{16,0},{17,129},{32,16},{33,145},{48,32},{49,161},... | collective-permute-start | bytes 393224 | tf_op jit(solution)/shard_map/ppermute | solution.py:297
  14.5 13.3 %collective-permute-start.4 = (bf16[256,256]{1,0:T(8,128)(2,1)S(1)}, bf16[256,256]{1,0:T(8,128)(2,1)S(1)}, u32[]{:S(2)}, u32[]{:S(2)}) collective-permute-start(bf16[256,256]{1,0:T(8,128)(2,1)S(1)} %constant_dynamic-slice_fusion), channel_id=1, source_target_pairs={{0,16},{1,145},{16,32},{17,161},{32,48},{33,177},{48,64},{49,193},... | collective-permute-start | bytes 393224 | tf_op jit(solution)/shard_map/ppermute | solution.py:297
  14.5 11.6 %collective-permute-start.7 = (bf16[128,256]{1,0:T(8,128)(2,1)S(1)}, bf16[128,256]{1,0:T(8,128)(2,1)S(1)}, u32[]{:S(2)}, u32[]{:S(2)}) collective-permute-start(bf16[128,256]{1,0:T(8,128)(2,1)S(1)} %slice.99), channel_id=1, source_target_pairs={{0,32},{16,48},{32,64},{48,80},{64,96},{80,112},{96,0},{112,16},{1... | collective-permute-start | bytes 196616 | tf_op jit(solution)/shard_map/ppermute | solution.py:28
  16.7 9.5 %collective-permute-start.8 = (bf16[128,256]{1,0:T(8,128)(2,1)S(1)}, bf16[128,256]{1,0:T(8,128)(2,1)S(1)}, u32[]{:S(2)}, u32[]{:S(2)}) collective-permute-start(bf16[128,256]{1,0:T(8,128)(2,1)S(1)} %slice.100), channel_id=1, source_target_pairs={{0,96},{16,112},{32,0},{48,16},{64,32},{80,48},{96,64},{112,80},{1... | collective-permute-start | bytes 196616 | tf_op jit(solution)/shard_map/ppermute | solution.py:28
  19.0 7.2 %collective-permute-start.9 = (bf16[256,256]{1,0:T(8,128)(2,1)S(1)}, bf16[256,256]{1,0:T(8,128)(2,1)S(1)}, u32[]{:S(2)}, u32[]{:S(2)}) collective-permute-start(bf16[256,256]{1,0:T(8,128)(2,1)S(1)} %collective-permute-done.3), channel_id=1, source_target_pairs={{0,16},{16,32},{32,48},{48,64},{64,80},{80,96},{96,112},{112,0},{1... | collective-permute-start | bytes 393224 | tf_op jit(solution)/shard_map/ppermute | solution.py:28
  20.8 5.3 %collective-permute-start.6 = (bf16[256,256]{1,0:T(8,128)(2,1)S(1)}, bf16[256,256]{1,0:T(8,128)(2,1)S(1)}, u32[]{:S(2)}, u32[]{:S(2)}) collective-permute-start(bf16[256,256]{1,0:T(8,128)(2,1)S(1)} %collective-permute-done.2), channel_id=1, source_target_pairs={{0,112},{16,0},{32,16},{48,32},{64,48},{80,64},{96,80},{112,96},{1... | collective-permute-start | bytes 393224 | tf_op jit(solution)/shard_map/ppermute | solution.py:28
  26.2 3.0 %collective-permute-start.10 = (bf16[768,256]{1,0:T(8,128)(2,1)S(1)}, bf16[768,256]{1,0:T(8,128)(2,1)S(1)}, u32[]{:S(2)}, u32[]{:S(2)}) collective-permute-start(bf16[768,256]{1,0:T(8,128)(2,1)S(1)} %constant_dynamic-update-slice_fusion.4), channel_id=1, source_target_pairs={{0,1},{1,0},{2,3},{3,2},{4,5},{5,4},{6,7},{7,6},{8,9},{9,8},{10,11... | collective-permute-start | bytes 1179656 | tf_op jit(solution)/shard_map/ppermute | solution.py:32
  27.8 2.3 %collective-permute-start.5 = (bf16[1280,256]{1,0:T(8,128)(2,1)S(1)}, bf16[1280,256]{1,0:T(8,128)(2,1)S(1)}, u32[]{:S(2)}, u32[]{:S(2)}) collective-permute-start(bf16[1280,256]{1,0:T(8,128)(2,1)S(1)} %constant_dynamic-update-slice_fusion), channel_id=1, source_target_pairs={{0,1},{1,0},{2,3},{3,2},{4,5},{5,4},{6,7},{7,6},{8,9},{9,8},{10,11... | collective-permute-start | bytes 1966088 | tf_op jit(solution)/shard_map/ppermute | solution.py:32
  30.2 1.0 copy-start
  30.2 1.0 %copy-start.1 = (bf16[256,512]{1,0:T(8,128)(2,1)S(1)}, bf16[256,512]{1,0:T(8,128)(2,1)}, u32[]{:S(2)}) copy-start(bf16[256,512]{1,0:T(8,128)(2,1)} %g_any.1) | copy-start | bytes 786436
  30.2 1.0 %copy-start.2 = (s32[4096]{0:T(1024)S(1)}, s32[4096]{0:T(1024)}, u32[]{:S(2)}) copy-start(s32[4096]{0:T(1024)} %param.12) | copy-start | bytes 49156
  30.2 1.0 %copy-start.3 = (s32[32]{0:T(128)S(1)}, s32[32]{0:T(128)}, u32[]{:S(2)}) copy-start(s32[32]{0:T(128)} %count_any.1) | copy-start | bytes 388
  30.2 1.0 %copy-start.4 = (s32[32]{0:T(128)S(1)}, s32[32]{0:T(128)}, u32[]{:S(2)}) copy-start(s32[32]{0:T(128)} %order_any.1) | copy-start | bytes 388
  45.8 2.0 %collective-permute-start.15 = (bf16[3,256,256]{2,1,0:T(8,128)(2,1)S(1)}, bf16[3,256,256]{2,1,0:T(8,128)(2,1)S(1)}, u32[]{:S(2)}, u32[]{:S(2)}) collective-permute-start(bf16[3,256,256]{2,1,0:T(8,128)(2,1)S(1)} %get-tuple-element.14), channel_id=1, source_target_pairs={{0,1},{1,0},{2,3},{3,2},{4,5},{5,4},{6,7},{7,6},{8,9},{9,8},{10,11... | collective-permute-start | bytes 1179656 | tf_op jit(solution)/shard_map/ppermute | solution.py:32
  46.4 7.9 %collective-permute-start.11 = (bf16[5,256,256]{2,1,0:T(8,128)(2,1)S(1)}, bf16[5,256,256]{2,1,0:T(8,128)(2,1)S(1)}, u32[]{:S(2)}, u32[]{:S(2)}) collective-permute-start(bf16[5,256,256]{2,1,0:T(8,128)(2,1)S(1)} %get-tuple-element.12), channel_id=1, source_target_pairs={{0,1},{1,0},{2,3},{3,2},{4,5},{5,4},{6,7},{7,6},{8,9},{9,8},{10,11... | collective-permute-start | bytes 1966088 | tf_op jit(solution)/shard_map/ppermute | solution.py:32
  47.9 7.5 %collective-permute-start.17 = (bf16[128,256]{1,0:T(8,128)(2,1)S(1)}, bf16[128,256]{1,0:T(8,128)(2,1)S(1)}, u32[]{:S(2)}, u32[]{:S(2)}) collective-permute-start(bf16[128,256]{1,0:T(8,128)(2,1)S(1)} %get-tuple-element.30), channel_id=1, source_target_pairs={{0,32},{16,48},{32,64},{48,80},{64,96},{80,112},{96,0},{112,16},{1... | collective-permute-start | bytes 196616 | tf_op jit(solution)/shard_map/ppermute | solution.py:28
  48.8 6.7 %collective-permute-start.20 = (bf16[128,256]{1,0:T(8,128)(2,1)S(1)}, bf16[128,256]{1,0:T(8,128)(2,1)S(1)}, u32[]{:S(2)}, u32[]{:S(2)}) collective-permute-start(bf16[128,256]{1,0:T(8,128)(2,1)S(1)} %get-tuple-element.31), channel_id=1, source_target_pairs={{0,96},{16,112},{32,0},{48,16},{64,32},{80,48},{96,64},{112,80},{1... | collective-permute-start | bytes 196616 | tf_op jit(solution)/shard_map/ppermute | solution.py:28
  51.6 5.1 %collective-permute-start.16 = (bf16[256,256]{1,0:T(8,128)(2,1)S(1)}, bf16[256,256]{1,0:T(8,128)(2,1)S(1)}, u32[]{:S(2)}, u32[]{:S(2)}) collective-permute-start(bf16[256,256]{1,0:T(8,128)(2,1)S(1)} %get-tuple-element.32), channel_id=1, source_target_pairs={{0,16},{16,32},{32,48},{48,64},{64,80},{80,96},{96,112},{112,0},{1... | collective-permute-start | bytes 393224 | tf_op jit(solution)/shard_map/ppermute | solution.py:28
  51.7 5.5 %collective-permute-start.19 = (bf16[256,256]{1,0:T(8,128)(2,1)S(1)}, bf16[256,256]{1,0:T(8,128)(2,1)S(1)}, u32[]{:S(2)}, u32[]{:S(2)}) collective-permute-start(bf16[256,256]{1,0:T(8,128)(2,1)S(1)} %get-tuple-element.33), channel_id=1, source_target_pairs={{0,112},{16,0},{32,16},{48,32},{64,48},{80,64},{96,80},{112,96},{1... | collective-permute-start | bytes 393224 | tf_op jit(solution)/shard_map/ppermute | solution.py:28
  57.3 10.0 %collective-permute-start.21 = (bf16[256,256]{1,0:T(8,128)(2,1)S(1)}, bf16[256,256]{1,0:T(8,128)(2,1)S(1)}, u32[]{:S(2)}, u32[]{:S(2)}) collective-permute-start(bf16[256,256]{1,0:T(8,128)(2,1)S(1)} %pad_maximum_fusion.2), channel_id=1, source_target_pairs={{0,96},{1,225},{16,112},{17,241},{32,0},{33,129},{48,16},{49,145},... | collective-permute-start | bytes 393224 | tf_op jit(solution)/shard_map/ppermute | solution.py:297
  59.4 9.6 %collective-permute-start.18 = (bf16[256,256]{1,0:T(8,128)(2,1)S(1)}, bf16[256,256]{1,0:T(8,128)(2,1)S(1)}, u32[]{:S(2)}, u32[]{:S(2)}) collective-permute-start(bf16[256,256]{1,0:T(8,128)(2,1)S(1)} %pad_maximum_fusion.1), channel_id=1, source_target_pairs={{0,32},{1,161},{16,48},{17,177},{32,64},{33,193},{48,80},{49,209},... | collective-permute-start | bytes 393224 | tf_op jit(solution)/shard_map/ppermute | solution.py:297
  60.8 9.6 %collective-permute-start.12 = (bf16[256,256]{1,0:T(8,128)(2,1)S(1)}, bf16[256,256]{1,0:T(8,128)(2,1)S(1)}, u32[]{:S(2)}, u32[]{:S(2)}) collective-permute-start(bf16[256,256]{1,0:T(8,128)(2,1)S(1)} %get-tuple-element.25), channel_id=1, source_target_pairs={{1,129},{17,145},{33,161},{49,177},{65,193},{81,209},{97,225},{113... | collective-permute-start | bytes 393224 | tf_op jit(solution)/shard_map/ppermute | solution.py:297
  63.4 7.2 %collective-permute-start.14 = (bf16[256,256]{1,0:T(8,128)(2,1)S(1)}, bf16[256,256]{1,0:T(8,128)(2,1)S(1)}, u32[]{:S(2)}, u32[]{:S(2)}) collective-permute-start(bf16[256,256]{1,0:T(8,128)(2,1)S(1)} %get-tuple-element.26), channel_id=1, source_target_pairs={{0,112},{1,241},{16,0},{17,129},{32,16},{33,145},{48,32},{49,161},... | collective-permute-start | bytes 393224 | tf_op jit(solution)/shard_map/ppermute | solution.py:297
  67.3 5.9 %collective-permute-start.13 = (bf16[256,256]{1,0:T(8,128)(2,1)S(1)}, bf16[256,256]{1,0:T(8,128)(2,1)S(1)}, u32[]{:S(2)}, u32[]{:S(2)}) collective-permute-start(bf16[256,256]{1,0:T(8,128)(2,1)S(1)} %get-tuple-element.27), channel_id=1, source_target_pairs={{0,16},{1,145},{16,32},{17,161},{32,48},{33,177},{48,64},{49,193},... | collective-permute-start | bytes 393224 | tf_op jit(solution)/shard_map/ppermute | solution.py:297
  73.4 2.3 %collective-permute-start.22 = (bf16[256,128]{1,0:T(8,128)(2,1)S(1)}, bf16[256,128]{1,0:T(8,128)(2,1)S(1)}, u32[]{:S(2)}, u32[]{:S(2)}) collective-permute-start(bf16[256,128]{1,0:T(8,128)(2,1)S(1)} %select_convert_fusion), channel_id=1, source_target_pairs={{0,1},{1,0},{2,3},{3,2},{4,5},{5,4},{6,7},{7,6},{8,9},{9,8},{10,11... | collective-permute-start | bytes 196616 | tf_op jit(solution)/shard_map/ppermute | solution.py:32
  92.8 3.3 %collective-permute-start.23 = (bf16[2048,128]{1,0:T(8,128)(2,1)S(1)}, bf16[2048,128]{1,0:T(8,128)(2,1)S(1)}, u32[]{:S(2)}, u32[]{:S(2)}) collective-permute-start(bf16[2048,128]{1,0:T(8,128)(2,1)S(1)} %bitcast.39), channel_id=1, source_target_pairs={{0,1},{1,0},{2,3},{3,2},{4,5},{5,4},{6,7},{7,6},{8,9},{9,8},{10,11... | collective-permute-start | bytes 1572872 | tf_op jit(solution)/shard_map/ppermute | solution.py:32

commit v2 on v1

--- a/solution.py
+++ b/solution.py
@@ -257,13 +257,13 @@
 
 
 def assemble_kernel(mine_ref, other_ref, out_ref):
-    core = lax.axis_index("core")
-    for y in range(4):
-        for xh in range(2):
-            rows = slice((2 * y + xh) * 2 * BLK, (2 * y + xh + 1) * 2 * BLK)
-            for ref, which in ((mine_ref, core), (other_ref, 1 - core)):
-                column = pl.multiple_of((2 * (xh * 4 + y) + which) * HD, HD)
-                out_ref[:, pl.ds(column, HD)] = ref[rows, :].astype(F32)
+    xh, y, core = lax.axis_index("xh"), lax.axis_index("y"), lax.axis_index("core")
+    for r, by in enumerate((2, 1, -1, 0)):
+        source_y = lax.rem(y - by + 4, 4)
+        for ref, side in ((mine_ref, core), (other_ref, 1 - core)):
+            source_xh = jnp.where(side == 0, xh, 1 - xh)
+            column = pl.multiple_of((source_xh * 4 + source_y) * 2 * HD, 2 * HD)
+            out_ref[:, pl.ds(column, 2 * HD)] = ref[r * 2 * BLK : (r + 1) * 2 * BLK, :].astype(F32)
 
 
 def assemble(mine, other):
@@ -296,40 +296,52 @@
         ]
         return lax.ppermute(value, ("x", "z", "core"), pairs)
 
-    def halves(value):
-        return jnp.where(first, value[:, :HD], value[:, HD:]), jnp.where(first, value[:, HD:], value[:, :HD])
+    def split(value, by):
+        pairs = [(2 * i + c, 2 * ((i + (by, -by)[c]) % 8) + c) for i in range(8) for c in range(2)]
+        return lax.ppermute(value, ("z", "core"), pairs)
+
+    def across_heads(value, by):
+        pairs = [
+            ((a * 4 + i) * 2 + c, ((a ^ c) * 4 + (i + by) % 4) * 2 + c)
+            for a in range(2)
+            for i in range(4)
+            for c in range(2)
+            if by or c
+        ]
+        return lax.ppermute(value, ("xh", "y", "core"), pairs)
 
     near = lax.dynamic_slice_in_dim(keyval, (xh * 4 + y) * 2 * HD, 2 * HD, 1)
     up2, down2 = across(near, 2), across(near, -2)
     up1, down1 = across(near, 1), across(near, -1)
     own = jnp.where(first, near, across(near, 0))
     up3, down3 = shift(up2, "z", 8, 1), shift(down2, "z", 8, -1)
-    up4, down4 = shift(up2[:BLK], "z", 8, 2), shift(down2[BLK:], "z", 8, -2)
+    four = split(jnp.where(first, up2, down2), 2)
     reached = jnp.concatenate([own, down1, down2, up2, up1], axis=0)
-    relayed = jnp.concatenate([down3, up4, down4, up3], axis=0)
+    relayed = jnp.concatenate([down3, four, up3], axis=0)
     sides = [(mine, swap(mine, "core")) for mine in (reached, relayed)]
     gathered = [jnp.where(first, mine, other) for mine, other in sides]
     gathered = jnp.concatenate(gathered + [jnp.where(first, other, mine) for mine, other in sides], axis=0)
+    inputs = (vis_blocks, vis_count, block_order, query, grad_out, segment_ids.reshape(NB, BLK))
+    inputs = [pltpu.with_memory_space_constraint(v, pltpu.HBM) for v in inputs]
     attn_out, grad_query, other_relayed, mine_relayed, other, mine = attention(
-        vis_blocks, vis_count, block_order, query, grad_out, segment_ids.reshape(NB, BLK), gathered
+        *inputs, gathered
     )
     relayed = wide(mine_relayed, swap(other_relayed, "core")).astype(BF)
     reached = wide(mine, swap(other, "core")).astype(BF)
     joined = dict(zip(RELAYED + REACHED, [relayed[k] for k in range(3)] + [reached[k] for k in range(5)]))
-    for4_up, for4_down = shift(joined[4][:BLK], "z", 8, 2), shift(joined[4][BLK:], "z", 8, -2)
+    for4 = split(joined[4], 2)
     for3_up, for3_down = shift(joined[3], "z", 8, 1), shift(joined[5], "z", 8, -1)
-    up2 = jnp.concatenate(
-        [wide(joined[2][:BLK], for3_up[:BLK], for4_up), wide(joined[2][BLK:], for3_up[BLK:])], axis=0
-    )
-    down2 = jnp.concatenate(
-        [wide(joined[6][:BLK], for3_down[:BLK]), wide(joined[6][BLK:], for3_down[BLK:], for4_down)], axis=0
-    )
+    zero = jnp.zeros_like(for4)
+    up2 = wide(joined[2], for3_up, jnp.where(first, for4, zero))
+    down2 = wide(joined[6], for3_down, jnp.where(first, zero, for4))
     for2_up, for2_down = across(up2.astype(BF), 2), across(down2.astype(BF), -2)
     for1_up, for1_down = across(joined[1], 1), across(joined[7], -1)
     own = jnp.where(first, joined[0], across(joined[0], 0))
-    kept, given = halves(wide(own, for1_up, for1_down, for2_up, for2_down))
-    summed = wide(kept, swap(given.astype(BF), "core")).astype(BF)
-    mine = lax.all_to_all(jnp.concatenate([summed] * KVH, axis=0), ("y", "xh"), 0, 0, tiled=True)
+    summed = wide(own, for1_up, for1_down, for2_up, for2_down).astype(BF)
+    summed = wide(summed, swap(summed, "core")).astype(BF)
+    pieces = [across_heads(summed, by) for by in (2, 1, -1, 0)]
+    pieces[3] = jnp.where(first, summed, pieces[3])
+    mine = jnp.concatenate(pieces, axis=0)
     return attn_out, grad_query, assemble(mine, swap(mine, "core"))
 
 

time: 97.3 us -> 97.7 us (level)
  blocking collectives: 17 us -> 0 us
  waiting for transfers between devices: 18.3 us -> 32.1 us
  starting transfers between devices: 41.5 us -> 45.4 us
    all_to_all x1 -> x0, blocking collectives: 17 us -> none  [shards(): lax.all_to_all(jnp.concatenate([summed] * KVH, axis=0), ('y', 'xh'), 0, 0...]
    ppermute x0 -> x6, starting transfers between devices: none -> 12 us  [the longest x4 11.5 us: across_heads(): return lax.ppermute(value, ('xh', 'y', 'core'), pairs)]
    ppermute x0 -> x6, waiting for transfers between devices: none -> 11.3 us  [the longest x2 6.51 us: split(): return lax.ppermute(value, ('z', 'core'), pairs)]
    ppermute x8 -> x4, starting transfers between devices: 13 us -> 4.47 us  [shift(): lax.ppermute(value, axis, [(i, (i + by) % size) for i in range(size)])]
    ppermute x10, starting transfers between devices: 22.8 us -> 25.9 us  [across(): return lax.ppermute(value, ('x', 'z', 'core'), pairs)]
    ppermute x6, starting transfers between devices: 5.7 us -> 3 us  [swap(): return lax.ppermute(value, axis, [(0, 1), (1, 0)])]
    ppermute x8 -> x4, waiting for transfers between devices: 6.01 us -> 7.57 us  [shift(): lax.ppermute(value, axis, [(i, (i + by) % size) for i in range(size)])]
    ppermute x10, waiting for transfers between devices: 6.6 us -> 7.71 us  [across(): return lax.ppermute(value, ('x', 'z', 'core'), pairs)]
  transfers between devices with their start and end apart: 24 -> 26, of which waited for: 14 -> 16; matrix products, arithmetic and copies ran while one was open for 2% -> 2% of each run, Pallas kernels for 0% -> 0%
where the time goes in v2:
time: 97.7 us; the launch traced here: 97.9 us
  starting transfers between devices  45.4 us (46%)
  waiting for transfers between devices  32.1 us (33%)
  Pallas kernels  16.1 us (16%)
  other arithmetic  1.82 us (2%)
  local copies, waits for them, and re-layouts  1.72 us (2%)
    ppermute x10, starting transfers between devices, across(): return lax.ppermute(value, ('x', 'z', 'core'), pairs)  25.9 us
    pallas_call x1, Pallas kernels, attention(): pl.pallas_call(attention_kernel, in_specs=[hbm] * 6 + [vmem], out_specs=[...  14.6 us
    ppermute x4, starting transfers between devices, across_heads(): return lax.ppermute(value, ('xh', 'y', 'core'), pairs)  11.5 us
    ppermute x10, waiting for transfers between devices, across(): return lax.ppermute(value, ('x', 'z', 'core'), pairs)  7.71 us
    ppermute x4, waiting for transfers between devices, shift(): lax.ppermute(value, axis, [(i, (i + by) % size) for i in range(size)])  7.57 us
    ppermute x2, waiting for transfers between devices, split(): return lax.ppermute(value, ('z', 'core'), pairs)  6.51 us
    ppermute x6, waiting for transfers between devices, swap(): return lax.ppermute(value, axis, [(0, 1), (1, 0)])  5.51 us
    ppermute x4, waiting for transfers between devices, across_heads(): return lax.ppermute(value, ('xh', 'y', 'core'), pairs)  4.78 us
  transfers between devices with their start and end apart: 26, of which 16 were waited for; matrix products, arithmetic and copies ran while one was open for 2% of the time, Pallas kernels for 0%

profile of v2, /device:TPU:1, one launch (start us, length us, event | category | flops | bytes accessed | tf_op | source)
XLA Modules:
  0.0 97.9 jit_solution(2187092307264094946)
XLA Ops:
  0.6 0.9 constant_dynamic-slice_fusion
  1.6 7.9 %collective-permute-start.2 = (bf16[256,256]{1,0:T(8,128)(2,1)S(1)}, bf16[256,256]{1,0:T(8,128)(2,1)S(1)}, u32[]{:S(2)}, u32[]{:S(2)}) collective-permute-start(bf16[256,256]{1,0:T(8,128)(2,1)S(1)} %constant_dynamic-slice_fusion), channel_id=1, source_target_pairs={{0,96},{1,225},{16,112},{17,241},{32,0},{33,129},{48,16},{49,145},... | collective-permute-start | bytes 393224 | tf_op jit(solution)/shard_map/ppermute | solution.py:297
  9.4 2.2 %collective-permute-start = (bf16[256,256]{1,0:T(8,128)(2,1)S(1)}, bf16[256,256]{1,0:T(8,128)(2,1)S(1)}, u32[]{:S(2)}, u32[]{:S(2)}) collective-permute-start(bf16[256,256]{1,0:T(8,128)(2,1)S(1)} %constant_dynamic-slice_fusion), channel_id=1, source_target_pairs={{1,129},{17,145},{33,161},{49,177},{65,193},{81,209},{97,225},{113... | collective-permute-start | bytes 393224 | tf_op jit(solution)/shard_map/ppermute | solution.py:297
  11.7 4.0 %collective-permute-start.1 = (bf16[256,256]{1,0:T(8,128)(2,1)S(1)}, bf16[256,256]{1,0:T(8,128)(2,1)S(1)}, u32[]{:S(2)}, u32[]{:S(2)}) collective-permute-start(bf16[256,256]{1,0:T(8,128)(2,1)S(1)} %constant_dynamic-slice_fusion), channel_id=1, source_target_pairs={{0,112},{1,241},{16,0},{17,129},{32,16},{33,145},{48,32},{49,161},... | collective-permute-start | bytes 393224 | tf_op jit(solution)/shard_map/ppermute | solution.py:297
  15.7 1.5 %collective-permute-start.6 = (bf16[256,256]{1,0:T(8,128)(2,1)S(1)}, bf16[256,256]{1,0:T(8,128)(2,1)S(1)}, u32[]{:S(2)}, u32[]{:S(2)}) collective-permute-start(bf16[256,256]{1,0:T(8,128)(2,1)S(1)} %collective-permute-done.2), channel_id=1, source_target_pairs={{0,112},{16,0},{32,16},{48,32},{64,48},{80,64},{96,80},{112,96},{1... | collective-permute-start | bytes 393224 | tf_op jit(solution)/shard_map/ppermute | solution.py:28
  17.2 0.9 select_dynamic-update-slice_fusion
  18.4 2.9 %collective-permute-done.3 = bf16[256,256]{1,0:T(8,128)(2,1)S(1)} collective-permute-done((bf16[256,256]{1,0:T(8,128)(2,1)S(1)}, bf16[256,256]{1,0:T(8,128)(2,1)S(1)}, u32[]{:S(2)}, u32[]{:S(2)}) %collective-permute-start.3) | collective-permute-done | bytes 131104 | tf_op jit(solution)/shard_map/ppermute | solution.py:297
  21.8 2.1 %collective-permute-start.4 = (bf16[256,256]{1,0:T(8,128)(2,1)S(1)}, bf16[256,256]{1,0:T(8,128)(2,1)S(1)}, u32[]{:S(2)}, u32[]{:S(2)}) collective-permute-start(bf16[256,256]{1,0:T(8,128)(2,1)S(1)} %constant_dynamic-slice_fusion), channel_id=1, source_target_pairs={{0,16},{1,145},{16,32},{17,161},{32,48},{33,177},{48,64},{49,193},... | collective-permute-start | bytes 393224 | tf_op jit(solution)/shard_map/ppermute | solution.py:297
  24.0 3.6 %collective-permute-done.7 = bf16[256,256]{1,0:T(8,128)(2,1)S(1)} collective-permute-done((bf16[256,256]{1,0:T(8,128)(2,1)S(1)}, bf16[256,256]{1,0:T(8,128)(2,1)S(1)}, u32[]{:S(2)}, u32[]{:S(2)}) %collective-permute-start.7) | collective-permute-done | bytes 131104 | tf_op jit(solution)/shard_map/ppermute | solution.py:301
  27.7 4.5 %collective-permute-done.8 = bf16[256,256]{1,0:T(8,128)(2,1)S(1)} collective-permute-done((bf16[256,256]{1,0:T(8,128)(2,1)S(1)}, bf16[256,256]{1,0:T(8,128)(2,1)S(1)}, u32[]{:S(2)}, u32[]{:S(2)}) %collective-permute-start.8) | collective-permute-done | bytes 131104 | tf_op jit(solution)/shard_map/ppermute | solution.py:28
  32.2 1.6 %collective-permute-start.9 = (bf16[768,256]{1,0:T(8,128)(2,1)S(1)}, bf16[768,256]{1,0:T(8,128)(2,1)S(1)}, u32[]{:S(2)}, u32[]{:S(2)}) collective-permute-start(bf16[768,256]{1,0:T(8,128)(2,1)S(1)} %constant_dynamic-update-slice_fusion.4), channel_id=1, source_target_pairs={{0,1},{1,0},{2,3},{3,2},{4,5},{5,4},{6,7},{7,6},{8,9},{9,8},{10,11... | collective-permute-start | bytes 1179656 | tf_op jit(solution)/shard_map/ppermute | solution.py:32
  35.2 0.9 collective-permute-done.5
  36.3 14.6 %attention.1 = (bf16[256,512]{1,0:T(8,128)(2,1)}, bf16[256,512]{1,0:T(8,128)(2,1)}, bf16[3,256,256]{2,1,0:T(8,128)(2,1)S(1)}, bf16[3,256,256]{2,1,0:T(8,128)(2,1...) custom-call(s32[32,24]{1,0:T(8,128)} %copy.10.vis_any, s32[32]{0:T(128)} %count_any.1, ...), custom_call_target="tpu_custom_call" | custom-call | tf_op jit(solution)/shard_map/attention/pallas_call | solution.py:227
  51.5 1.2 %collective-permute-done.14 = bf16[3,256,256]{2,1,0:T(8,128)(2,1)S(1)} collective-permute-done((bf16[3,256,256]{2,1,0:T(8,128)(2,1)S(1)}, bf16[3,256,256]{2,1,0:T(8,128)(2,1)S(1)}, u32[]{:S(2)}, u32[]{:S(2)}) %collective-permute-start.14) | collective-permute-done | bytes 393248 | tf_op jit(solution)/shard_map/ppermute | solution.py:32
  53.1 2.7 %collective-permute-start.18 = (bf16[256,256]{1,0:T(8,128)(2,1)S(1)}, bf16[256,256]{1,0:T(8,128)(2,1)S(1)}, u32[]{:S(2)}, u32[]{:S(2)}) collective-permute-start(bf16[256,256]{1,0:T(8,128)(2,1)S(1)} %get-tuple-element.25), channel_id=1, source_target_pairs={{0,112},{16,0},{32,16},{48,32},{64,48},{80,64},{96,80},{112,96},{1... | collective-permute-start | bytes 393224 | tf_op jit(solution)/shard_map/ppermute | solution.py:28
  56.0 3.1 %collective-permute-done.15 = bf16[256,256]{1,0:T(8,128)(2,1)S(1)} collective-permute-done((bf16[256,256]{1,0:T(8,128)(2,1)S(1)}, bf16[256,256]{1,0:T(8,128)(2,1)S(1)}, u32[]{:S(2)}, u32[]{:S(2)}) %collective-permute-start.15) | collective-permute-done | bytes 131104 | tf_op jit(solution)/shard_map/ppermute | solution.py:28
  59.1 2.9 %collective-permute-done.16 = bf16[256,256]{1,0:T(8,128)(2,1)S(1)} collective-permute-done((bf16[256,256]{1,0:T(8,128)(2,1)S(1)}, bf16[256,256]{1,0:T(8,128)(2,1)S(1)}, u32[]{:S(2)}, u32[]{:S(2)}) %collective-permute-start.16) | collective-permute-done | bytes 131104 | tf_op jit(solution)/shard_map/ppermute | solution.py:301
  62.2 4.4 %collective-permute-start.19 = (bf16[256,256]{1,0:T(8,128)(2,1)S(1)}, bf16[256,256]{1,0:T(8,128)(2,1)S(1)}, u32[]{:S(2)}, u32[]{:S(2)}) collective-permute-start(bf16[256,256]{1,0:T(8,128)(2,1)S(1)} %get-tuple-element.18), channel_id=1, source_target_pairs={{0,96},{1,225},{16,112},{17,241},{32,0},{33,129},{48,16},{49,145},... | collective-permute-start | bytes 393224 | tf_op jit(solution)/shard_map/ppermute | solution.py:297
  66.6 2.7 %collective-permute-start.11 = (bf16[256,256]{1,0:T(8,128)(2,1)S(1)}, bf16[256,256]{1,0:T(8,128)(2,1)S(1)}, u32[]{:S(2)}, u32[]{:S(2)}) collective-permute-start(bf16[256,256]{1,0:T(8,128)(2,1)S(1)} %get-tuple-element.21), channel_id=1, source_target_pairs={{1,129},{17,145},{33,161},{49,177},{65,193},{81,209},{97,225},{113... | collective-permute-start | bytes 393224 | tf_op jit(solution)/shard_map/ppermute | solution.py:297
  69.3 1.1 %collective-permute-start.13 = (bf16[256,256]{1,0:T(8,128)(2,1)S(1)}, bf16[256,256]{1,0:T(8,128)(2,1)S(1)}, u32[]{:S(2)}, u32[]{:S(2)}) collective-permute-start(bf16[256,256]{1,0:T(8,128)(2,1)S(1)} %get-tuple-element.22), channel_id=1, source_target_pairs={{0,112},{1,241},{16,0},{17,129},{32,16},{33,145},{48,32},{49,161},... | collective-permute-start | bytes 393224 | tf_op jit(solution)/shard_map/ppermute | solution.py:297
  70.4 1.4 %collective-permute-start.12 = (bf16[256,256]{1,0:T(8,128)(2,1)S(1)}, bf16[256,256]{1,0:T(8,128)(2,1)S(1)}, u32[]{:S(2)}, u32[]{:S(2)}) collective-permute-start(bf16[256,256]{1,0:T(8,128)(2,1)S(1)} %get-tuple-element.23), channel_id=1, source_target_pairs={{0,16},{1,145},{16,32},{17,161},{32,48},{33,177},{48,64},{49,193},... | collective-permute-start | bytes 393224 | tf_op jit(solution)/shard_map/ppermute | solution.py:297
  72.2 3.0 %collective-permute-done.11 = bf16[256,256]{1,0:T(8,128)(2,1)S(1)} collective-permute-done((bf16[256,256]{1,0:T(8,128)(2,1)S(1)}, bf16[256,256]{1,0:T(8,128)(2,1)S(1)}, u32[]{:S(2)}, u32[]{:S(2)}) %collective-permute-start.11) | collective-permute-done | bytes 131104 | tf_op jit(solution)/shard_map/ppermute | solution.py:297
  75.2 1.1 %collective-permute-done.12 = bf16[256,256]{1,0:T(8,128)(2,1)S(1)} collective-permute-done((bf16[256,256]{1,0:T(8,128)(2,1)S(1)}, bf16[256,256]{1,0:T(8,128)(2,1)S(1)}, u32[]{:S(2)}, u32[]{:S(2)}) %collective-permute-start.12) | collective-permute-done | bytes 131104 | tf_op jit(solution)/shard_map/ppermute | solution.py:297
  77.1 1.0 %collective-permute-done.20 = bf16[256,256]{1,0:T(8,128)(2,1)S(1)} collective-permute-done((bf16[256,256]{1,0:T(8,128)(2,1)S(1)}, bf16[256,256]{1,0:T(8,128)(2,1)S(1)}, u32[]{:S(2)}, u32[]{:S(2)}) %collective-permute-start.20) | collective-permute-done | bytes 131104 | tf_op jit(solution)/shard_map/ppermute | solution.py:32
  78.1 4.6 %collective-permute-start.24 = (bf16[256,256]{1,0:T(8,128)(2,1)S(1)}, bf16[256,256]{1,0:T(8,128)(2,1)S(1)}, u32[]{:S(2)}, u32[]{:S(2)}) collective-permute-start(bf16[256,256]{1,0:T(8,128)(2,1)S(1)} %add_convert_fusion.2), channel_id=1, source_target_pairs={{1,9},{3,11},{5,13},{7,15},{9,1},{11,3},{13,5},{15,7},{17,25},{19,... | collective-permute-start | bytes 393224 | tf_op jit(solution)/shard_map/ppermute | solution.py:311
  82.7 2.8 %collective-permute-start.23 = (bf16[256,256]{1,0:T(8,128)(2,1)S(1)}, bf16[256,256]{1,0:T(8,128)(2,1)S(1)}, u32[]{:S(2)}, u32[]{:S(2)}) collective-permute-start(bf16[256,256]{1,0:T(8,128)(2,1)S(1)} %add_convert_fusion.2), channel_id=1, source_target_pairs={{0,6},{1,15},{2,0},{3,9},{4,2},{5,11},{6,4},{7,13},{8,14},{9,7},{1... | collective-permute-start | bytes 393224 | tf_op jit(solution)/shard_map/ppermute | solution.py:311
  85.5 1.1 %collective-permute-start.22 = (bf16[256,256]{1,0:T(8,128)(2,1)S(1)}, bf16[256,256]{1,0:T(8,128)(2,1)S(1)}, u32[]{:S(2)}, u32[]{:S(2)}) collective-permute-start(bf16[256,256]{1,0:T(8,128)(2,1)S(1)} %add_convert_fusion.2), channel_id=1, source_target_pairs={{0,2},{1,11},{2,4},{3,13},{4,6},{5,15},{6,0},{7,9},{8,10},{9,3},{1... | collective-permute-start | bytes 393224 | tf_op jit(solution)/shard_map/ppermute | solution.py:311
  86.7 2.9 %collective-permute-start.21 = (bf16[256,256]{1,0:T(8,128)(2,1)S(1)}, bf16[256,256]{1,0:T(8,128)(2,1)S(1)}, u32[]{:S(2)}, u32[]{:S(2)}) collective-permute-start(bf16[256,256]{1,0:T(8,128)(2,1)S(1)} %add_convert_fusion.2), channel_id=1, source_target_pairs={{0,4},{1,13},{2,6},{3,15},{4,0},{5,9},{6,2},{7,11},{8,12},{9,5},{1... | collective-permute-start | bytes 393224 | tf_op jit(solution)/shard_map/ppermute | solution.py:311
  89.6 3.3 %collective-permute-done.22 = bf16[256,256]{1,0:T(8,128)(2,1)S(1)} collective-permute-done((bf16[256,256]{1,0:T(8,128)(2,1)S(1)}, bf16[256,256]{1,0:T(8,128)(2,1)S(1)}, u32[]{:S(2)}, u32[]{:S(2)}) %collective-permute-start.22) | collective-permute-done | bytes 131104 | tf_op jit(solution)/shard_map/ppermute | solution.py:311
  93.0 1.4 %collective-permute-done.21 = bf16[256,256]{1,0:T(8,128)(2,1)S(1)} collective-permute-done((bf16[256,256]{1,0:T(8,128)(2,1)S(1)}, bf16[256,256]{1,0:T(8,128)(2,1)S(1)}, u32[]{:S(2)}, u32[]{:S(2)}) %collective-permute-start.21) | collective-permute-done | bytes 131104 | tf_op jit(solution)/shard_map/ppermute | solution.py:311
  94.5 1.9 %collective-permute-done.25.other_ref = bf16[1024,256]{1,0:T(8,128)(2,1)S(1)} collective-permute-done((bf16[1024,256]{1,0:T(8,128)(2,1)S(1)}, bf16[1024,256]{1,0:T(8,128)(2,1)S(1)}, u32[]{:S(2)}, u32[]{:S(2)}) %collective-permute-start.25) | collective-permute-done | bytes 524320 | tf_op jit(solution)/shard_map/ppermute | solution.py:32
  96.4 1.5 %assemble.1 = f32[256,2048]{1,0:T(8,128)} custom-call(bf16[1024,256]{1,0:T(8,128)(2,1)S(1)} %pad_maximum_fusion.1.mine_ref, bf16[1024,256]{1,0:T(8,128)(2,1)S(1)} %collective-permute-done.25.other_ref), custom_call_target="tpu_custom_call" | custom-call | tf_op jit(solution)/shard_map/assemble/pallas_call | solution.py:271
  (46 shorter events, 5.5 us)
Async XLA Ops:
  0.6 33.3 %copy-start = (s32[32,24]{0,1:T(8,128)S(1)}, s32[32,24]{0,1:T(8,128)}, u32[]{:S(2)}) copy-start(s32[32,24]{0,1:T(8,128)} %param.10) | copy-start | bytes 9220
  1.6 14.1 %collective-permute-start.2 = (bf16[256,256]{1,0:T(8,128)(2,1)S(1)}, bf16[256,256]{1,0:T(8,128)(2,1)S(1)}, u32[]{:S(2)}, u32[]{:S(2)}) collective-permute-start(bf16[256,256]{1,0:T(8,128)(2,1)S(1)} %constant_dynamic-slice_fusion), channel_id=1, source_target_pairs={{0,96},{1,225},{16,112},{17,241},{32,0},{33,129},{48,16},{49,145},... | collective-permute-start | bytes 393224 | tf_op jit(solution)/shard_map/ppermute | solution.py:297
  9.4 7.8 %collective-permute-start = (bf16[256,256]{1,0:T(8,128)(2,1)S(1)}, bf16[256,256]{1,0:T(8,128)(2,1)S(1)}, u32[]{:S(2)}, u32[]{:S(2)}) collective-permute-start(bf16[256,256]{1,0:T(8,128)(2,1)S(1)} %constant_dynamic-slice_fusion), channel_id=1, source_target_pairs={{1,129},{17,145},{33,161},{49,177},{65,193},{81,209},{97,225},{113... | collective-permute-start | bytes 393224 | tf_op jit(solution)/shard_map/ppermute | solution.py:297
  11.6 9.7 %collective-permute-start.3 = (bf16[256,256]{1,0:T(8,128)(2,1)S(1)}, bf16[256,256]{1,0:T(8,128)(2,1)S(1)}, u32[]{:S(2)}, u32[]{:S(2)}) collective-permute-start(bf16[256,256]{1,0:T(8,128)(2,1)S(1)} %constant_dynamic-slice_fusion), channel_id=1, source_target_pairs={{0,32},{1,161},{16,48},{17,177},{32,64},{33,193},{48,80},{49,209},... | collective-permute-start | bytes 393224 | tf_op jit(solution)/shard_map/ppermute | solution.py:297
  11.7 6.7 %collective-permute-start.1 = (bf16[256,256]{1,0:T(8,128)(2,1)S(1)}, bf16[256,256]{1,0:T(8,128)(2,1)S(1)}, u32[]{:S(2)}, u32[]{:S(2)}) collective-permute-start(bf16[256,256]{1,0:T(8,128)(2,1)S(1)} %constant_dynamic-slice_fusion), channel_id=1, source_target_pairs={{0,112},{1,241},{16,0},{17,129},{32,16},{33,145},{48,32},{49,161},... | collective-permute-start | bytes 393224 | tf_op jit(solution)/shard_map/ppermute | solution.py:297
  15.7 8.3 %collective-permute-start.6 = (bf16[256,256]{1,0:T(8,128)(2,1)S(1)}, bf16[256,256]{1,0:T(8,128)(2,1)S(1)}, u32[]{:S(2)}, u32[]{:S(2)}) collective-permute-start(bf16[256,256]{1,0:T(8,128)(2,1)S(1)} %collective-permute-done.2), channel_id=1, source_target_pairs={{0,112},{16,0},{32,16},{48,32},{64,48},{80,64},{96,80},{112,96},{1... | collective-permute-start | bytes 393224 | tf_op jit(solution)/shard_map/ppermute | solution.py:28
  21.3 6.4 %collective-permute-start.7 = (bf16[256,256]{1,0:T(8,128)(2,1)S(1)}, bf16[256,256]{1,0:T(8,128)(2,1)S(1)}, u32[]{:S(2)}, u32[]{:S(2)}) collective-permute-start(bf16[256,256]{1,0:T(8,128)(2,1)S(1)} %get-tuple-element.28), channel_id=1, source_target_pairs={{0,32},{1,97},{16,48},{17,113},{32,64},{33,1},{48,80},{49,17},{64,... | collective-permute-start | bytes 393224 | tf_op jit(solution)/shard_map/ppermute | solution.py:301
  21.8 12.0 %collective-permute-start.4 = (bf16[256,256]{1,0:T(8,128)(2,1)S(1)}, bf16[256,256]{1,0:T(8,128)(2,1)S(1)}, u32[]{:S(2)}, u32[]{:S(2)}) collective-permute-start(bf16[256,256]{1,0:T(8,128)(2,1)S(1)} %constant_dynamic-slice_fusion), channel_id=1, source_target_pairs={{0,16},{1,145},{16,32},{17,161},{32,48},{33,177},{48,64},{49,193},... | collective-permute-start | bytes 393224 | tf_op jit(solution)/shard_map/ppermute | solution.py:297
  23.9 8.3 %collective-permute-start.8 = (bf16[256,256]{1,0:T(8,128)(2,1)S(1)}, bf16[256,256]{1,0:T(8,128)(2,1)S(1)}, u32[]{:S(2)}, u32[]{:S(2)}) collective-permute-start(bf16[256,256]{1,0:T(8,128)(2,1)S(1)} %collective-permute-done.3), channel_id=1, source_target_pairs={{0,16},{16,32},{32,48},{48,64},{64,80},{80,96},{96,112},{112,0},{1... | collective-permute-start | bytes 393224 | tf_op jit(solution)/shard_map/ppermute | solution.py:28
  32.2 2.9 %collective-permute-start.9 = (bf16[768,256]{1,0:T(8,128)(2,1)S(1)}, bf16[768,256]{1,0:T(8,128)(2,1)S(1)}, u32[]{:S(2)}, u32[]{:S(2)}) collective-permute-start(bf16[768,256]{1,0:T(8,128)(2,1)S(1)} %constant_dynamic-update-slice_fusion.4), channel_id=1, source_target_pairs={{0,1},{1,0},{2,3},{3,2},{4,5},{5,4},{6,7},{7,6},{8,9},{9,8},{10,11... | collective-permute-start | bytes 1179656 | tf_op jit(solution)/shard_map/ppermute | solution.py:32
  33.8 2.3 %collective-permute-start.5 = (bf16[1280,256]{1,0:T(8,128)(2,1)S(1)}, bf16[1280,256]{1,0:T(8,128)(2,1)S(1)}, u32[]{:S(2)}, u32[]{:S(2)}) collective-permute-start(bf16[1280,256]{1,0:T(8,128)(2,1)S(1)} %constant_dynamic-update-slice_fusion), channel_id=1, source_target_pairs={{0,1},{1,0},{2,3},{3,2},{4,5},{5,4},{6,7},{7,6},{8,9},{9,8},{10,11... | collective-permute-start | bytes 1966088 | tf_op jit(solution)/shard_map/ppermute | solution.py:32
  50.9 1.8 %collective-permute-start.14 = (bf16[3,256,256]{2,1,0:T(8,128)(2,1)S(1)}, bf16[3,256,256]{2,1,0:T(8,128)(2,1)S(1)}, u32[]{:S(2)}, u32[]{:S(2)}) collective-permute-start(bf16[3,256,256]{2,1,0:T(8,128)(2,1)S(1)} %get-tuple-element.14), channel_id=1, source_target_pairs={{0,1},{1,0},{2,3},{3,2},{4,5},{5,4},{6,7},{7,6},{8,9},{9,8},{10,11... | collective-permute-start | bytes 1179656 | tf_op jit(solution)/shard_map/ppermute | solution.py:32
  51.3 4.5 %collective-permute-start.10 = (bf16[5,256,256]{2,1,0:T(8,128)(2,1)S(1)}, bf16[5,256,256]{2,1,0:T(8,128)(2,1)S(1)}, u32[]{:S(2)}, u32[]{:S(2)}) collective-permute-start(bf16[5,256,256]{2,1,0:T(8,128)(2,1)S(1)} %get-tuple-element.12), channel_id=1, source_target_pairs={{0,1},{1,0},{2,3},{3,2},{4,5},{5,4},{6,7},{7,6},{8,9},{9,8},{10,11... | collective-permute-start | bytes 1966088 | tf_op jit(solution)/shard_map/ppermute | solution.py:32
  52.9 6.2 %collective-permute-start.15 = (bf16[256,256]{1,0:T(8,128)(2,1)S(1)}, bf16[256,256]{1,0:T(8,128)(2,1)S(1)}, u32[]{:S(2)}, u32[]{:S(2)}) collective-permute-start(bf16[256,256]{1,0:T(8,128)(2,1)S(1)} %get-tuple-element.24), channel_id=1, source_target_pairs={{0,16},{16,32},{32,48},{48,64},{64,80},{80,96},{96,112},{112,0},{1... | collective-permute-start | bytes 393224 | tf_op jit(solution)/shard_map/ppermute | solution.py:28
  53.1 5.9 %collective-permute-start.18 = (bf16[256,256]{1,0:T(8,128)(2,1)S(1)}, bf16[256,256]{1,0:T(8,128)(2,1)S(1)}, u32[]{:S(2)}, u32[]{:S(2)}) collective-permute-start(bf16[256,256]{1,0:T(8,128)(2,1)S(1)} %get-tuple-element.25), channel_id=1, source_target_pairs={{0,112},{16,0},{32,16},{48,32},{64,48},{80,64},{96,80},{112,96},{1... | collective-permute-start | bytes 393224 | tf_op jit(solution)/shard_map/ppermute | solution.py:28
  55.8 6.1 %collective-permute-start.16 = (bf16[256,256]{1,0:T(8,128)(2,1)S(1)}, bf16[256,256]{1,0:T(8,128)(2,1)S(1)}, u32[]{:S(2)}, u32[]{:S(2)}) collective-permute-start(bf16[256,256]{1,0:T(8,128)(2,1)S(1)} %get-tuple-element.26), channel_id=1, source_target_pairs={{0,32},{1,97},{16,48},{17,113},{32,64},{33,1},{48,80},{49,17},{64,... | collective-permute-start | bytes 393224 | tf_op jit(solution)/shard_map/ppermute | solution.py:301
  62.0 10.2 %collective-permute-start.17 = (bf16[256,256]{1,0:T(8,128)(2,1)S(1)}, bf16[256,256]{1,0:T(8,128)(2,1)S(1)}, u32[]{:S(2)}, u32[]{:S(2)}) collective-permute-start(bf16[256,256]{1,0:T(8,128)(2,1)S(1)} %get-tuple-element.17), channel_id=1, source_target_pairs={{0,32},{1,161},{16,48},{17,177},{32,64},{33,193},{48,80},{49,209},... | collective-permute-start | bytes 393224 | tf_op jit(solution)/shard_map/ppermute | solution.py:297
  62.2 10.0 %collective-permute-start.19 = (bf16[256,256]{1,0:T(8,128)(2,1)S(1)}, bf16[256,256]{1,0:T(8,128)(2,1)S(1)}, u32[]{:S(2)}, u32[]{:S(2)}) collective-permute-start(bf16[256,256]{1,0:T(8,128)(2,1)S(1)} %get-tuple-element.18), channel_id=1, source_target_pairs={{0,96},{1,225},{16,112},{17,241},{32,0},{33,129},{48,16},{49,145},... | collective-permute-start | bytes 393224 | tf_op jit(solution)/shard_map/ppermute | solution.py:297
  66.6 8.6 %collective-permute-start.11 = (bf16[256,256]{1,0:T(8,128)(2,1)S(1)}, bf16[256,256]{1,0:T(8,128)(2,1)S(1)}, u32[]{:S(2)}, u32[]{:S(2)}) collective-permute-start(bf16[256,256]{1,0:T(8,128)(2,1)S(1)} %get-tuple-element.21), channel_id=1, source_target_pairs={{1,129},{17,145},{33,161},{49,177},{65,193},{81,209},{97,225},{113... | collective-permute-start | bytes 393224 | tf_op jit(solution)/shard_map/ppermute | solution.py:297
  69.3 5.9 %collective-permute-start.13 = (bf16[256,256]{1,0:T(8,128)(2,1)S(1)}, bf16[256,256]{1,0:T(8,128)(2,1)S(1)}, u32[]{:S(2)}, u32[]{:S(2)}) collective-permute-start(bf16[256,256]{1,0:T(8,128)(2,1)S(1)} %get-tuple-element.22), channel_id=1, source_target_pairs={{0,112},{1,241},{16,0},{17,129},{32,16},{33,145},{48,32},{49,161},... | collective-permute-start | bytes 393224 | tf_op jit(solution)/shard_map/ppermute | solution.py:297
  70.4 6.0 %collective-permute-start.12 = (bf16[256,256]{1,0:T(8,128)(2,1)S(1)}, bf16[256,256]{1,0:T(8,128)(2,1)S(1)}, u32[]{:S(2)}, u32[]{:S(2)}) collective-permute-start(bf16[256,256]{1,0:T(8,128)(2,1)S(1)} %get-tuple-element.23), channel_id=1, source_target_pairs={{0,16},{1,145},{16,32},{17,161},{32,48},{33,177},{48,64},{49,193},... | collective-permute-start | bytes 393224 | tf_op jit(solution)/shard_map/ppermute | solution.py:297
  76.4 1.6 %collective-permute-start.20 = (bf16[256,256]{1,0:T(8,128)(2,1)S(1)}, bf16[256,256]{1,0:T(8,128)(2,1)S(1)}, u32[]{:S(2)}, u32[]{:S(2)}) collective-permute-start(bf16[256,256]{1,0:T(8,128)(2,1)S(1)} %add_convert_fusion.3), channel_id=1, source_target_pairs={{0,1},{1,0},{2,3},{3,2},{4,5},{5,4},{6,7},{7,6},{8,9},{9,8},{10,11... | collective-permute-start | bytes 393224 | tf_op jit(solution)/shard_map/ppermute | solution.py:32
  78.1 11.5 %collective-permute-start.24 = (bf16[256,256]{1,0:T(8,128)(2,1)S(1)}, bf16[256,256]{1,0:T(8,128)(2,1)S(1)}, u32[]{:S(2)}, u32[]{:S(2)}) collective-permute-start(bf16[256,256]{1,0:T(8,128)(2,1)S(1)} %add_convert_fusion.2), channel_id=1, source_target_pairs={{1,9},{3,11},{5,13},{7,15},{9,1},{11,3},{13,5},{15,7},{17,25},{19,... | collective-permute-start | bytes 393224 | tf_op jit(solution)/shard_map/ppermute | solution.py:311
  82.7 6.9 %collective-permute-start.23 = (bf16[256,256]{1,0:T(8,128)(2,1)S(1)}, bf16[256,256]{1,0:T(8,128)(2,1)S(1)}, u32[]{:S(2)}, u32[]{:S(2)}) collective-permute-start(bf16[256,256]{1,0:T(8,128)(2,1)S(1)} %add_convert_fusion.2), channel_id=1, source_target_pairs={{0,6},{1,15},{2,0},{3,9},{4,2},{5,11},{6,4},{7,13},{8,14},{9,7},{1... | collective-permute-start | bytes 393224 | tf_op jit(solution)/shard_map/ppermute | solution.py:311
  85.5 7.4 %collective-permute-start.22 = (bf16[256,256]{1,0:T(8,128)(2,1)S(1)}, bf16[256,256]{1,0:T(8,128)(2,1)S(1)}, u32[]{:S(2)}, u32[]{:S(2)}) collective-permute-start(bf16[256,256]{1,0:T(8,128)(2,1)S(1)} %add_convert_fusion.2), channel_id=1, source_target_pairs={{0,2},{1,11},{2,4},{3,13},{4,6},{5,15},{6,0},{7,9},{8,10},{9,3},{1... | collective-permute-start | bytes 393224 | tf_op jit(solution)/shard_map/ppermute | solution.py:311
  86.7 7.7 %collective-permute-start.21 = (bf16[256,256]{1,0:T(8,128)(2,1)S(1)}, bf16[256,256]{1,0:T(8,128)(2,1)S(1)}, u32[]{:S(2)}, u32[]{:S(2)}) collective-permute-start(bf16[256,256]{1,0:T(8,128)(2,1)S(1)} %add_convert_fusion.2), channel_id=1, source_target_pairs={{0,4},{1,13},{2,6},{3,15},{4,0},{5,9},{6,2},{7,11},{8,12},{9,5},{1... | collective-permute-start | bytes 393224 | tf_op jit(solution)/shard_map/ppermute | solution.py:311
  94.4 2.0 %collective-permute-start.25 = (bf16[1024,256]{1,0:T(8,128)(2,1)S(1)}, bf16[1024,256]{1,0:T(8,128)(2,1)S(1)}, u32[]{:S(2)}, u32[]{:S(2)}) collective-permute-start(bf16[1024,256]{1,0:T(8,128)(2,1)S(1)} %pad_maximum_fusion.1.mine_ref), channel_id=1, source_target_pairs={{0,1},{1,0},{2,3},{3,2},{4,5},{5,4},{6,7},{7,6},{8,9},{9,8},{10,11... | collective-permute-start | bytes 1572872 | tf_op jit(solution)/shard_map/ppermute | solution.py:32

commit v3 on v1

--- a/solution.py
+++ b/solution.py
@@ -292,7 +292,6 @@
             for a in range(2)
             for i in range(8)
             for c in range(2)
-            if by or c
         ]
         return lax.ppermute(value, ("x", "z", "core"), pairs)
 
@@ -302,7 +301,7 @@
     near = lax.dynamic_slice_in_dim(keyval, (xh * 4 + y) * 2 * HD, 2 * HD, 1)
     up2, down2 = across(near, 2), across(near, -2)
     up1, down1 = across(near, 1), across(near, -1)
-    own = jnp.where(first, near, across(near, 0))
+    own = across(near, 0)
     up3, down3 = shift(up2, "z", 8, 1), shift(down2, "z", 8, -1)
     up4, down4 = shift(up2[:BLK], "z", 8, 2), shift(down2[BLK:], "z", 8, -2)
     reached = jnp.concatenate([own, down1, down2, up2, up1], axis=0)
@@ -310,8 +309,10 @@
     sides = [(mine, swap(mine, "core")) for mine in (reached, relayed)]
     gathered = [jnp.where(first, mine, other) for mine, other in sides]
     gathered = jnp.concatenate(gathered + [jnp.where(first, other, mine) for mine, other in sides], axis=0)
+    inputs = (vis_blocks, vis_count, block_order, query, grad_out, segment_ids.reshape(NB, BLK))
+    inputs = [pltpu.with_memory_space_constraint(v, pltpu.HBM) for v in inputs]
     attn_out, grad_query, other_relayed, mine_relayed, other, mine = attention(
-        vis_blocks, vis_count, block_order, query, grad_out, segment_ids.reshape(NB, BLK), gathered
+        *inputs, gathered
     )
     relayed = wide(mine_relayed, swap(other_relayed, "core")).astype(BF)
     reached = wide(mine, swap(other, "core")).astype(BF)
@@ -326,7 +327,7 @@
     )
     for2_up, for2_down = across(up2.astype(BF), 2), across(down2.astype(BF), -2)
     for1_up, for1_down = across(joined[1], 1), across(joined[7], -1)
-    own = jnp.where(first, joined[0], across(joined[0], 0))
+    own = across(joined[0], 0)
     kept, given = halves(wide(own, for1_up, for1_down, for2_up, for2_down))
     summed = wide(kept, swap(given.astype(BF), "core")).astype(BF)
     mine = lax.all_to_all(jnp.concatenate([summed] * KVH, axis=0), ("y", "xh"), 0, 0, tiled=True)

time: 97.3 us -> 97.7 us (level)
  starting transfers between devices: 41.5 us -> 38.9 us
  waiting for transfers between devices: 18.3 us -> 20.9 us
  other arithmetic: 1.76 us -> 0.75 us
    ppermute x6, starting transfers between devices: 5.7 us -> 3.06 us  [swap(): return lax.ppermute(value, axis, [(0, 1), (1, 0)])]
    ppermute x10, waiting for transfers between devices: 6.6 us -> 8.3 us  [across(): return lax.ppermute(value, ('x', 'z', 'core'), pairs)]
    ppermute x8, waiting for transfers between devices: 6.01 us -> 7.35 us  [shift(): lax.ppermute(value, axis, [(i, (i + by) % size) for i in range(size)])]
    unnamed x25 -> x18, local copies, waits for them, and re-layouts: 1.07 us -> 2.04 us
  transfers between devices with their start and end apart: 24 -> 24, of which waited for: 14 -> 14; matrix products, arithmetic and copies ran while one was open for 2% -> 1% of each run, Pallas kernels for 0% -> 0%
where the time goes in v3:
time: 97.7 us; the launch traced here: 97.6 us
  starting transfers between devices  38.9 us (40%)
  waiting for transfers between devices  20.9 us (21%)
  blocking collectives  17.7 us (18%)
  Pallas kernels  16.2 us (17%)
  local copies, waits for them, and re-layouts  2.16 us (2%)
    ppermute x10, starting transfers between devices, across(): return lax.ppermute(value, ('x', 'z', 'core'), pairs)  23 us
    all_to_all x1, blocking collectives, shards(): lax.all_to_all(jnp.concatenate([summed] * KVH, axis=0), ('y', 'xh'), 0, 0...  17.7 us
    pallas_call x1, Pallas kernels, attention(): pl.pallas_call(attention_kernel, in_specs=[hbm] * 6 + [vmem], out_specs=[...  14.6 us
    ppermute x8, starting transfers between devices, shift(): lax.ppermute(value, axis, [(i, (i + by) % size) for i in range(size)])  12.9 us
    ppermute x10, waiting for transfers between devices, across(): return lax.ppermute(value, ('x', 'z', 'core'), pairs)  8.3 us
    ppermute x8, waiting for transfers between devices, shift(): lax.ppermute(value, axis, [(i, (i + by) % size) for i in range(size)])  7.35 us
    ppermute x6, waiting for transfers between devices, swap(): return lax.ppermute(value, axis, [(0, 1), (1, 0)])  5.26 us
    ppermute x6, starting transfers between devices, swap(): return lax.ppermute(value, axis, [(0, 1), (1, 0)])  3.06 us
  transfers between devices with their start and end apart: 24, of which 14 were waited for; matrix products, arithmetic and copies ran while one was open for 1% of the time, Pallas kernels for 0%

profile of v3, /device:TPU:1, one launch (start us, length us, event | category | flops | bytes accessed | tf_op | source)
XLA Modules:
  0.0 97.6 jit_solution(11163711835423047954)
XLA Ops:
  0.7 1.2 %copy-done = bf16[256,2048]{1,0:T(8,128)(2,1)S(1)} copy-done((bf16[256,2048]{1,0:T(8,128)(2,1)S(1)}, bf16[256,2048]{1,0:T(8,128)(2,1)}, u32[]{:S(2)}) %copy-start) | copy-done | bytes 1048600
  1.9 4.8 %collective-permute-start.3 = (bf16[256,256]{1,0:T(8,128)(2,1)S(1)}, bf16[256,256]{1,0:T(8,128)(2,1)S(1)}, u32[]{:S(2)}, u32[]{:S(2)}) collective-permute-start(bf16[256,256]{1,0:T(8,128)(2,1)S(1)} %constant_dynamic-slice_fusion), channel_id=1, source_target_pairs={{0,32},{1,161},{16,48},{17,177},{32,64},{33,193},{48,80},{49,209},... | collective-permute-start | bytes 393224 | tf_op jit(solution)/shard_map/ppermute | solution.py:296
  6.7 3.1 %collective-permute-start.2 = (bf16[256,256]{1,0:T(8,128)(2,1)S(1)}, bf16[256,256]{1,0:T(8,128)(2,1)S(1)}, u32[]{:S(2)}, u32[]{:S(2)}) collective-permute-start(bf16[256,256]{1,0:T(8,128)(2,1)S(1)} %constant_dynamic-slice_fusion), channel_id=1, source_target_pairs={{0,96},{1,225},{16,112},{17,241},{32,0},{33,129},{48,16},{49,145},... | collective-permute-start | bytes 393224 | tf_op jit(solution)/shard_map/ppermute | solution.py:296
  9.8 2.2 %collective-permute-start = (bf16[256,256]{1,0:T(8,128)(2,1)S(1)}, bf16[256,256]{1,0:T(8,128)(2,1)S(1)}, u32[]{:S(2)}, u32[]{:S(2)}) collective-permute-start(bf16[256,256]{1,0:T(8,128)(2,1)S(1)} %constant_dynamic-slice_fusion), channel_id=1, source_target_pairs={{0,0},{1,129},{16,16},{17,145},{32,32},{33,161},{48,48},{49,177},{... | collective-permute-start | bytes 393224 | tf_op jit(solution)/shard_map/ppermute | solution.py:296
  12.0 2.8 %collective-permute-start.1 = (bf16[256,256]{1,0:T(8,128)(2,1)S(1)}, bf16[256,256]{1,0:T(8,128)(2,1)S(1)}, u32[]{:S(2)}, u32[]{:S(2)}) collective-permute-start(bf16[256,256]{1,0:T(8,128)(2,1)S(1)} %constant_dynamic-slice_fusion), channel_id=1, source_target_pairs={{0,112},{1,241},{16,0},{17,129},{32,16},{33,145},{48,32},{49,161},... | collective-permute-start | bytes 393224 | tf_op jit(solution)/shard_map/ppermute | solution.py:296
  14.8 1.5 %collective-permute-start.7 = (bf16[128,256]{1,0:T(8,128)(2,1)S(1)}, bf16[128,256]{1,0:T(8,128)(2,1)S(1)}, u32[]{:S(2)}, u32[]{:S(2)}) collective-permute-start(bf16[128,256]{1,0:T(8,128)(2,1)S(1)} %slice.99), channel_id=1, source_target_pairs={{0,32},{16,48},{32,64},{48,80},{64,96},{80,112},{96,0},{112,16},{1... | collective-permute-start | bytes 196616 | tf_op jit(solution)/shard_map/ppermute | solution.py:28
  16.3 0.7 collective-permute-done.2
  17.0 2.3 %collective-permute-start.8 = (bf16[128,256]{1,0:T(8,128)(2,1)S(1)}, bf16[128,256]{1,0:T(8,128)(2,1)S(1)}, u32[]{:S(2)}, u32[]{:S(2)}) collective-permute-start(bf16[128,256]{1,0:T(8,128)(2,1)S(1)} %slice.100), channel_id=1, source_target_pairs={{0,96},{16,112},{32,0},{48,16},{64,32},{80,48},{96,64},{112,80},{1... | collective-permute-start | bytes 196616 | tf_op jit(solution)/shard_map/ppermute | solution.py:28
  19.3 0.9 collective-permute-start.9
  20.4 1.7 %collective-permute-start.6 = (bf16[256,256]{1,0:T(8,128)(2,1)S(1)}, bf16[256,256]{1,0:T(8,128)(2,1)S(1)}, u32[]{:S(2)}, u32[]{:S(2)}) collective-permute-start(bf16[256,256]{1,0:T(8,128)(2,1)S(1)} %collective-permute-done.2), channel_id=1, source_target_pairs={{0,112},{16,0},{32,16},{48,32},{64,48},{80,64},{96,80},{112,96},{1... | collective-permute-start | bytes 393224 | tf_op jit(solution)/shard_map/ppermute | solution.py:28
  22.2 4.9 %collective-permute-done.6 = bf16[256,256]{1,0:T(8,128)(2,1)S(1)} collective-permute-done((bf16[256,256]{1,0:T(8,128)(2,1)S(1)}, bf16[256,256]{1,0:T(8,128)(2,1)S(1)}, u32[]{:S(2)}, u32[]{:S(2)}) %collective-permute-start.6) | collective-permute-done | bytes 131104 | tf_op jit(solution)/shard_map/ppermute | solution.py:28
  27.2 0.8 collective-permute-start.10
  28.1 0.7 copy.10.vis_any
  28.8 0.5 collective-permute-done.10
  29.4 0.9 collective-permute-done.5
  30.5 14.6 %attention.1 = (bf16[256,512]{1,0:T(8,128)(2,1)}, bf16[256,512]{1,0:T(8,128)(2,1)}, bf16[3,256,256]{2,1,0:T(8,128)(2,1)S(1)}, bf16[3,256,256]{2,1,0:T(8,128)(2,1...) custom-call(s32[32,24]{1,0:T(8,128)} %copy.10.vis_any, s32[32]{0:T(128)} %count_any.1, ...), custom_call_target="tpu_custom_call" | custom-call | tf_op jit(solution)/shard_map/attention/pallas_call | solution.py:227
  45.9 1.1 %collective-permute-done.15 = bf16[3,256,256]{2,1,0:T(8,128)(2,1)S(1)} collective-permute-done((bf16[3,256,256]{2,1,0:T(8,128)(2,1)S(1)}, bf16[3,256,256]{2,1,0:T(8,128)(2,1)S(1)}, u32[]{:S(2)}, u32[]{:S(2)}) %collective-permute-start.15) | collective-permute-done | bytes 393248 | tf_op jit(solution)/shard_map/ppermute | solution.py:32
  47.2 3.6 %collective-permute-start.20 = (bf16[128,256]{1,0:T(8,128)(2,1)S(1)}, bf16[128,256]{1,0:T(8,128)(2,1)S(1)}, u32[]{:S(2)}, u32[]{:S(2)}) collective-permute-start(bf16[128,256]{1,0:T(8,128)(2,1)S(1)} %get-tuple-element.31), channel_id=1, source_target_pairs={{0,96},{16,112},{32,0},{48,16},{64,32},{80,48},{96,64},{112,80},{1... | collective-permute-start | bytes 196616 | tf_op jit(solution)/shard_map/ppermute | solution.py:28
  50.8 2.7 %collective-permute-start.19 = (bf16[256,256]{1,0:T(8,128)(2,1)S(1)}, bf16[256,256]{1,0:T(8,128)(2,1)S(1)}, u32[]{:S(2)}, u32[]{:S(2)}) collective-permute-start(bf16[256,256]{1,0:T(8,128)(2,1)S(1)} %get-tuple-element.33), channel_id=1, source_target_pairs={{0,112},{16,0},{32,16},{48,32},{64,48},{80,64},{96,80},{112,96},{1... | collective-permute-start | bytes 393224 | tf_op jit(solution)/shard_map/ppermute | solution.py:28
  53.7 2.1 %collective-permute-done.16 = bf16[256,256]{1,0:T(8,128)(2,1)S(1)} collective-permute-done((bf16[256,256]{1,0:T(8,128)(2,1)S(1)}, bf16[256,256]{1,0:T(8,128)(2,1)S(1)}, u32[]{:S(2)}, u32[]{:S(2)}) %collective-permute-start.16) | collective-permute-done | bytes 131104 | tf_op jit(solution)/shard_map/ppermute | solution.py:28
  56.3 4.5 %collective-permute-start.21 = (bf16[256,256]{1,0:T(8,128)(2,1)S(1)}, bf16[256,256]{1,0:T(8,128)(2,1)S(1)}, u32[]{:S(2)}, u32[]{:S(2)}) collective-permute-start(bf16[256,256]{1,0:T(8,128)(2,1)S(1)} %pad_maximum_fusion.2), channel_id=1, source_target_pairs={{0,96},{1,225},{16,112},{17,241},{32,0},{33,129},{48,16},{49,145},... | collective-permute-start | bytes 393224 | tf_op jit(solution)/shard_map/ppermute | solution.py:296
  60.8 0.8 collective-permute-start.18
  61.6 2.0 %collective-permute-start.12 = (bf16[256,256]{1,0:T(8,128)(2,1)S(1)}, bf16[256,256]{1,0:T(8,128)(2,1)S(1)}, u32[]{:S(2)}, u32[]{:S(2)}) collective-permute-start(bf16[256,256]{1,0:T(8,128)(2,1)S(1)} %get-tuple-element.25), channel_id=1, source_target_pairs={{0,0},{1,129},{16,16},{17,145},{32,32},{33,161},{48,48},{49,177},{... | collective-permute-start | bytes 393224 | tf_op jit(solution)/shard_map/ppermute | solution.py:296
  63.6 2.8 %collective-permute-start.14 = (bf16[256,256]{1,0:T(8,128)(2,1)S(1)}, bf16[256,256]{1,0:T(8,128)(2,1)S(1)}, u32[]{:S(2)}, u32[]{:S(2)}) collective-permute-start(bf16[256,256]{1,0:T(8,128)(2,1)S(1)} %get-tuple-element.26), channel_id=1, source_target_pairs={{0,112},{1,241},{16,0},{17,129},{32,16},{33,145},{48,32},{49,161},... | collective-permute-start | bytes 393224 | tf_op jit(solution)/shard_map/ppermute | solution.py:296
  66.4 1.6 %collective-permute-done.21 = bf16[256,256]{1,0:T(8,128)(2,1)S(1)} collective-permute-done((bf16[256,256]{1,0:T(8,128)(2,1)S(1)}, bf16[256,256]{1,0:T(8,128)(2,1)S(1)}, u32[]{:S(2)}, u32[]{:S(2)}) %collective-permute-start.21) | collective-permute-done | bytes 131104 | tf_op jit(solution)/shard_map/ppermute | solution.py:296
  68.0 2.7 %collective-permute-done.18 = bf16[256,256]{1,0:T(8,128)(2,1)S(1)} collective-permute-done((bf16[256,256]{1,0:T(8,128)(2,1)S(1)}, bf16[256,256]{1,0:T(8,128)(2,1)S(1)}, u32[]{:S(2)}, u32[]{:S(2)}) %collective-permute-start.18) | collective-permute-done | bytes 131104 | tf_op jit(solution)/shard_map/ppermute | solution.py:296
  70.9 3.0 %collective-permute-done.13 = bf16[256,256]{1,0:T(8,128)(2,1)S(1)} collective-permute-done((bf16[256,256]{1,0:T(8,128)(2,1)S(1)}, bf16[256,256]{1,0:T(8,128)(2,1)S(1)}, u32[]{:S(2)}, u32[]{:S(2)}) %collective-permute-start.13) | collective-permute-done | bytes 131104 | tf_op jit(solution)/shard_map/ppermute | solution.py:296
  74.1 1.2 %collective-permute-done.22 = bf16[256,128]{1,0:T(8,128)(2,1)S(1)} collective-permute-done((bf16[256,128]{1,0:T(8,128)(2,1)S(1)}, bf16[256,128]{1,0:T(8,128)(2,1)S(1)}, u32[]{:S(2)}, u32[]{:S(2)}) %collective-permute-start.22) | collective-permute-done | bytes 65568 | tf_op jit(solution)/shard_map/ppermute | solution.py:32
  75.5 17.7 %all_to_all.11 = bf16[8,256,128]{2,1,0:T(8,128)(2,1)S(1)} all-to-all(bf16[8,256,128]{2,1,0:T(8,128)(2,1)S(1)} %bitcast.39), channel_id=1, replica_groups=mesh['x'=2,'z'=8,'xh'=2,'y'=4,'core'=2] {'y','xh'}, dimensions={0} | all-to-all | bytes 1048576 | tf_op jit(solution)/shard_map/all_to_all | solution.py:333
  93.2 1.3 %collective-permute-start.23 = (bf16[2048,128]{1,0:T(8,128)(2,1)S(1)}, bf16[2048,128]{1,0:T(8,128)(2,1)S(1)}, u32[]{:S(2)}, u32[]{:S(2)}) collective-permute-start(bf16[2048,128]{1,0:T(8,128)(2,1)S(1)} %bitcast.37), channel_id=1, source_target_pairs={{0,1},{1,0},{2,3},{3,2},{4,5},{5,4},{6,7},{7,6},{8,9},{9,8},{10,11... | collective-permute-start | bytes 1572872 | tf_op jit(solution)/shard_map/ppermute | solution.py:32
  94.4 1.5 %collective-permute-done.23.other_ref = bf16[2048,128]{1,0:T(8,128)(2,1)S(1)} collective-permute-done((bf16[2048,128]{1,0:T(8,128)(2,1)S(1)}, bf16[2048,128]{1,0:T(8,128)(2,1)S(1)}, u32[]{:S(2)}, u32[]{:S(2)}) %collective-permute-start.23) | collective-permute-done | bytes 524320 | tf_op jit(solution)/shard_map/ppermute | solution.py:32
  96.0 1.6 %assemble.1 = f32[256,2048]{1,0:T(8,128)} custom-call(bf16[2048,128]{1,0:T(8,128)(2,1)S(1)} %bitcast.38, bf16[2048,128]{1,0:T(8,128)(2,1)S(1)} %collective-permute-done.23.other_ref), custom_call_target="tpu_custom_call" | custom-call | tf_op jit(solution)/shard_map/assemble/pallas_call | solution.py:271
  (57 shorter events, 2.9 us)
Async XLA Ops:
  0.6 1.2 %copy-start = (bf16[256,2048]{1,0:T(8,128)(2,1)S(1)}, bf16[256,2048]{1,0:T(8,128)(2,1)}, u32[]{:S(2)}) copy-start(bf16[256,2048]{1,0:T(8,128)(2,1)} %param.8) | copy-start | bytes 3145732
  0.6 27.5 %copy-start.1 = (s32[32,24]{0,1:T(8,128)S(1)}, s32[32,24]{0,1:T(8,128)}, u32[]{:S(2)}) copy-start(s32[32,24]{0,1:T(8,128)} %param.10) | copy-start | bytes 9220
  1.9 12.9 %collective-permute-start.3 = (bf16[256,256]{1,0:T(8,128)(2,1)S(1)}, bf16[256,256]{1,0:T(8,128)(2,1)S(1)}, u32[]{:S(2)}, u32[]{:S(2)}) collective-permute-start(bf16[256,256]{1,0:T(8,128)(2,1)S(1)} %constant_dynamic-slice_fusion), channel_id=1, source_target_pairs={{0,32},{1,161},{16,48},{17,177},{32,64},{33,193},{48,80},{49,209},... | collective-permute-start | bytes 393224 | tf_op jit(solution)/shard_map/ppermute | solution.py:296
  6.7 10.3 %collective-permute-start.2 = (bf16[256,256]{1,0:T(8,128)(2,1)S(1)}, bf16[256,256]{1,0:T(8,128)(2,1)S(1)}, u32[]{:S(2)}, u32[]{:S(2)}) collective-permute-start(bf16[256,256]{1,0:T(8,128)(2,1)S(1)} %constant_dynamic-slice_fusion), channel_id=1, source_target_pairs={{0,96},{1,225},{16,112},{17,241},{32,0},{33,129},{48,16},{49,145},... | collective-permute-start | bytes 393224 | tf_op jit(solution)/shard_map/ppermute | solution.py:296
  9.8 9.5 %collective-permute-start = (bf16[256,256]{1,0:T(8,128)(2,1)S(1)}, bf16[256,256]{1,0:T(8,128)(2,1)S(1)}, u32[]{:S(2)}, u32[]{:S(2)}) collective-permute-start(bf16[256,256]{1,0:T(8,128)(2,1)S(1)} %constant_dynamic-slice_fusion), channel_id=1, source_target_pairs={{0,0},{1,129},{16,16},{17,145},{32,32},{33,161},{48,48},{49,177},{... | collective-permute-start | bytes 393224 | tf_op jit(solution)/shard_map/ppermute | solution.py:296
  12.0 8.4 %collective-permute-start.1 = (bf16[256,256]{1,0:T(8,128)(2,1)S(1)}, bf16[256,256]{1,0:T(8,128)(2,1)S(1)}, u32[]{:S(2)}, u32[]{:S(2)}) collective-permute-start(bf16[256,256]{1,0:T(8,128)(2,1)S(1)} %constant_dynamic-slice_fusion), channel_id=1, source_target_pairs={{0,112},{1,241},{16,0},{17,129},{32,16},{33,145},{48,32},{49,161},... | collective-permute-start | bytes 393224 | tf_op jit(solution)/shard_map/ppermute | solution.py:296
  14.8 13.2 %collective-permute-start.4 = (bf16[256,256]{1,0:T(8,128)(2,1)S(1)}, bf16[256,256]{1,0:T(8,128)(2,1)S(1)}, u32[]{:S(2)}, u32[]{:S(2)}) collective-permute-start(bf16[256,256]{1,0:T(8,128)(2,1)S(1)} %constant_dynamic-slice_fusion), channel_id=1, source_target_pairs={{0,16},{1,145},{16,32},{17,161},{32,48},{33,177},{48,64},{49,193},... | collective-permute-start | bytes 393224 | tf_op jit(solution)/shard_map/ppermute | solution.py:296
  14.8 12.3 %collective-permute-start.7 = (bf16[128,256]{1,0:T(8,128)(2,1)S(1)}, bf16[128,256]{1,0:T(8,128)(2,1)S(1)}, u32[]{:S(2)}, u32[]{:S(2)}) collective-permute-start(bf16[128,256]{1,0:T(8,128)(2,1)S(1)} %slice.99), channel_id=1, source_target_pairs={{0,32},{16,48},{32,64},{48,80},{64,96},{80,112},{96,0},{112,16},{1... | collective-permute-start | bytes 196616 | tf_op jit(solution)/shard_map/ppermute | solution.py:28
  17.0 10.1 %collective-permute-start.8 = (bf16[128,256]{1,0:T(8,128)(2,1)S(1)}, bf16[128,256]{1,0:T(8,128)(2,1)S(1)}, u32[]{:S(2)}, u32[]{:S(2)}) collective-permute-start(bf16[128,256]{1,0:T(8,128)(2,1)S(1)} %slice.100), channel_id=1, source_target_pairs={{0,96},{16,112},{32,0},{48,16},{64,32},{80,48},{96,64},{112,80},{1... | collective-permute-start | bytes 196616 | tf_op jit(solution)/shard_map/ppermute | solution.py:28
  19.3 7.8 %collective-permute-start.9 = (bf16[256,256]{1,0:T(8,128)(2,1)S(1)}, bf16[256,256]{1,0:T(8,128)(2,1)S(1)}, u32[]{:S(2)}, u32[]{:S(2)}) collective-permute-start(bf16[256,256]{1,0:T(8,128)(2,1)S(1)} %collective-permute-done.3), channel_id=1, source_target_pairs={{0,16},{16,32},{32,48},{48,64},{64,80},{80,96},{96,112},{112,0},{1... | collective-permute-start | bytes 393224 | tf_op jit(solution)/shard_map/ppermute | solution.py:28
  20.4 6.7 %collective-permute-start.6 = (bf16[256,256]{1,0:T(8,128)(2,1)S(1)}, bf16[256,256]{1,0:T(8,128)(2,1)S(1)}, u32[]{:S(2)}, u32[]{:S(2)}) collective-permute-start(bf16[256,256]{1,0:T(8,128)(2,1)S(1)} %collective-permute-done.2), channel_id=1, source_target_pairs={{0,112},{16,0},{32,16},{48,32},{64,48},{80,64},{96,80},{112,96},{1... | collective-permute-start | bytes 393224 | tf_op jit(solution)/shard_map/ppermute | solution.py:28
  27.2 2.2 %collective-permute-start.10 = (bf16[768,256]{1,0:T(8,128)(2,1)S(1)}, bf16[768,256]{1,0:T(8,128)(2,1)S(1)}, u32[]{:S(2)}, u32[]{:S(2)}) collective-permute-start(bf16[768,256]{1,0:T(8,128)(2,1)S(1)} %constant_dynamic-update-slice_fusion.5), channel_id=1, source_target_pairs={{0,1},{1,0},{2,3},{3,2},{4,5},{5,4},{6,7},{7,6},{8,9},{9,8},{10,11... | collective-permute-start | bytes 1179656 | tf_op jit(solution)/shard_map/ppermute | solution.py:32
  28.0 2.3 %collective-permute-start.5 = (bf16[1280,256]{1,0:T(8,128)(2,1)S(1)}, bf16[1280,256]{1,0:T(8,128)(2,1)S(1)}, u32[]{:S(2)}, u32[]{:S(2)}) collective-permute-start(bf16[1280,256]{1,0:T(8,128)(2,1)S(1)} %constant_dynamic-update-slice_fusion), channel_id=1, source_target_pairs={{0,1},{1,0},{2,3},{3,2},{4,5},{5,4},{6,7},{7,6},{8,9},{9,8},{10,11... | collective-permute-start | bytes 1966088 | tf_op jit(solution)/shard_map/ppermute | solution.py:32
  45.1 1.8 %collective-permute-start.15 = (bf16[3,256,256]{2,1,0:T(8,128)(2,1)S(1)}, bf16[3,256,256]{2,1,0:T(8,128)(2,1)S(1)}, u32[]{:S(2)}, u32[]{:S(2)}) collective-permute-start(bf16[3,256,256]{2,1,0:T(8,128)(2,1)S(1)} %get-tuple-element.14), channel_id=1, source_target_pairs={{0,1},{1,0},{2,3},{3,2},{4,5},{5,4},{6,7},{7,6},{8,9},{9,8},{10,11... | collective-permute-start | bytes 1179656 | tf_op jit(solution)/shard_map/ppermute | solution.py:32
  45.6 7.9 %collective-permute-start.11 = (bf16[5,256,256]{2,1,0:T(8,128)(2,1)S(1)}, bf16[5,256,256]{2,1,0:T(8,128)(2,1)S(1)}, u32[]{:S(2)}, u32[]{:S(2)}) collective-permute-start(bf16[5,256,256]{2,1,0:T(8,128)(2,1)S(1)} %get-tuple-element.12), channel_id=1, source_target_pairs={{0,1},{1,0},{2,3},{3,2},{4,5},{5,4},{6,7},{7,6},{8,9},{9,8},{10,11... | collective-permute-start | bytes 1966088 | tf_op jit(solution)/shard_map/ppermute | solution.py:32
  47.1 6.6 %collective-permute-start.17 = (bf16[128,256]{1,0:T(8,128)(2,1)S(1)}, bf16[128,256]{1,0:T(8,128)(2,1)S(1)}, u32[]{:S(2)}, u32[]{:S(2)}) collective-permute-start(bf16[128,256]{1,0:T(8,128)(2,1)S(1)} %get-tuple-element.30), channel_id=1, source_target_pairs={{0,32},{16,48},{32,64},{48,80},{64,96},{80,112},{96,0},{112,16},{1... | collective-permute-start | bytes 196616 | tf_op jit(solution)/shard_map/ppermute | solution.py:28
  47.2 6.6 %collective-permute-start.20 = (bf16[128,256]{1,0:T(8,128)(2,1)S(1)}, bf16[128,256]{1,0:T(8,128)(2,1)S(1)}, u32[]{:S(2)}, u32[]{:S(2)}) collective-permute-start(bf16[128,256]{1,0:T(8,128)(2,1)S(1)} %get-tuple-element.31), channel_id=1, source_target_pairs={{0,96},{16,112},{32,0},{48,16},{64,32},{80,48},{96,64},{112,80},{1... | collective-permute-start | bytes 196616 | tf_op jit(solution)/shard_map/ppermute | solution.py:28
  50.7 5.1 %collective-permute-start.16 = (bf16[256,256]{1,0:T(8,128)(2,1)S(1)}, bf16[256,256]{1,0:T(8,128)(2,1)S(1)}, u32[]{:S(2)}, u32[]{:S(2)}) collective-permute-start(bf16[256,256]{1,0:T(8,128)(2,1)S(1)} %get-tuple-element.32), channel_id=1, source_target_pairs={{0,16},{16,32},{32,48},{48,64},{64,80},{80,96},{96,112},{112,0},{1... | collective-permute-start | bytes 393224 | tf_op jit(solution)/shard_map/ppermute | solution.py:28
  50.8 5.4 %collective-permute-start.19 = (bf16[256,256]{1,0:T(8,128)(2,1)S(1)}, bf16[256,256]{1,0:T(8,128)(2,1)S(1)}, u32[]{:S(2)}, u32[]{:S(2)}) collective-permute-start(bf16[256,256]{1,0:T(8,128)(2,1)S(1)} %get-tuple-element.33), channel_id=1, source_target_pairs={{0,112},{16,0},{32,16},{48,32},{64,48},{80,64},{96,80},{112,96},{1... | collective-permute-start | bytes 393224 | tf_op jit(solution)/shard_map/ppermute | solution.py:28
  56.3 11.7 %collective-permute-start.21 = (bf16[256,256]{1,0:T(8,128)(2,1)S(1)}, bf16[256,256]{1,0:T(8,128)(2,1)S(1)}, u32[]{:S(2)}, u32[]{:S(2)}) collective-permute-start(bf16[256,256]{1,0:T(8,128)(2,1)S(1)} %pad_maximum_fusion.2), channel_id=1, source_target_pairs={{0,96},{1,225},{16,112},{17,241},{32,0},{33,129},{48,16},{49,145},... | collective-permute-start | bytes 393224 | tf_op jit(solution)/shard_map/ppermute | solution.py:296
  60.8 9.9 %collective-permute-start.18 = (bf16[256,256]{1,0:T(8,128)(2,1)S(1)}, bf16[256,256]{1,0:T(8,128)(2,1)S(1)}, u32[]{:S(2)}, u32[]{:S(2)}) collective-permute-start(bf16[256,256]{1,0:T(8,128)(2,1)S(1)} %pad_maximum_fusion.1), channel_id=1, source_target_pairs={{0,32},{1,161},{16,48},{17,177},{32,64},{33,193},{48,80},{49,209},... | collective-permute-start | bytes 393224 | tf_op jit(solution)/shard_map/ppermute | solution.py:296
  61.6 9.1 %collective-permute-start.12 = (bf16[256,256]{1,0:T(8,128)(2,1)S(1)}, bf16[256,256]{1,0:T(8,128)(2,1)S(1)}, u32[]{:S(2)}, u32[]{:S(2)}) collective-permute-start(bf16[256,256]{1,0:T(8,128)(2,1)S(1)} %get-tuple-element.25), channel_id=1, source_target_pairs={{0,0},{1,129},{16,16},{17,145},{32,32},{33,161},{48,48},{49,177},{... | collective-permute-start | bytes 393224 | tf_op jit(solution)/shard_map/ppermute | solution.py:296
  63.6 7.3 %collective-permute-start.14 = (bf16[256,256]{1,0:T(8,128)(2,1)S(1)}, bf16[256,256]{1,0:T(8,128)(2,1)S(1)}, u32[]{:S(2)}, u32[]{:S(2)}) collective-permute-start(bf16[256,256]{1,0:T(8,128)(2,1)S(1)} %get-tuple-element.26), channel_id=1, source_target_pairs={{0,112},{1,241},{16,0},{17,129},{32,16},{33,145},{48,32},{49,161},... | collective-permute-start | bytes 393224 | tf_op jit(solution)/shard_map/ppermute | solution.py:296
  66.4 7.4 %collective-permute-start.13 = (bf16[256,256]{1,0:T(8,128)(2,1)S(1)}, bf16[256,256]{1,0:T(8,128)(2,1)S(1)}, u32[]{:S(2)}, u32[]{:S(2)}) collective-permute-start(bf16[256,256]{1,0:T(8,128)(2,1)S(1)} %get-tuple-element.27), channel_id=1, source_target_pairs={{0,16},{1,145},{16,32},{17,161},{32,48},{33,177},{48,64},{49,193},... | collective-permute-start | bytes 393224 | tf_op jit(solution)/shard_map/ppermute | solution.py:296
  74.0 1.3 %collective-permute-start.22 = (bf16[256,128]{1,0:T(8,128)(2,1)S(1)}, bf16[256,128]{1,0:T(8,128)(2,1)S(1)}, u32[]{:S(2)}, u32[]{:S(2)}) collective-permute-start(bf16[256,128]{1,0:T(8,128)(2,1)S(1)} %select_convert_fusion), channel_id=1, source_target_pairs={{0,1},{1,0},{2,3},{3,2},{4,5},{5,4},{6,7},{7,6},{8,9},{9,8},{10,11... | collective-permute-start | bytes 196616 | tf_op jit(solution)/shard_map/ppermute | solution.py:32
  93.2 2.8 %collective-permute-start.23 = (bf16[2048,128]{1,0:T(8,128)(2,1)S(1)}, bf16[2048,128]{1,0:T(8,128)(2,1)S(1)}, u32[]{:S(2)}, u32[]{:S(2)}) collective-permute-start(bf16[2048,128]{1,0:T(8,128)(2,1)S(1)} %bitcast.37), channel_id=1, source_target_pairs={{0,1},{1,0},{2,3},{3,2},{4,5},{5,4},{6,7},{7,6},{8,9},{9,8},{10,11... | collective-permute-start | bytes 1572872 | tf_op jit(solution)/shard_map/ppermute | solution.py:32

commit v4 on v3

--- a/solution.py
+++ b/solution.py
@@ -13,7 +13,7 @@
 BLK = 128
 NB = 32
 HEADS = 4
-GROUP = 4
+GROUP = 8
 REACHED = (0, 1, 2, 6, 7)
 RELAYED = (3, 4, 5)
 ROWS = HEADS * BLK
@@ -73,7 +73,7 @@
         inv[order[j]] = jnp.where(shard // 8 == x, 0, 16) + 2 * at + lax.rem(j, 2)
         return carry
 
-    lax.fori_loop(0, NB, place, 0)
+    lax.fori_loop(0, NB, place, 0, unroll=True)
     for copy in inputs[1:5]:
         copy.wait()
 
@@ -171,7 +171,6 @@
         high = norm.astype(BF)
         rest_low = (norm - high.astype(F32)).astype(BF)
         norm_col = tn(jnp.concatenate([high, rest_low], axis=0), eighth)
-        delta = jnp.zeros((8, ROWS), F32)
         for h in range(HEADS):
             rows = slice(h * BLK, (h + 1) * BLK)
             out_ref[at, h * HD : (h + 1) * HD] = out_low[rows]
@@ -183,7 +182,12 @@
         deltas.append((nt(ones, high) + nt(ones, rest_low))[0:1])
     outputs = [
         pltpu.make_async_copy(out_ref, out_any, io_sem.at[6]),
-        pltpu.make_async_copy(dq_ref, dq_any, io_sem.at[7]),
+        *[
+            pltpu.make_async_copy(
+                dq_ref.at[pl.ds(i * BLK, BLK)], dq_any.at[pl.ds(i * BLK, BLK)], io_sem.at[7 + i]
+            )
+            for i in range(2)
+        ],
     ]
     outputs[0].start()
     for i in range(2):
@@ -198,14 +202,12 @@
             return carry
 
         lax.fori_loop(0, groups[i], grad_pass, 0)
-
-    for i in range(2):
         at = slice(i * BLK, (i + 1) * BLK)
         dq = jnp.transpose((accum[i] * SCALE).astype(BF))
         for h in range(HEADS):
             dq_ref[at, h * HD : (h + 1) * HD] = dq[h * BLK : (h + 1) * BLK]
-
-    outputs[1].start()
+        outputs[1 + i].start()
+
     for ref, side, start in (
         (other_relayed_ref, 1 - core, 5),
         (mine_relayed_ref, core, 5),
@@ -249,7 +251,7 @@
             pltpu.SMEM((NB,), jnp.int32),
             pltpu.SMEM((NB,), jnp.int32),
             pltpu.SMEM((NB,), jnp.int32),
-            pltpu.SemaphoreType.DMA((8,)),
+            pltpu.SemaphoreType.DMA((9,)),
         ],
         compiler_params=pltpu.CompilerParams(vmem_limit_bytes=48 * 1024 * 1024),
         name="attention",

time: 97.7 us -> 96.7 us (0.990)
  Pallas kernels: 16.2 us -> 14.9 us
    pallas_call x1, Pallas kernels: 14.6 us -> 13.3 us  [attention(): pl.pallas_call(attention_kernel, in_specs=[hbm] * 6 + [vmem], out_specs=[...]
    ppermute x6, starting transfers between devices: 3.06 us -> 4.05 us  [swap(): return lax.ppermute(value, axis, [(0, 1), (1, 0)])]
  transfers between devices with their start and end apart: 24 -> 24, of which waited for: 14 -> 13; matrix products, arithmetic and copies ran while one was open for 1% -> 1% of each run, Pallas kernels for 0% -> 0%
where the time goes in v4:
time: 96.7 us; the launch traced here: 96.3 us
  starting transfers between devices  39.8 us (41%)
  waiting for transfers between devices  20.7 us (21%)
  blocking collectives  17.2 us (18%)
  Pallas kernels  14.9 us (15%)
  local copies, waits for them, and re-layouts  2.16 us (2%)
    ppermute x10, starting transfers between devices, across(): return lax.ppermute(value, ('x', 'z', 'core'), pairs)  22.9 us
    all_to_all x1, blocking collectives, shards(): lax.all_to_all(jnp.concatenate([summed] * KVH, axis=0), ('y', 'xh'), 0, 0...  17.2 us
    pallas_call x1, Pallas kernels, attention(): pl.pallas_call(attention_kernel, in_specs=[hbm] * 6 + [vmem], out_specs=[...  13.3 us
    ppermute x8, starting transfers between devices, shift(): lax.ppermute(value, axis, [(i, (i + by) % size) for i in range(size)])  12.9 us
    ppermute x10, waiting for transfers between devices, across(): return lax.ppermute(value, ('x', 'z', 'core'), pairs)  7.98 us
    ppermute x8, waiting for transfers between devices, shift(): lax.ppermute(value, axis, [(i, (i + by) % size) for i in range(size)])  7.62 us
    ppermute x6, waiting for transfers between devices, swap(): return lax.ppermute(value, axis, [(0, 1), (1, 0)])  5.07 us
    ppermute x6, starting transfers between devices, swap(): return lax.ppermute(value, axis, [(0, 1), (1, 0)])  4.05 us
  transfers between devices with their start and end apart: 24, of which 13 were waited for; matrix products, arithmetic and copies ran while one was open for 1% of the time, Pallas kernels for 0%

profile of v4, /device:TPU:1, one launch (start us, length us, event | category | flops | bytes accessed | tf_op | source)
XLA Modules:
  0.0 96.3 jit_solution(8901547208392595474)
XLA Ops:
  0.7 1.2 %copy-done = bf16[256,2048]{1,0:T(8,128)(2,1)S(1)} copy-done((bf16[256,2048]{1,0:T(8,128)(2,1)S(1)}, bf16[256,2048]{1,0:T(8,128)(2,1)}, u32[]{:S(2)}) %copy-start) | copy-done | bytes 1048600
  1.9 4.8 %collective-permute-start.3 = (bf16[256,256]{1,0:T(8,128)(2,1)S(1)}, bf16[256,256]{1,0:T(8,128)(2,1)S(1)}, u32[]{:S(2)}, u32[]{:S(2)}) collective-permute-start(bf16[256,256]{1,0:T(8,128)(2,1)S(1)} %constant_dynamic-slice_fusion), channel_id=1, source_target_pairs={{0,32},{1,161},{16,48},{17,177},{32,64},{33,193},{48,80},{49,209},... | collective-permute-start | bytes 393224 | tf_op jit(solution)/shard_map/ppermute | solution.py:298
  6.7 3.1 %collective-permute-start.2 = (bf16[256,256]{1,0:T(8,128)(2,1)S(1)}, bf16[256,256]{1,0:T(8,128)(2,1)S(1)}, u32[]{:S(2)}, u32[]{:S(2)}) collective-permute-start(bf16[256,256]{1,0:T(8,128)(2,1)S(1)} %constant_dynamic-slice_fusion), channel_id=1, source_target_pairs={{0,96},{1,225},{16,112},{17,241},{32,0},{33,129},{48,16},{49,145},... | collective-permute-start | bytes 393224 | tf_op jit(solution)/shard_map/ppermute | solution.py:298
  9.8 2.2 %collective-permute-start = (bf16[256,256]{1,0:T(8,128)(2,1)S(1)}, bf16[256,256]{1,0:T(8,128)(2,1)S(1)}, u32[]{:S(2)}, u32[]{:S(2)}) collective-permute-start(bf16[256,256]{1,0:T(8,128)(2,1)S(1)} %constant_dynamic-slice_fusion), channel_id=1, source_target_pairs={{0,0},{1,129},{16,16},{17,145},{32,32},{33,161},{48,48},{49,177},{... | collective-permute-start | bytes 393224 | tf_op jit(solution)/shard_map/ppermute | solution.py:298
  12.0 2.8 %collective-permute-start.1 = (bf16[256,256]{1,0:T(8,128)(2,1)S(1)}, bf16[256,256]{1,0:T(8,128)(2,1)S(1)}, u32[]{:S(2)}, u32[]{:S(2)}) collective-permute-start(bf16[256,256]{1,0:T(8,128)(2,1)S(1)} %constant_dynamic-slice_fusion), channel_id=1, source_target_pairs={{0,112},{1,241},{16,0},{17,129},{32,16},{33,145},{48,32},{49,161},... | collective-permute-start | bytes 393224 | tf_op jit(solution)/shard_map/ppermute | solution.py:298
  14.8 1.5 %collective-permute-start.7 = (bf16[128,256]{1,0:T(8,128)(2,1)S(1)}, bf16[128,256]{1,0:T(8,128)(2,1)S(1)}, u32[]{:S(2)}, u32[]{:S(2)}) collective-permute-start(bf16[128,256]{1,0:T(8,128)(2,1)S(1)} %slice.99), channel_id=1, source_target_pairs={{0,32},{16,48},{32,64},{48,80},{64,96},{80,112},{96,0},{112,16},{1... | collective-permute-start | bytes 196616 | tf_op jit(solution)/shard_map/ppermute | solution.py:28
  17.0 2.3 %collective-permute-start.8 = (bf16[128,256]{1,0:T(8,128)(2,1)S(1)}, bf16[128,256]{1,0:T(8,128)(2,1)S(1)}, u32[]{:S(2)}, u32[]{:S(2)}) collective-permute-start(bf16[128,256]{1,0:T(8,128)(2,1)S(1)} %slice.100), channel_id=1, source_target_pairs={{0,96},{16,112},{32,0},{48,16},{64,32},{80,48},{96,64},{112,80},{1... | collective-permute-start | bytes 196616 | tf_op jit(solution)/shard_map/ppermute | solution.py:28
  19.3 0.9 collective-permute-start.9
  20.4 1.7 %collective-permute-start.6 = (bf16[256,256]{1,0:T(8,128)(2,1)S(1)}, bf16[256,256]{1,0:T(8,128)(2,1)S(1)}, u32[]{:S(2)}, u32[]{:S(2)}) collective-permute-start(bf16[256,256]{1,0:T(8,128)(2,1)S(1)} %collective-permute-done.2), channel_id=1, source_target_pairs={{0,112},{16,0},{32,16},{48,32},{64,48},{80,64},{96,80},{112,96},{1... | collective-permute-start | bytes 393224 | tf_op jit(solution)/shard_map/ppermute | solution.py:28
  22.2 4.9 %collective-permute-done.6 = bf16[256,256]{1,0:T(8,128)(2,1)S(1)} collective-permute-done((bf16[256,256]{1,0:T(8,128)(2,1)S(1)}, bf16[256,256]{1,0:T(8,128)(2,1)S(1)}, u32[]{:S(2)}, u32[]{:S(2)}) %collective-permute-start.6) | collective-permute-done | bytes 131104 | tf_op jit(solution)/shard_map/ppermute | solution.py:28
  27.2 0.8 collective-permute-start.10
  28.1 0.7 copy.10.vis_any
  29.4 0.9 collective-permute-done.5
  30.5 13.3 %attention.1 = (bf16[256,512]{1,0:T(8,128)(2,1)}, bf16[256,512]{1,0:T(8,128)(2,1)}, bf16[3,256,256]{2,1,0:T(8,128)(2,1)S(1)}, bf16[3,256,256]{2,1,0:T(8,128)(2,1...) custom-call(s32[32,24]{1,0:T(8,128)} %copy.10.vis_any, s32[32]{0:T(128)} %count_any.1, ...), custom_call_target="tpu_custom_call" | custom-call | tf_op jit(solution)/shard_map/attention/pallas_call | solution.py:229
  44.5 1.2 %collective-permute-done.15 = bf16[3,256,256]{2,1,0:T(8,128)(2,1)S(1)} collective-permute-done((bf16[3,256,256]{2,1,0:T(8,128)(2,1)S(1)}, bf16[3,256,256]{2,1,0:T(8,128)(2,1)S(1)}, u32[]{:S(2)}, u32[]{:S(2)}) %collective-permute-start.15) | collective-permute-done | bytes 393248 | tf_op jit(solution)/shard_map/ppermute | solution.py:32
  45.8 1.1 %collective-permute-start.17 = (bf16[128,256]{1,0:T(8,128)(2,1)S(1)}, bf16[128,256]{1,0:T(8,128)(2,1)S(1)}, u32[]{:S(2)}, u32[]{:S(2)}) collective-permute-start(bf16[128,256]{1,0:T(8,128)(2,1)S(1)} %get-tuple-element.30), channel_id=1, source_target_pairs={{0,32},{16,48},{32,64},{48,80},{64,96},{80,112},{96,0},{112,16},{1... | collective-permute-start | bytes 196616 | tf_op jit(solution)/shard_map/ppermute | solution.py:28
  46.9 2.6 %collective-permute-start.20 = (bf16[128,256]{1,0:T(8,128)(2,1)S(1)}, bf16[128,256]{1,0:T(8,128)(2,1)S(1)}, u32[]{:S(2)}, u32[]{:S(2)}) collective-permute-start(bf16[128,256]{1,0:T(8,128)(2,1)S(1)} %get-tuple-element.31), channel_id=1, source_target_pairs={{0,96},{16,112},{32,0},{48,16},{64,32},{80,48},{96,64},{112,80},{1... | collective-permute-start | bytes 196616 | tf_op jit(solution)/shard_map/ppermute | solution.py:28
  49.5 0.7 collective-permute-start.16
  50.2 2.0 %collective-permute-start.19 = (bf16[256,256]{1,0:T(8,128)(2,1)S(1)}, bf16[256,256]{1,0:T(8,128)(2,1)S(1)}, u32[]{:S(2)}, u32[]{:S(2)}) collective-permute-start(bf16[256,256]{1,0:T(8,128)(2,1)S(1)} %get-tuple-element.33), channel_id=1, source_target_pairs={{0,112},{16,0},{32,16},{48,32},{64,48},{80,64},{96,80},{112,96},{1... | collective-permute-start | bytes 393224 | tf_op jit(solution)/shard_map/ppermute | solution.py:28
  52.5 2.7 %collective-permute-done.16 = bf16[256,256]{1,0:T(8,128)(2,1)S(1)} collective-permute-done((bf16[256,256]{1,0:T(8,128)(2,1)S(1)}, bf16[256,256]{1,0:T(8,128)(2,1)S(1)}, u32[]{:S(2)}, u32[]{:S(2)}) %collective-permute-start.16) | collective-permute-done | bytes 131104 | tf_op jit(solution)/shard_map/ppermute | solution.py:28
  55.3 4.2 %collective-permute-start.21 = (bf16[256,256]{1,0:T(8,128)(2,1)S(1)}, bf16[256,256]{1,0:T(8,128)(2,1)S(1)}, u32[]{:S(2)}, u32[]{:S(2)}) collective-permute-start(bf16[256,256]{1,0:T(8,128)(2,1)S(1)} %pad_maximum_fusion.2), channel_id=1, source_target_pairs={{0,96},{1,225},{16,112},{17,241},{32,0},{33,129},{48,16},{49,145},... | collective-permute-start | bytes 393224 | tf_op jit(solution)/shard_map/ppermute | solution.py:298
  59.8 2.2 %collective-permute-start.12 = (bf16[256,256]{1,0:T(8,128)(2,1)S(1)}, bf16[256,256]{1,0:T(8,128)(2,1)S(1)}, u32[]{:S(2)}, u32[]{:S(2)}) collective-permute-start(bf16[256,256]{1,0:T(8,128)(2,1)S(1)} %get-tuple-element.25), channel_id=1, source_target_pairs={{0,0},{1,129},{16,16},{17,145},{32,32},{33,161},{48,48},{49,177},{... | collective-permute-start | bytes 393224 | tf_op jit(solution)/shard_map/ppermute | solution.py:298
  61.9 3.3 %collective-permute-start.14 = (bf16[256,256]{1,0:T(8,128)(2,1)S(1)}, bf16[256,256]{1,0:T(8,128)(2,1)S(1)}, u32[]{:S(2)}, u32[]{:S(2)}) collective-permute-start(bf16[256,256]{1,0:T(8,128)(2,1)S(1)} %get-tuple-element.26), channel_id=1, source_target_pairs={{0,112},{1,241},{16,0},{17,129},{32,16},{33,145},{48,32},{49,161},... | collective-permute-start | bytes 393224 | tf_op jit(solution)/shard_map/ppermute | solution.py:298
  65.6 1.9 %collective-permute-done.18 = bf16[256,256]{1,0:T(8,128)(2,1)S(1)} collective-permute-done((bf16[256,256]{1,0:T(8,128)(2,1)S(1)}, bf16[256,256]{1,0:T(8,128)(2,1)S(1)}, u32[]{:S(2)}, u32[]{:S(2)}) %collective-permute-start.18) | collective-permute-done | bytes 131104 | tf_op jit(solution)/shard_map/ppermute | solution.py:298
  67.5 1.4 %collective-permute-done.12 = bf16[256,256]{1,0:T(8,128)(2,1)S(1)} collective-permute-done((bf16[256,256]{1,0:T(8,128)(2,1)S(1)}, bf16[256,256]{1,0:T(8,128)(2,1)S(1)}, u32[]{:S(2)}, u32[]{:S(2)}) %collective-permute-start.12) | collective-permute-done | bytes 131104 | tf_op jit(solution)/shard_map/ppermute | solution.py:298
  69.0 3.4 %collective-permute-done.13 = bf16[256,256]{1,0:T(8,128)(2,1)S(1)} collective-permute-done((bf16[256,256]{1,0:T(8,128)(2,1)S(1)}, bf16[256,256]{1,0:T(8,128)(2,1)S(1)}, u32[]{:S(2)}, u32[]{:S(2)}) %collective-permute-start.13) | collective-permute-done | bytes 131104 | tf_op jit(solution)/shard_map/ppermute | solution.py:298
  72.5 0.7 collective-permute-start.22
  73.2 0.9 collective-permute-done.22
  74.3 17.2 %all_to_all.11 = bf16[8,256,128]{2,1,0:T(8,128)(2,1)S(1)} all-to-all(bf16[8,256,128]{2,1,0:T(8,128)(2,1)S(1)} %bitcast.39), channel_id=1, replica_groups=mesh['x'=2,'z'=8,'xh'=2,'y'=4,'core'=2] {'y','xh'}, dimensions={0} | all-to-all | bytes 1048576 | tf_op jit(solution)/shard_map/all_to_all | solution.py:335
  91.4 1.8 %collective-permute-start.23 = (bf16[2048,128]{1,0:T(8,128)(2,1)S(1)}, bf16[2048,128]{1,0:T(8,128)(2,1)S(1)}, u32[]{:S(2)}, u32[]{:S(2)}) collective-permute-start(bf16[2048,128]{1,0:T(8,128)(2,1)S(1)} %bitcast.37), channel_id=1, source_target_pairs={{0,1},{1,0},{2,3},{3,2},{4,5},{5,4},{6,7},{7,6},{8,9},{9,8},{10,11... | collective-permute-start | bytes 1572872 | tf_op jit(solution)/shard_map/ppermute | solution.py:32
  93.2 1.5 %collective-permute-done.23.other_ref = bf16[2048,128]{1,0:T(8,128)(2,1)S(1)} collective-permute-done((bf16[2048,128]{1,0:T(8,128)(2,1)S(1)}, bf16[2048,128]{1,0:T(8,128)(2,1)S(1)}, u32[]{:S(2)}, u32[]{:S(2)}) %collective-permute-start.23) | collective-permute-done | bytes 524320 | tf_op jit(solution)/shard_map/ppermute | solution.py:32
  94.8 1.6 %assemble.1 = f32[256,2048]{1,0:T(8,128)} custom-call(bf16[2048,128]{1,0:T(8,128)(2,1)S(1)} %bitcast.38, bf16[2048,128]{1,0:T(8,128)(2,1)S(1)} %collective-permute-done.23.other_ref), custom_call_target="tpu_custom_call" | custom-call | tf_op jit(solution)/shard_map/assemble/pallas_call | solution.py:273
  (57 shorter events, 3.7 us)
Async XLA Ops:
  0.6 1.2 %copy-start = (bf16[256,2048]{1,0:T(8,128)(2,1)S(1)}, bf16[256,2048]{1,0:T(8,128)(2,1)}, u32[]{:S(2)}) copy-start(bf16[256,2048]{1,0:T(8,128)(2,1)} %param.8) | copy-start | bytes 3145732
  0.6 27.5 %copy-start.1 = (s32[32,24]{0,1:T(8,128)S(1)}, s32[32,24]{0,1:T(8,128)}, u32[]{:S(2)}) copy-start(s32[32,24]{0,1:T(8,128)} %param.10) | copy-start | bytes 9220
  1.9 12.9 %collective-permute-start.3 = (bf16[256,256]{1,0:T(8,128)(2,1)S(1)}, bf16[256,256]{1,0:T(8,128)(2,1)S(1)}, u32[]{:S(2)}, u32[]{:S(2)}) collective-permute-start(bf16[256,256]{1,0:T(8,128)(2,1)S(1)} %constant_dynamic-slice_fusion), channel_id=1, source_target_pairs={{0,32},{1,161},{16,48},{17,177},{32,64},{33,193},{48,80},{49,209},... | collective-permute-start | bytes 393224 | tf_op jit(solution)/shard_map/ppermute | solution.py:298
  6.7 10.3 %collective-permute-start.2 = (bf16[256,256]{1,0:T(8,128)(2,1)S(1)}, bf16[256,256]{1,0:T(8,128)(2,1)S(1)}, u32[]{:S(2)}, u32[]{:S(2)}) collective-permute-start(bf16[256,256]{1,0:T(8,128)(2,1)S(1)} %constant_dynamic-slice_fusion), channel_id=1, source_target_pairs={{0,96},{1,225},{16,112},{17,241},{32,0},{33,129},{48,16},{49,145},... | collective-permute-start | bytes 393224 | tf_op jit(solution)/shard_map/ppermute | solution.py:298
  9.8 9.5 %collective-permute-start = (bf16[256,256]{1,0:T(8,128)(2,1)S(1)}, bf16[256,256]{1,0:T(8,128)(2,1)S(1)}, u32[]{:S(2)}, u32[]{:S(2)}) collective-permute-start(bf16[256,256]{1,0:T(8,128)(2,1)S(1)} %constant_dynamic-slice_fusion), channel_id=1, source_target_pairs={{0,0},{1,129},{16,16},{17,145},{32,32},{33,161},{48,48},{49,177},{... | collective-permute-start | bytes 393224 | tf_op jit(solution)/shard_map/ppermute | solution.py:298
  12.0 8.4 %collective-permute-start.1 = (bf16[256,256]{1,0:T(8,128)(2,1)S(1)}, bf16[256,256]{1,0:T(8,128)(2,1)S(1)}, u32[]{:S(2)}, u32[]{:S(2)}) collective-permute-start(bf16[256,256]{1,0:T(8,128)(2,1)S(1)} %constant_dynamic-slice_fusion), channel_id=1, source_target_pairs={{0,112},{1,241},{16,0},{17,129},{32,16},{33,145},{48,32},{49,161},... | collective-permute-start | bytes 393224 | tf_op jit(solution)/shard_map/ppermute | solution.py:298
  14.8 13.2 %collective-permute-start.4 = (bf16[256,256]{1,0:T(8,128)(2,1)S(1)}, bf16[256,256]{1,0:T(8,128)(2,1)S(1)}, u32[]{:S(2)}, u32[]{:S(2)}) collective-permute-start(bf16[256,256]{1,0:T(8,128)(2,1)S(1)} %constant_dynamic-slice_fusion), channel_id=1, source_target_pairs={{0,16},{1,145},{16,32},{17,161},{32,48},{33,177},{48,64},{49,193},... | collective-permute-start | bytes 393224 | tf_op jit(solution)/shard_map/ppermute | solution.py:298
  14.8 12.3 %collective-permute-start.7 = (bf16[128,256]{1,0:T(8,128)(2,1)S(1)}, bf16[128,256]{1,0:T(8,128)(2,1)S(1)}, u32[]{:S(2)}, u32[]{:S(2)}) collective-permute-start(bf16[128,256]{1,0:T(8,128)(2,1)S(1)} %slice.99), channel_id=1, source_target_pairs={{0,32},{16,48},{32,64},{48,80},{64,96},{80,112},{96,0},{112,16},{1... | collective-permute-start | bytes 196616 | tf_op jit(solution)/shard_map/ppermute | solution.py:28
  17.0 10.1 %collective-permute-start.8 = (bf16[128,256]{1,0:T(8,128)(2,1)S(1)}, bf16[128,256]{1,0:T(8,128)(2,1)S(1)}, u32[]{:S(2)}, u32[]{:S(2)}) collective-permute-start(bf16[128,256]{1,0:T(8,128)(2,1)S(1)} %slice.100), channel_id=1, source_target_pairs={{0,96},{16,112},{32,0},{48,16},{64,32},{80,48},{96,64},{112,80},{1... | collective-permute-start | bytes 196616 | tf_op jit(solution)/shard_map/ppermute | solution.py:28
  19.3 7.8 %collective-permute-start.9 = (bf16[256,256]{1,0:T(8,128)(2,1)S(1)}, bf16[256,256]{1,0:T(8,128)(2,1)S(1)}, u32[]{:S(2)}, u32[]{:S(2)}) collective-permute-start(bf16[256,256]{1,0:T(8,128)(2,1)S(1)} %collective-permute-done.3), channel_id=1, source_target_pairs={{0,16},{16,32},{32,48},{48,64},{64,80},{80,96},{96,112},{112,0},{1... | collective-permute-start | bytes 393224 | tf_op jit(solution)/shard_map/ppermute | solution.py:28
  20.4 6.7 %collective-permute-start.6 = (bf16[256,256]{1,0:T(8,128)(2,1)S(1)}, bf16[256,256]{1,0:T(8,128)(2,1)S(1)}, u32[]{:S(2)}, u32[]{:S(2)}) collective-permute-start(bf16[256,256]{1,0:T(8,128)(2,1)S(1)} %collective-permute-done.2), channel_id=1, source_target_pairs={{0,112},{16,0},{32,16},{48,32},{64,48},{80,64},{96,80},{112,96},{1... | collective-permute-start | bytes 393224 | tf_op jit(solution)/shard_map/ppermute | solution.py:28
  27.2 2.2 %collective-permute-start.10 = (bf16[768,256]{1,0:T(8,128)(2,1)S(1)}, bf16[768,256]{1,0:T(8,128)(2,1)S(1)}, u32[]{:S(2)}, u32[]{:S(2)}) collective-permute-start(bf16[768,256]{1,0:T(8,128)(2,1)S(1)} %constant_dynamic-update-slice_fusion.5), channel_id=1, source_target_pairs={{0,1},{1,0},{2,3},{3,2},{4,5},{5,4},{6,7},{7,6},{8,9},{9,8},{10,11... | collective-permute-start | bytes 1179656 | tf_op jit(solution)/shard_map/ppermute | solution.py:32
  28.0 2.3 %collective-permute-start.5 = (bf16[1280,256]{1,0:T(8,128)(2,1)S(1)}, bf16[1280,256]{1,0:T(8,128)(2,1)S(1)}, u32[]{:S(2)}, u32[]{:S(2)}) collective-permute-start(bf16[1280,256]{1,0:T(8,128)(2,1)S(1)} %constant_dynamic-update-slice_fusion), channel_id=1, source_target_pairs={{0,1},{1,0},{2,3},{3,2},{4,5},{5,4},{6,7},{7,6},{8,9},{9,8},{10,11... | collective-permute-start | bytes 1966088 | tf_op jit(solution)/shard_map/ppermute | solution.py:32
  43.9 1.8 %collective-permute-start.15 = (bf16[3,256,256]{2,1,0:T(8,128)(2,1)S(1)}, bf16[3,256,256]{2,1,0:T(8,128)(2,1)S(1)}, u32[]{:S(2)}, u32[]{:S(2)}) collective-permute-start(bf16[3,256,256]{2,1,0:T(8,128)(2,1)S(1)} %get-tuple-element.14), channel_id=1, source_target_pairs={{0,1},{1,0},{2,3},{3,2},{4,5},{5,4},{6,7},{7,6},{8,9},{9,8},{10,11... | collective-permute-start | bytes 1179656 | tf_op jit(solution)/shard_map/ppermute | solution.py:32
  44.3 7.9 %collective-permute-start.11 = (bf16[5,256,256]{2,1,0:T(8,128)(2,1)S(1)}, bf16[5,256,256]{2,1,0:T(8,128)(2,1)S(1)}, u32[]{:S(2)}, u32[]{:S(2)}) collective-permute-start(bf16[5,256,256]{2,1,0:T(8,128)(2,1)S(1)} %get-tuple-element.12), channel_id=1, source_target_pairs={{0,1},{1,0},{2,3},{3,2},{4,5},{5,4},{6,7},{7,6},{8,9},{9,8},{10,11... | collective-permute-start | bytes 1966088 | tf_op jit(solution)/shard_map/ppermute | solution.py:32
  45.8 6.6 %collective-permute-start.17 = (bf16[128,256]{1,0:T(8,128)(2,1)S(1)}, bf16[128,256]{1,0:T(8,128)(2,1)S(1)}, u32[]{:S(2)}, u32[]{:S(2)}) collective-permute-start(bf16[128,256]{1,0:T(8,128)(2,1)S(1)} %get-tuple-element.30), channel_id=1, source_target_pairs={{0,32},{16,48},{32,64},{48,80},{64,96},{80,112},{96,0},{112,16},{1... | collective-permute-start | bytes 196616 | tf_op jit(solution)/shard_map/ppermute | solution.py:28
  46.9 5.6 %collective-permute-start.20 = (bf16[128,256]{1,0:T(8,128)(2,1)S(1)}, bf16[128,256]{1,0:T(8,128)(2,1)S(1)}, u32[]{:S(2)}, u32[]{:S(2)}) collective-permute-start(bf16[128,256]{1,0:T(8,128)(2,1)S(1)} %get-tuple-element.31), channel_id=1, source_target_pairs={{0,96},{16,112},{32,0},{48,16},{64,32},{80,48},{96,64},{112,80},{1... | collective-permute-start | bytes 196616 | tf_op jit(solution)/shard_map/ppermute | solution.py:28
  49.5 5.7 %collective-permute-start.16 = (bf16[256,256]{1,0:T(8,128)(2,1)S(1)}, bf16[256,256]{1,0:T(8,128)(2,1)S(1)}, u32[]{:S(2)}, u32[]{:S(2)}) collective-permute-start(bf16[256,256]{1,0:T(8,128)(2,1)S(1)} %get-tuple-element.32), channel_id=1, source_target_pairs={{0,16},{16,32},{32,48},{48,64},{64,80},{80,96},{96,112},{112,0},{1... | collective-permute-start | bytes 393224 | tf_op jit(solution)/shard_map/ppermute | solution.py:28
  50.2 5.0 %collective-permute-start.19 = (bf16[256,256]{1,0:T(8,128)(2,1)S(1)}, bf16[256,256]{1,0:T(8,128)(2,1)S(1)}, u32[]{:S(2)}, u32[]{:S(2)}) collective-permute-start(bf16[256,256]{1,0:T(8,128)(2,1)S(1)} %get-tuple-element.33), channel_id=1, source_target_pairs={{0,112},{16,0},{32,16},{48,32},{64,48},{80,64},{96,80},{112,96},{1... | collective-permute-start | bytes 393224 | tf_op jit(solution)/shard_map/ppermute | solution.py:28
  55.3 10.3 %collective-permute-start.21 = (bf16[256,256]{1,0:T(8,128)(2,1)S(1)}, bf16[256,256]{1,0:T(8,128)(2,1)S(1)}, u32[]{:S(2)}, u32[]{:S(2)}) collective-permute-start(bf16[256,256]{1,0:T(8,128)(2,1)S(1)} %pad_maximum_fusion.2), channel_id=1, source_target_pairs={{0,96},{1,225},{16,112},{17,241},{32,0},{33,129},{48,16},{49,145},... | collective-permute-start | bytes 393224 | tf_op jit(solution)/shard_map/ppermute | solution.py:298
  59.6 8.0 %collective-permute-start.18 = (bf16[256,256]{1,0:T(8,128)(2,1)S(1)}, bf16[256,256]{1,0:T(8,128)(2,1)S(1)}, u32[]{:S(2)}, u32[]{:S(2)}) collective-permute-start(bf16[256,256]{1,0:T(8,128)(2,1)S(1)} %pad_maximum_fusion.1), channel_id=1, source_target_pairs={{0,32},{1,161},{16,48},{17,177},{32,64},{33,193},{48,80},{49,209},... | collective-permute-start | bytes 393224 | tf_op jit(solution)/shard_map/ppermute | solution.py:298
  59.8 9.2 %collective-permute-start.12 = (bf16[256,256]{1,0:T(8,128)(2,1)S(1)}, bf16[256,256]{1,0:T(8,128)(2,1)S(1)}, u32[]{:S(2)}, u32[]{:S(2)}) collective-permute-start(bf16[256,256]{1,0:T(8,128)(2,1)S(1)} %get-tuple-element.25), channel_id=1, source_target_pairs={{0,0},{1,129},{16,16},{17,145},{32,32},{33,161},{48,48},{49,177},{... | collective-permute-start | bytes 393224 | tf_op jit(solution)/shard_map/ppermute | solution.py:298
  61.9 7.0 %collective-permute-start.14 = (bf16[256,256]{1,0:T(8,128)(2,1)S(1)}, bf16[256,256]{1,0:T(8,128)(2,1)S(1)}, u32[]{:S(2)}, u32[]{:S(2)}) collective-permute-start(bf16[256,256]{1,0:T(8,128)(2,1)S(1)} %get-tuple-element.26), channel_id=1, source_target_pairs={{0,112},{1,241},{16,0},{17,129},{32,16},{33,145},{48,32},{49,161},... | collective-permute-start | bytes 393224 | tf_op jit(solution)/shard_map/ppermute | solution.py:298
  65.3 7.1 %collective-permute-start.13 = (bf16[256,256]{1,0:T(8,128)(2,1)S(1)}, bf16[256,256]{1,0:T(8,128)(2,1)S(1)}, u32[]{:S(2)}, u32[]{:S(2)}) collective-permute-start(bf16[256,256]{1,0:T(8,128)(2,1)S(1)} %get-tuple-element.27), channel_id=1, source_target_pairs={{0,16},{1,145},{16,32},{17,161},{32,48},{33,177},{48,64},{49,193},... | collective-permute-start | bytes 393224 | tf_op jit(solution)/shard_map/ppermute | solution.py:298
  72.5 1.6 %collective-permute-start.22 = (bf16[256,128]{1,0:T(8,128)(2,1)S(1)}, bf16[256,128]{1,0:T(8,128)(2,1)S(1)}, u32[]{:S(2)}, u32[]{:S(2)}) collective-permute-start(bf16[256,128]{1,0:T(8,128)(2,1)S(1)} %select_convert_fusion), channel_id=1, source_target_pairs={{0,1},{1,0},{2,3},{3,2},{4,5},{5,4},{6,7},{7,6},{8,9},{9,8},{10,11... | collective-permute-start | bytes 196616 | tf_op jit(solution)/shard_map/ppermute | solution.py:32
  91.4 3.3 %collective-permute-start.23 = (bf16[2048,128]{1,0:T(8,128)(2,1)S(1)}, bf16[2048,128]{1,0:T(8,128)(2,1)S(1)}, u32[]{:S(2)}, u32[]{:S(2)}) collective-permute-start(bf16[2048,128]{1,0:T(8,128)(2,1)S(1)} %bitcast.37), channel_id=1, source_target_pairs={{0,1},{1,0},{2,3},{3,2},{4,5},{5,4},{6,7},{7,6},{8,9},{9,8},{10,11... | collective-permute-start | bytes 1572872 | tf_op jit(solution)/shard_map/ppermute | solution.py:32

commit v5 on v4

--- a/solution.py
+++ b/solution.py
@@ -297,6 +297,10 @@
         ]
         return lax.ppermute(value, ("x", "z", "core"), pairs)
 
+    def split(value, by):
+        pairs = [(2 * i + c, 2 * ((i + (by, -by)[c]) % 8) + c) for i in range(8) for c in range(2)]
+        return lax.ppermute(value, ("z", "core"), pairs)
+
     def halves(value):
         return jnp.where(first, value[:, :HD], value[:, HD:]), jnp.where(first, value[:, HD:], value[:, :HD])
 
@@ -319,14 +323,11 @@
     relayed = wide(mine_relayed, swap(other_relayed, "core")).astype(BF)
     reached = wide(mine, swap(other, "core")).astype(BF)
     joined = dict(zip(RELAYED + REACHED, [relayed[k] for k in range(3)] + [reached[k] for k in range(5)]))
-    for4_up, for4_down = shift(joined[4][:BLK], "z", 8, 2), shift(joined[4][BLK:], "z", 8, -2)
+    for4 = split(joined[4], 2)
     for3_up, for3_down = shift(joined[3], "z", 8, 1), shift(joined[5], "z", 8, -1)
-    up2 = jnp.concatenate(
-        [wide(joined[2][:BLK], for3_up[:BLK], for4_up), wide(joined[2][BLK:], for3_up[BLK:])], axis=0
-    )
-    down2 = jnp.concatenate(
-        [wide(joined[6][:BLK], for3_down[:BLK]), wide(joined[6][BLK:], for3_down[BLK:], for4_down)], axis=0
-    )
+    zero = jnp.zeros_like(for4)
+    up2 = wide(joined[2], for3_up, jnp.where(first, for4, zero))
+    down2 = wide(joined[6], for3_down, jnp.where(first, zero, for4))
     for2_up, for2_down = across(up2.astype(BF), 2), across(down2.astype(BF), -2)
     for1_up, for1_down = across(joined[1], 1), across(joined[7], -1)
     own = across(joined[0], 0)

time: 96.7 us -> 94.4 us (0.976)
  starting transfers between devices: 39.8 us -> 36.1 us
  waiting for transfers between devices: 20.7 us -> 22.3 us
    ppermute x8 -> x6, starting transfers between devices: 12.9 us -> 9.21 us  [shift(): lax.ppermute(value, axis, [(i, (i + by) % size) for i in range(size)])]
    ppermute x0 -> x1, waiting for transfers between devices: none -> 3.22 us  [split(): return lax.ppermute(value, ('z', 'core'), pairs)]
    ppermute x10, waiting for transfers between devices: 7.98 us -> 6.8 us  [across(): return lax.ppermute(value, ('x', 'z', 'core'), pairs)]
    ppermute x6, starting transfers between devices: 4.05 us -> 2.92 us  [swap(): return lax.ppermute(value, axis, [(0, 1), (1, 0)])]
    ppermute x0 -> x1, starting transfers between devices: none -> 1.07 us  [split(): return lax.ppermute(value, ('z', 'core'), pairs)]
    ppermute x8 -> x6, waiting for transfers between devices: 7.62 us -> 6.88 us  [shift(): lax.ppermute(value, axis, [(i, (i + by) % size) for i in range(size)])]
  transfers between devices with their start and end apart: 24 -> 23, of which waited for: 13 -> 13; matrix products, arithmetic and copies ran while one was open for 1% -> 1% of each run, Pallas kernels for 0% -> 0%
where the time goes in v5:
time: 94.4 us; the launch traced here: 94.6 us
  starting transfers between devices  36.1 us (38%)
  waiting for transfers between devices  22.3 us (24%)
  blocking collectives  17.4 us (18%)
  Pallas kernels  14.9 us (16%)
  local copies, waits for them, and re-layouts  2.16 us (2%)
    ppermute x10, starting transfers between devices, across(): return lax.ppermute(value, ('x', 'z', 'core'), pairs)  22.9 us
    all_to_all x1, blocking collectives, shards(): lax.all_to_all(jnp.concatenate([summed] * KVH, axis=0), ('y', 'xh'), 0, 0...  17.4 us
    pallas_call x1, Pallas kernels, attention(): pl.pallas_call(attention_kernel, in_specs=[hbm] * 6 + [vmem], out_specs=[...  13.3 us
    ppermute x6, starting transfers between devices, shift(): lax.ppermute(value, axis, [(i, (i + by) % size) for i in range(size)])  9.21 us
    ppermute x6, waiting for transfers between devices, shift(): lax.ppermute(value, axis, [(i, (i + by) % size) for i in range(size)])  6.88 us
    ppermute x10, waiting for transfers between devices, across(): return lax.ppermute(value, ('x', 'z', 'core'), pairs)  6.8 us
    ppermute x6, waiting for transfers between devices, swap(): return lax.ppermute(value, axis, [(0, 1), (1, 0)])  5.41 us
    ppermute x1, waiting for transfers between devices, split(): return lax.ppermute(value, ('z', 'core'), pairs)  3.22 us
  transfers between devices with their start and end apart: 23, of which 13 were waited for; matrix products, arithmetic and copies ran while one was open for 1% of the time, Pallas kernels for 0%

profile of v5, /device:TPU:1, one launch (start us, length us, event | category | flops | bytes accessed | tf_op | source)
XLA Modules:
  0.0 94.6 jit_solution(12473535132421400445)
XLA Ops:
  0.7 1.2 %copy-done = bf16[256,2048]{1,0:T(8,128)(2,1)S(1)} copy-done((bf16[256,2048]{1,0:T(8,128)(2,1)S(1)}, bf16[256,2048]{1,0:T(8,128)(2,1)}, u32[]{:S(2)}) %copy-start) | copy-done | bytes 1048600
  1.9 4.8 %collective-permute-start.3 = (bf16[256,256]{1,0:T(8,128)(2,1)S(1)}, bf16[256,256]{1,0:T(8,128)(2,1)S(1)}, u32[]{:S(2)}, u32[]{:S(2)}) collective-permute-start(bf16[256,256]{1,0:T(8,128)(2,1)S(1)} %constant_dynamic-slice_fusion), channel_id=1, source_target_pairs={{0,32},{1,161},{16,48},{17,177},{32,64},{33,193},{48,80},{49,209},... | collective-permute-start | bytes 393224 | tf_op jit(solution)/shard_map/ppermute | solution.py:298
  6.7 3.1 %collective-permute-start.2 = (bf16[256,256]{1,0:T(8,128)(2,1)S(1)}, bf16[256,256]{1,0:T(8,128)(2,1)S(1)}, u32[]{:S(2)}, u32[]{:S(2)}) collective-permute-start(bf16[256,256]{1,0:T(8,128)(2,1)S(1)} %constant_dynamic-slice_fusion), channel_id=1, source_target_pairs={{0,96},{1,225},{16,112},{17,241},{32,0},{33,129},{48,16},{49,145},... | collective-permute-start | bytes 393224 | tf_op jit(solution)/shard_map/ppermute | solution.py:298
  9.8 2.2 %collective-permute-start = (bf16[256,256]{1,0:T(8,128)(2,1)S(1)}, bf16[256,256]{1,0:T(8,128)(2,1)S(1)}, u32[]{:S(2)}, u32[]{:S(2)}) collective-permute-start(bf16[256,256]{1,0:T(8,128)(2,1)S(1)} %constant_dynamic-slice_fusion), channel_id=1, source_target_pairs={{0,0},{1,129},{16,16},{17,145},{32,32},{33,161},{48,48},{49,177},{... | collective-permute-start | bytes 393224 | tf_op jit(solution)/shard_map/ppermute | solution.py:298
  12.0 2.8 %collective-permute-start.1 = (bf16[256,256]{1,0:T(8,128)(2,1)S(1)}, bf16[256,256]{1,0:T(8,128)(2,1)S(1)}, u32[]{:S(2)}, u32[]{:S(2)}) collective-permute-start(bf16[256,256]{1,0:T(8,128)(2,1)S(1)} %constant_dynamic-slice_fusion), channel_id=1, source_target_pairs={{0,112},{1,241},{16,0},{17,129},{32,16},{33,145},{48,32},{49,161},... | collective-permute-start | bytes 393224 | tf_op jit(solution)/shard_map/ppermute | solution.py:298
  14.8 1.5 %collective-permute-start.7 = (bf16[128,256]{1,0:T(8,128)(2,1)S(1)}, bf16[128,256]{1,0:T(8,128)(2,1)S(1)}, u32[]{:S(2)}, u32[]{:S(2)}) collective-permute-start(bf16[128,256]{1,0:T(8,128)(2,1)S(1)} %slice.50), channel_id=1, source_target_pairs={{0,32},{16,48},{32,64},{48,80},{64,96},{80,112},{96,0},{112,16},{1... | collective-permute-start | bytes 196616 | tf_op jit(solution)/shard_map/ppermute | solution.py:28
  17.0 2.3 %collective-permute-start.8 = (bf16[128,256]{1,0:T(8,128)(2,1)S(1)}, bf16[128,256]{1,0:T(8,128)(2,1)S(1)}, u32[]{:S(2)}, u32[]{:S(2)}) collective-permute-start(bf16[128,256]{1,0:T(8,128)(2,1)S(1)} %slice.51), channel_id=1, source_target_pairs={{0,96},{16,112},{32,0},{48,16},{64,32},{80,48},{96,64},{112,80},{1... | collective-permute-start | bytes 196616 | tf_op jit(solution)/shard_map/ppermute | solution.py:28
  19.3 0.9 collective-permute-start.9
  20.4 1.7 %collective-permute-start.6 = (bf16[256,256]{1,0:T(8,128)(2,1)S(1)}, bf16[256,256]{1,0:T(8,128)(2,1)S(1)}, u32[]{:S(2)}, u32[]{:S(2)}) collective-permute-start(bf16[256,256]{1,0:T(8,128)(2,1)S(1)} %collective-permute-done.2), channel_id=1, source_target_pairs={{0,112},{16,0},{32,16},{48,32},{64,48},{80,64},{96,80},{112,96},{1... | collective-permute-start | bytes 393224 | tf_op jit(solution)/shard_map/ppermute | solution.py:28
  22.2 4.9 %collective-permute-done.6 = bf16[256,256]{1,0:T(8,128)(2,1)S(1)} collective-permute-done((bf16[256,256]{1,0:T(8,128)(2,1)S(1)}, bf16[256,256]{1,0:T(8,128)(2,1)S(1)}, u32[]{:S(2)}, u32[]{:S(2)}) %collective-permute-start.6) | collective-permute-done | bytes 131104 | tf_op jit(solution)/shard_map/ppermute | solution.py:28
  27.2 0.8 collective-permute-start.10
  28.1 0.7 copy.10.vis_any
  29.4 0.9 collective-permute-done.5
  30.5 13.3 %attention.1 = (bf16[256,512]{1,0:T(8,128)(2,1)}, bf16[256,512]{1,0:T(8,128)(2,1)}, bf16[3,256,256]{2,1,0:T(8,128)(2,1)S(1)}, bf16[3,256,256]{2,1,0:T(8,128)(2,1...) custom-call(s32[32,24]{1,0:T(8,128)} %copy.10.vis_any, s32[32]{0:T(128)} %count_any.1, ...), custom_call_target="tpu_custom_call" | custom-call | tf_op jit(solution)/shard_map/attention/pallas_call | solution.py:229
  44.5 1.2 %collective-permute-done.15 = bf16[3,256,256]{2,1,0:T(8,128)(2,1)S(1)} collective-permute-done((bf16[3,256,256]{2,1,0:T(8,128)(2,1)S(1)}, bf16[3,256,256]{2,1,0:T(8,128)(2,1)S(1)}, u32[]{:S(2)}, u32[]{:S(2)}) %collective-permute-start.15) | collective-permute-done | bytes 393248 | tf_op jit(solution)/shard_map/ppermute | solution.py:32
  45.9 2.7 %collective-permute-start.19 = (bf16[256,256]{1,0:T(8,128)(2,1)S(1)}, bf16[256,256]{1,0:T(8,128)(2,1)S(1)}, u32[]{:S(2)}, u32[]{:S(2)}) collective-permute-start(bf16[256,256]{1,0:T(8,128)(2,1)S(1)} %get-tuple-element.27), channel_id=1, source_target_pairs={{0,112},{16,0},{32,16},{48,32},{64,48},{80,64},{96,80},{112,96},{1... | collective-permute-start | bytes 393224 | tf_op jit(solution)/shard_map/ppermute | solution.py:28
  48.6 1.1 %collective-permute-start.17 = (bf16[256,256]{1,0:T(8,128)(2,1)S(1)}, bf16[256,256]{1,0:T(8,128)(2,1)S(1)}, u32[]{:S(2)}, u32[]{:S(2)}) collective-permute-start(bf16[256,256]{1,0:T(8,128)(2,1)S(1)} %get-tuple-element.28), channel_id=1, source_target_pairs={{0,32},{1,97},{16,48},{17,113},{32,64},{33,1},{48,80},{49,17},{64,... | collective-permute-start | bytes 393224 | tf_op jit(solution)/shard_map/ppermute | solution.py:302
  49.9 2.0 %collective-permute-done.16 = bf16[256,256]{1,0:T(8,128)(2,1)S(1)} collective-permute-done((bf16[256,256]{1,0:T(8,128)(2,1)S(1)}, bf16[256,256]{1,0:T(8,128)(2,1)S(1)}, u32[]{:S(2)}, u32[]{:S(2)}) %collective-permute-start.16) | collective-permute-done | bytes 131104 | tf_op jit(solution)/shard_map/ppermute | solution.py:28
  51.9 3.2 %collective-permute-done.17 = bf16[256,256]{1,0:T(8,128)(2,1)S(1)} collective-permute-done((bf16[256,256]{1,0:T(8,128)(2,1)S(1)}, bf16[256,256]{1,0:T(8,128)(2,1)S(1)}, u32[]{:S(2)}, u32[]{:S(2)}) %collective-permute-start.17) | collective-permute-done | bytes 131104 | tf_op jit(solution)/shard_map/ppermute | solution.py:302
  55.2 3.8 %collective-permute-start.18 = (bf16[256,256]{1,0:T(8,128)(2,1)S(1)}, bf16[256,256]{1,0:T(8,128)(2,1)S(1)}, u32[]{:S(2)}, u32[]{:S(2)}) collective-permute-start(bf16[256,256]{1,0:T(8,128)(2,1)S(1)} %get-tuple-element.19), channel_id=1, source_target_pairs={{0,32},{1,161},{16,48},{17,177},{32,64},{33,193},{48,80},{49,209},... | collective-permute-start | bytes 393224 | tf_op jit(solution)/shard_map/ppermute | solution.py:298
  59.0 0.8 collective-permute-start.20
  59.7 3.0 %collective-permute-start.12 = (bf16[256,256]{1,0:T(8,128)(2,1)S(1)}, bf16[256,256]{1,0:T(8,128)(2,1)S(1)}, u32[]{:S(2)}, u32[]{:S(2)}) collective-permute-start(bf16[256,256]{1,0:T(8,128)(2,1)S(1)} %get-tuple-element.23), channel_id=1, source_target_pairs={{0,0},{1,129},{16,16},{17,145},{32,32},{33,161},{48,48},{49,177},{... | collective-permute-start | bytes 393224 | tf_op jit(solution)/shard_map/ppermute | solution.py:298
  62.7 1.1 %collective-permute-start.14 = (bf16[256,256]{1,0:T(8,128)(2,1)S(1)}, bf16[256,256]{1,0:T(8,128)(2,1)S(1)}, u32[]{:S(2)}, u32[]{:S(2)}) collective-permute-start(bf16[256,256]{1,0:T(8,128)(2,1)S(1)} %get-tuple-element.24), channel_id=1, source_target_pairs={{0,112},{1,241},{16,0},{17,129},{32,16},{33,145},{48,32},{49,161},... | collective-permute-start | bytes 393224 | tf_op jit(solution)/shard_map/ppermute | solution.py:298
  63.8 1.4 %collective-permute-start.13 = (bf16[256,256]{1,0:T(8,128)(2,1)S(1)}, bf16[256,256]{1,0:T(8,128)(2,1)S(1)}, u32[]{:S(2)}, u32[]{:S(2)}) collective-permute-start(bf16[256,256]{1,0:T(8,128)(2,1)S(1)} %get-tuple-element.25), channel_id=1, source_target_pairs={{0,16},{1,145},{16,32},{17,161},{32,48},{33,177},{48,64},{49,193},... | collective-permute-start | bytes 393224 | tf_op jit(solution)/shard_map/ppermute | solution.py:298
  65.2 0.8 collective-permute-done.18
  66.0 2.3 %collective-permute-done.20 = bf16[256,256]{1,0:T(8,128)(2,1)S(1)} collective-permute-done((bf16[256,256]{1,0:T(8,128)(2,1)S(1)}, bf16[256,256]{1,0:T(8,128)(2,1)S(1)}, u32[]{:S(2)}, u32[]{:S(2)}) %collective-permute-start.20) | collective-permute-done | bytes 131104 | tf_op jit(solution)/shard_map/ppermute | solution.py:298
  68.2 2.9 %collective-permute-done.14 = bf16[256,256]{1,0:T(8,128)(2,1)S(1)} collective-permute-done((bf16[256,256]{1,0:T(8,128)(2,1)S(1)}, bf16[256,256]{1,0:T(8,128)(2,1)S(1)}, u32[]{:S(2)}, u32[]{:S(2)}) %collective-permute-start.14) | collective-permute-done | bytes 131104 | tf_op jit(solution)/shard_map/ppermute | solution.py:298
  71.3 1.2 %collective-permute-done.21 = bf16[256,128]{1,0:T(8,128)(2,1)S(1)} collective-permute-done((bf16[256,128]{1,0:T(8,128)(2,1)S(1)}, bf16[256,128]{1,0:T(8,128)(2,1)S(1)}, u32[]{:S(2)}, u32[]{:S(2)}) %collective-permute-start.21) | collective-permute-done | bytes 65568 | tf_op jit(solution)/shard_map/ppermute | solution.py:32
  72.7 17.4 %all_to_all.11 = bf16[8,256,128]{2,1,0:T(8,128)(2,1)S(1)} all-to-all(bf16[8,256,128]{2,1,0:T(8,128)(2,1)S(1)} %bitcast.27), channel_id=1, replica_groups=mesh['x'=2,'z'=8,'xh'=2,'y'=4,'core'=2] {'y','xh'}, dimensions={0} | all-to-all | bytes 1048576 | tf_op jit(solution)/shard_map/all_to_all | solution.py:336
  90.1 1.3 %collective-permute-start.22 = (bf16[2048,128]{1,0:T(8,128)(2,1)S(1)}, bf16[2048,128]{1,0:T(8,128)(2,1)S(1)}, u32[]{:S(2)}, u32[]{:S(2)}) collective-permute-start(bf16[2048,128]{1,0:T(8,128)(2,1)S(1)} %bitcast.25), channel_id=1, source_target_pairs={{0,1},{1,0},{2,3},{3,2},{4,5},{5,4},{6,7},{7,6},{8,9},{9,8},{10,11... | collective-permute-start | bytes 1572872 | tf_op jit(solution)/shard_map/ppermute | solution.py:32
  91.4 1.5 %collective-permute-done.22.other_ref = bf16[2048,128]{1,0:T(8,128)(2,1)S(1)} collective-permute-done((bf16[2048,128]{1,0:T(8,128)(2,1)S(1)}, bf16[2048,128]{1,0:T(8,128)(2,1)S(1)}, u32[]{:S(2)}, u32[]{:S(2)}) %collective-permute-start.22) | collective-permute-done | bytes 524320 | tf_op jit(solution)/shard_map/ppermute | solution.py:32
  93.0 1.6 %assemble.1 = f32[256,2048]{1,0:T(8,128)} custom-call(bf16[2048,128]{1,0:T(8,128)(2,1)S(1)} %bitcast.26, bf16[2048,128]{1,0:T(8,128)(2,1)S(1)} %collective-permute-done.22.other_ref), custom_call_target="tpu_custom_call" | custom-call | tf_op jit(solution)/shard_map/assemble/pallas_call | solution.py:273
  (52 shorter events, 3.3 us)
Async XLA Ops:
  0.6 1.2 %copy-start = (bf16[256,2048]{1,0:T(8,128)(2,1)S(1)}, bf16[256,2048]{1,0:T(8,128)(2,1)}, u32[]{:S(2)}) copy-start(bf16[256,2048]{1,0:T(8,128)(2,1)} %param.8) | copy-start | bytes 3145732
  0.6 27.5 %copy-start.1 = (s32[32,24]{0,1:T(8,128)S(1)}, s32[32,24]{0,1:T(8,128)}, u32[]{:S(2)}) copy-start(s32[32,24]{0,1:T(8,128)} %param.10) | copy-start | bytes 9220
  1.9 12.9 %collective-permute-start.3 = (bf16[256,256]{1,0:T(8,128)(2,1)S(1)}, bf16[256,256]{1,0:T(8,128)(2,1)S(1)}, u32[]{:S(2)}, u32[]{:S(2)}) collective-permute-start(bf16[256,256]{1,0:T(8,128)(2,1)S(1)} %constant_dynamic-slice_fusion), channel_id=1, source_target_pairs={{0,32},{1,161},{16,48},{17,177},{32,64},{33,193},{48,80},{49,209},... | collective-permute-start | bytes 393224 | tf_op jit(solution)/shard_map/ppermute | solution.py:298
  6.7 10.3 %collective-permute-start.2 = (bf16[256,256]{1,0:T(8,128)(2,1)S(1)}, bf16[256,256]{1,0:T(8,128)(2,1)S(1)}, u32[]{:S(2)}, u32[]{:S(2)}) collective-permute-start(bf16[256,256]{1,0:T(8,128)(2,1)S(1)} %constant_dynamic-slice_fusion), channel_id=1, source_target_pairs={{0,96},{1,225},{16,112},{17,241},{32,0},{33,129},{48,16},{49,145},... | collective-permute-start | bytes 393224 | tf_op jit(solution)/shard_map/ppermute | solution.py:298
  9.8 9.5 %collective-permute-start = (bf16[256,256]{1,0:T(8,128)(2,1)S(1)}, bf16[256,256]{1,0:T(8,128)(2,1)S(1)}, u32[]{:S(2)}, u32[]{:S(2)}) collective-permute-start(bf16[256,256]{1,0:T(8,128)(2,1)S(1)} %constant_dynamic-slice_fusion), channel_id=1, source_target_pairs={{0,0},{1,129},{16,16},{17,145},{32,32},{33,161},{48,48},{49,177},{... | collective-permute-start | bytes 393224 | tf_op jit(solution)/shard_map/ppermute | solution.py:298
  12.0 8.4 %collective-permute-start.1 = (bf16[256,256]{1,0:T(8,128)(2,1)S(1)}, bf16[256,256]{1,0:T(8,128)(2,1)S(1)}, u32[]{:S(2)}, u32[]{:S(2)}) collective-permute-start(bf16[256,256]{1,0:T(8,128)(2,1)S(1)} %constant_dynamic-slice_fusion), channel_id=1, source_target_pairs={{0,112},{1,241},{16,0},{17,129},{32,16},{33,145},{48,32},{49,161},... | collective-permute-start | bytes 393224 | tf_op jit(solution)/shard_map/ppermute | solution.py:298
  14.8 13.2 %collective-permute-start.4 = (bf16[256,256]{1,0:T(8,128)(2,1)S(1)}, bf16[256,256]{1,0:T(8,128)(2,1)S(1)}, u32[]{:S(2)}, u32[]{:S(2)}) collective-permute-start(bf16[256,256]{1,0:T(8,128)(2,1)S(1)} %constant_dynamic-slice_fusion), channel_id=1, source_target_pairs={{0,16},{1,145},{16,32},{17,161},{32,48},{33,177},{48,64},{49,193},... | collective-permute-start | bytes 393224 | tf_op jit(solution)/shard_map/ppermute | solution.py:298
  14.8 12.3 %collective-permute-start.7 = (bf16[128,256]{1,0:T(8,128)(2,1)S(1)}, bf16[128,256]{1,0:T(8,128)(2,1)S(1)}, u32[]{:S(2)}, u32[]{:S(2)}) collective-permute-start(bf16[128,256]{1,0:T(8,128)(2,1)S(1)} %slice.50), channel_id=1, source_target_pairs={{0,32},{16,48},{32,64},{48,80},{64,96},{80,112},{96,0},{112,16},{1... | collective-permute-start | bytes 196616 | tf_op jit(solution)/shard_map/ppermute | solution.py:28
  17.0 10.1 %collective-permute-start.8 = (bf16[128,256]{1,0:T(8,128)(2,1)S(1)}, bf16[128,256]{1,0:T(8,128)(2,1)S(1)}, u32[]{:S(2)}, u32[]{:S(2)}) collective-permute-start(bf16[128,256]{1,0:T(8,128)(2,1)S(1)} %slice.51), channel_id=1, source_target_pairs={{0,96},{16,112},{32,0},{48,16},{64,32},{80,48},{96,64},{112,80},{1... | collective-permute-start | bytes 196616 | tf_op jit(solution)/shard_map/ppermute | solution.py:28
  19.3 7.8 %collective-permute-start.9 = (bf16[256,256]{1,0:T(8,128)(2,1)S(1)}, bf16[256,256]{1,0:T(8,128)(2,1)S(1)}, u32[]{:S(2)}, u32[]{:S(2)}) collective-permute-start(bf16[256,256]{1,0:T(8,128)(2,1)S(1)} %collective-permute-done.3), channel_id=1, source_target_pairs={{0,16},{16,32},{32,48},{48,64},{64,80},{80,96},{96,112},{112,0},{1... | collective-permute-start | bytes 393224 | tf_op jit(solution)/shard_map/ppermute | solution.py:28
  20.4 6.7 %collective-permute-start.6 = (bf16[256,256]{1,0:T(8,128)(2,1)S(1)}, bf16[256,256]{1,0:T(8,128)(2,1)S(1)}, u32[]{:S(2)}, u32[]{:S(2)}) collective-permute-start(bf16[256,256]{1,0:T(8,128)(2,1)S(1)} %collective-permute-done.2), channel_id=1, source_target_pairs={{0,112},{16,0},{32,16},{48,32},{64,48},{80,64},{96,80},{112,96},{1... | collective-permute-start | bytes 393224 | tf_op jit(solution)/shard_map/ppermute | solution.py:28
  27.2 2.2 %collective-permute-start.10 = (bf16[768,256]{1,0:T(8,128)(2,1)S(1)}, bf16[768,256]{1,0:T(8,128)(2,1)S(1)}, u32[]{:S(2)}, u32[]{:S(2)}) collective-permute-start(bf16[768,256]{1,0:T(8,128)(2,1)S(1)} %constant_dynamic-update-slice_fusion.5), channel_id=1, source_target_pairs={{0,1},{1,0},{2,3},{3,2},{4,5},{5,4},{6,7},{7,6},{8,9},{9,8},{10,11... | collective-permute-start | bytes 1179656 | tf_op jit(solution)/shard_map/ppermute | solution.py:32
  28.0 2.3 %collective-permute-start.5 = (bf16[1280,256]{1,0:T(8,128)(2,1)S(1)}, bf16[1280,256]{1,0:T(8,128)(2,1)S(1)}, u32[]{:S(2)}, u32[]{:S(2)}) collective-permute-start(bf16[1280,256]{1,0:T(8,128)(2,1)S(1)} %constant_dynamic-update-slice_fusion), channel_id=1, source_target_pairs={{0,1},{1,0},{2,3},{3,2},{4,5},{5,4},{6,7},{7,6},{8,9},{9,8},{10,11... | collective-permute-start | bytes 1966088 | tf_op jit(solution)/shard_map/ppermute | solution.py:32
  43.9 1.8 %collective-permute-start.15 = (bf16[3,256,256]{2,1,0:T(8,128)(2,1)S(1)}, bf16[3,256,256]{2,1,0:T(8,128)(2,1)S(1)}, u32[]{:S(2)}, u32[]{:S(2)}) collective-permute-start(bf16[3,256,256]{2,1,0:T(8,128)(2,1)S(1)} %get-tuple-element.14), channel_id=1, source_target_pairs={{0,1},{1,0},{2,3},{3,2},{4,5},{5,4},{6,7},{7,6},{8,9},{9,8},{10,11... | collective-permute-start | bytes 1179656 | tf_op jit(solution)/shard_map/ppermute | solution.py:32
  44.3 5.3 %collective-permute-start.11 = (bf16[5,256,256]{2,1,0:T(8,128)(2,1)S(1)}, bf16[5,256,256]{2,1,0:T(8,128)(2,1)S(1)}, u32[]{:S(2)}, u32[]{:S(2)}) collective-permute-start(bf16[5,256,256]{2,1,0:T(8,128)(2,1)S(1)} %get-tuple-element.12), channel_id=1, source_target_pairs={{0,1},{1,0},{2,3},{3,2},{4,5},{5,4},{6,7},{7,6},{8,9},{9,8},{10,11... | collective-permute-start | bytes 1966088 | tf_op jit(solution)/shard_map/ppermute | solution.py:32
  45.8 6.0 %collective-permute-start.16 = (bf16[256,256]{1,0:T(8,128)(2,1)S(1)}, bf16[256,256]{1,0:T(8,128)(2,1)S(1)}, u32[]{:S(2)}, u32[]{:S(2)}) collective-permute-start(bf16[256,256]{1,0:T(8,128)(2,1)S(1)} %get-tuple-element.26), channel_id=1, source_target_pairs={{0,16},{16,32},{32,48},{48,64},{64,80},{80,96},{96,112},{112,0},{1... | collective-permute-start | bytes 393224 | tf_op jit(solution)/shard_map/ppermute | solution.py:28
  45.9 5.9 %collective-permute-start.19 = (bf16[256,256]{1,0:T(8,128)(2,1)S(1)}, bf16[256,256]{1,0:T(8,128)(2,1)S(1)}, u32[]{:S(2)}, u32[]{:S(2)}) collective-permute-start(bf16[256,256]{1,0:T(8,128)(2,1)S(1)} %get-tuple-element.27), channel_id=1, source_target_pairs={{0,112},{16,0},{32,16},{48,32},{64,48},{80,64},{96,80},{112,96},{1... | collective-permute-start | bytes 393224 | tf_op jit(solution)/shard_map/ppermute | solution.py:28
  48.6 6.5 %collective-permute-start.17 = (bf16[256,256]{1,0:T(8,128)(2,1)S(1)}, bf16[256,256]{1,0:T(8,128)(2,1)S(1)}, u32[]{:S(2)}, u32[]{:S(2)}) collective-permute-start(bf16[256,256]{1,0:T(8,128)(2,1)S(1)} %get-tuple-element.28), channel_id=1, source_target_pairs={{0,32},{1,97},{16,48},{17,113},{32,64},{33,1},{48,80},{49,17},{64,... | collective-permute-start | bytes 393224 | tf_op jit(solution)/shard_map/ppermute | solution.py:302
  55.2 10.8 %collective-permute-start.18 = (bf16[256,256]{1,0:T(8,128)(2,1)S(1)}, bf16[256,256]{1,0:T(8,128)(2,1)S(1)}, u32[]{:S(2)}, u32[]{:S(2)}) collective-permute-start(bf16[256,256]{1,0:T(8,128)(2,1)S(1)} %get-tuple-element.19), channel_id=1, source_target_pairs={{0,32},{1,161},{16,48},{17,177},{32,64},{33,193},{48,80},{49,209},... | collective-permute-start | bytes 393224 | tf_op jit(solution)/shard_map/ppermute | solution.py:298
  59.0 9.3 %collective-permute-start.20 = (bf16[256,256]{1,0:T(8,128)(2,1)S(1)}, bf16[256,256]{1,0:T(8,128)(2,1)S(1)}, u32[]{:S(2)}, u32[]{:S(2)}) collective-permute-start(bf16[256,256]{1,0:T(8,128)(2,1)S(1)} %get-tuple-element.20), channel_id=1, source_target_pairs={{0,96},{1,225},{16,112},{17,241},{32,0},{33,129},{48,16},{49,145},... | collective-permute-start | bytes 393224 | tf_op jit(solution)/shard_map/ppermute | solution.py:298
  59.7 8.5 %collective-permute-start.12 = (bf16[256,256]{1,0:T(8,128)(2,1)S(1)}, bf16[256,256]{1,0:T(8,128)(2,1)S(1)}, u32[]{:S(2)}, u32[]{:S(2)}) collective-permute-start(bf16[256,256]{1,0:T(8,128)(2,1)S(1)} %get-tuple-element.23), channel_id=1, source_target_pairs={{0,0},{1,129},{16,16},{17,145},{32,32},{33,161},{48,48},{49,177},{... | collective-permute-start | bytes 393224 | tf_op jit(solution)/shard_map/ppermute | solution.py:298
  62.7 8.4 %collective-permute-start.14 = (bf16[256,256]{1,0:T(8,128)(2,1)S(1)}, bf16[256,256]{1,0:T(8,128)(2,1)S(1)}, u32[]{:S(2)}, u32[]{:S(2)}) collective-permute-start(bf16[256,256]{1,0:T(8,128)(2,1)S(1)} %get-tuple-element.24), channel_id=1, source_target_pairs={{0,112},{1,241},{16,0},{17,129},{32,16},{33,145},{48,32},{49,161},... | collective-permute-start | bytes 393224 | tf_op jit(solution)/shard_map/ppermute | solution.py:298
  63.8 7.3 %collective-permute-start.13 = (bf16[256,256]{1,0:T(8,128)(2,1)S(1)}, bf16[256,256]{1,0:T(8,128)(2,1)S(1)}, u32[]{:S(2)}, u32[]{:S(2)}) collective-permute-start(bf16[256,256]{1,0:T(8,128)(2,1)S(1)} %get-tuple-element.25), channel_id=1, source_target_pairs={{0,16},{1,145},{16,32},{17,161},{32,48},{33,177},{48,64},{49,193},... | collective-permute-start | bytes 393224 | tf_op jit(solution)/shard_map/ppermute | solution.py:298
  71.2 1.3 %collective-permute-start.21 = (bf16[256,128]{1,0:T(8,128)(2,1)S(1)}, bf16[256,128]{1,0:T(8,128)(2,1)S(1)}, u32[]{:S(2)}, u32[]{:S(2)}) collective-permute-start(bf16[256,128]{1,0:T(8,128)(2,1)S(1)} %select_convert_fusion), channel_id=1, source_target_pairs={{0,1},{1,0},{2,3},{3,2},{4,5},{5,4},{6,7},{7,6},{8,9},{9,8},{10,11... | collective-permute-start | bytes 196616 | tf_op jit(solution)/shard_map/ppermute | solution.py:32
  90.1 2.8 %collective-permute-start.22 = (bf16[2048,128]{1,0:T(8,128)(2,1)S(1)}, bf16[2048,128]{1,0:T(8,128)(2,1)S(1)}, u32[]{:S(2)}, u32[]{:S(2)}) collective-permute-start(bf16[2048,128]{1,0:T(8,128)(2,1)S(1)} %bitcast.25), channel_id=1, source_target_pairs={{0,1},{1,0},{2,3},{3,2},{4,5},{5,4},{6,7},{7,6},{8,9},{9,8},{10,11... | collective-permute-start | bytes 1572872 | tf_op jit(solution)/shard_map/ppermute | solution.py:32
